TPU v7x, 32 devices: a whole 2x2x4 slice. The times are simulated.
32 devices in a mesh: ctx: 8 (over z, core), tp: 4 (over y, x).
Axes of the slice: x: 2, y: 2, z: 4, core: 2. Of those that a mesh axis runs over, the one named last changes fastest.
Arguments:
- query_proj: bfloat16 [4096, 8192], P('tp', 'ctx'), may hold values from -6 to 6
- key_proj: bfloat16 [4096, 8192], P('tp', 'ctx'), may hold values from -6 to 6
- value_proj: bfloat16 [4096, 8192], P('tp', 'ctx'), may hold values from -6 to 6
- short_taps: float32 [3, 3, 4096], P(None, None, 'tp'), may hold values from -3.5 to 3.5
- long_filter: float32 [4096, 8192], P(('tp', 'ctx')), may hold values from -0.0625 to 0.0625
- out_weight: bfloat16 [4096, 4096], P('tp'), may hold values from -0.125 to 0.125
- medium_taps: bfloat16 [128, 4096], P(None, 'tp'), may hold values from -0.5 to 0.5
Outputs:
- operator: bfloat16 [4096, 8192], P('tp', 'ctx')
- medium: bfloat16 [4096, 8192], P('tp', 'ctx')
All inputs are finite; a program needn't handle non-finite values.
Results may differ from a plain program's by a relative error of at most 0.014.
Values may be sent and summed in bfloat16 or wider, within the bound.
No kernel may reach another device: no remote copies, remote signals or barrier semaphores. Data moves between devices by JAX's collectives and lax.ppermute only.
A program may use at most 320 MiB of HBM per device.

v0:
```python
import functools
import math

import jax
import jax.numpy as jnp
import numpy as np
from jax import lax
from jax.experimental import pallas as pl
from jax.experimental.pallas import tpu as pltpu
from jax.sharding import PartitionSpec as P


LANES = 128
BF16 = jnp.bfloat16
F32 = jnp.float32


def split_table(table):
    high = np.asarray(table, np.float32).astype(BF16)
    low = (np.asarray(table, np.float64) - high.astype(np.float64)).astype(BF16)
    return high, low


def rotation(rows, cols, period):
    angles = 2.0 * math.pi * np.outer(rows, cols) / period
    return np.cos(angles), np.sin(angles)


@functools.lru_cache
def long_tables(length, groups):
    n1 = length // LANES
    first = np.arange(n1)
    lanes = np.arange(LANES)
    cos1, sin1 = rotation(first + 0.25, first, n1)
    outer = np.concatenate([cos1, -sin1], axis=0)
    back = np.concatenate([cos1.T, -sin1.T], axis=1) / n1
    twist_re, twist_im = rotation(first + 0.25, lanes, length)
    cos2, sin2 = rotation(lanes, lanes, LANES)
    inner = np.block([[cos2, -sin2], [sin2, cos2]])
    inner_back = np.block([[cos2, sin2], [-sin2, cos2]]) / LANES
    per = n1 // groups
    fore, rear = [], []
    for me in range(groups):
        ids = np.concatenate([((me - s) % groups) * per + np.arange(per) for s in range(groups)])
        out = np.concatenate([((me + s) % groups) * per + np.arange(per) for s in range(groups)])
        high, low = split_table(outer[:, ids])
        fore.append(np.concatenate([high, low], axis=1))
        high, low = split_table(back[out])
        rear.append(np.concatenate([high, low], axis=1))
    high, low = split_table(outer)
    plain = np.concatenate([high, high, low], axis=1)
    twist = np.stack([twist_re, -twist_im]).astype(np.float32)
    inner_high, inner_low = split_table(inner)
    return dict(
        fore=np.stack(fore),
        rear=np.stack(rear),
        plain=plain,
        twist=twist,
        inner=inner_high,
        inner_low=inner_low,
        inner_back=split_table(inner_back)[0],
    )


@functools.lru_cache
def medium_tables(width):
    span = 2 * width
    cos, sin = rotation(np.arange(span), np.arange(width) + 0.5, span)
    high, low = split_table(np.concatenate([cos, -sin], axis=1))
    last = slice(width, span)
    back = np.concatenate([cos[last].T, -sin[last].T], axis=0) / width
    return high, low, split_table(back)[0]


def grant(mib):
    return pltpu.CompilerParams(vmem_limit_bytes=mib * 1024 * 1024)


def dot(left, right):
    return jnp.dot(left, right, preferred_element_type=F32)


def short_conv(block, edge, taps):
    lane = lax.broadcasted_iota(jnp.int32, block.shape, 1)
    older, newer = edge[:, 0:1], edge[:, 1:2]
    back1 = jnp.where(lane == 0, newer, pltpu.roll(block, 1, 1))
    back2 = jnp.where(lane == 0, older, jnp.where(lane == 1, newer, pltpu.roll(block, 2, 1)))
    return taps[:, 0:1] * block + taps[:, 1:2] * back1 + taps[:, 2:3] * back2


def mix_kernel(ids_ref, key_ref, value_ref, aux_ref, *out_refs):
    aux = aux_ref[...]
    keys = short_conv(key_ref[...].astype(F32), aux[:, 11:13], aux[:, 3:6])
    values = short_conv(value_ref[...].astype(F32), aux[:, 13:15], aux[:, 6:9])
    mixed = (keys * values).astype(BF16)
    for at, out_ref in enumerate(out_refs):

        @pl.when(pl.program_id(0) == at)
        def _():
            for j in range(out_ref.shape[0]):
                out_ref[j] = mixed[:, j * LANES : (j + 1) * LANES]


def mix(ids, key_proj, value_proj, aux, first, count, groups):
    channels, tokens = key_proj.shape
    rows = channels // groups
    where = lambda i, ids: (lax.rem(ids[0] + first + i, groups), 0)
    piece = (tokens // LANES, rows, LANES)
    return pl.pallas_call(
        mix_kernel,
        out_shape=[jax.ShapeDtypeStruct(piece, BF16)] * count,
        grid_spec=pltpu.PrefetchScalarGridSpec(
            num_scalar_prefetch=1,
            grid=(count,),
            in_specs=[
                pl.BlockSpec((rows, tokens), where),
                pl.BlockSpec((rows, tokens), where),
                pl.BlockSpec((rows, aux.shape[1]), where),
            ],
            out_specs=[whole(piece)] * count,
        ),
        compiler_params=grant(12),
        name="mix",
    )(ids, key_proj, value_proj, aux)


def twisted(wide, twist_re, twist_im, count):
    half = wide.shape[0] // 2
    out = []
    for c in range(count):
        re = wide[:half, c * LANES : (c + 1) * LANES]
        im = wide[half:, c * LANES : (c + 1) * LANES]
        out.append((re * twist_re - im * twist_im, re * twist_im + im * twist_re))
    return out


def filter_kernel(filter_ref, plain_ref, twist_ref, inner_ref, inner_low_ref, out_ref, rows_ref):
    block = filter_ref.shape[0]
    n1 = filter_ref.shape[1] // LANES
    for n in range(n1):
        rows_ref[n * block : (n + 1) * block, :] = filter_ref[:, n * LANES : (n + 1) * LANES]

    group = math.gcd(block, 8)

    def body(at, carry):
        base = at * group
        highs, lows = [], []
        for pair in range(group // 2):
            loaded = [
                rows_ref[pl.ds(base + 2 * pair + c, n1, stride=block), :] for c in range(2)
            ]
            both = jnp.concatenate(loaded, axis=1)
            high = both.astype(BF16)
            low = (both - high.astype(F32)).astype(BF16)
            wide = dot(plain_ref[...], jnp.concatenate([high, low, high], axis=0))
            for re, im in twisted(wide, twist_ref[0], twist_ref[1], 2):
                line = jnp.concatenate([re, im], axis=1)
                high = line.astype(BF16)
                highs.append(high)
                lows.append((line - high.astype(F32)).astype(BF16))
        high = jnp.concatenate(highs, axis=0)
        low = jnp.concatenate(lows, axis=0)
        spectrum = (
            dot(high, inner_ref[...]) + dot(low, inner_ref[...]) + dot(high, inner_low_ref[...])
        )
        out_ref[pl.ds(base, group)] = spectrum.reshape(group, n1, 2 * LANES)
        return carry

    lax.fori_loop(0, block // group, body, 0)


def whole(shape):
    return pl.BlockSpec(shape, lambda *_: (0,) * len(shape))


def spectra(long_filter, tables, block):
    channels, length = long_filter.shape
    n1 = length // LANES
    names = ("plain", "twist", "inner", "inner_low")
    return pl.pallas_call(
        filter_kernel,
        out_shape=jax.ShapeDtypeStruct((channels, n1, 2 * LANES), F32),
        grid=(channels // block,),
        in_specs=[pl.BlockSpec((block, length), lambda i: (i, 0))]
        + [whole(tables[name].shape) for name in names],
        out_specs=pl.BlockSpec((block, n1, 2 * LANES), lambda i: (i, 0, 0)),
        scratch_shapes=[pltpu.VMEM((n1 * block, LANES), F32)],
        compiler_params=grant(20),
        name="spectra",
    )(long_filter, *[tables[name] for name in names])


def conv_kernel(groups, ids_ref, *refs):
    pieces = refs[:groups]
    spec_ref, fore_ref, rear_ref, twist_ref, inner_ref, back_ref = refs[groups : groups + 6]
    outs = refs[groups + 6 : 3 * groups + 6]
    rows_ref, done_ref = refs[3 * groups + 6 :]
    per, block, _ = pieces[0].shape
    n1 = groups * per
    for s in range(groups):
        part = pieces[s][...].astype(F32)
        rows_ref[s * per * block : (s + 1) * per * block, :] = part.reshape(per * block, LANES)
    group = math.gcd(block, 8)

    def body(at, carry):
        base = at * group
        lines = []
        for pair in range(group // 2):
            loaded = [
                rows_ref[pl.ds(base + 2 * pair + c, n1, stride=block), :].astype(BF16)
                for c in range(2)
            ]
            both = jnp.concatenate(loaded, axis=1)
            wide = dot(fore_ref[0], jnp.concatenate([both, both], axis=0))
            for re, im in twisted(wide, twist_ref[0], twist_ref[1], 2):
                lines.append(jnp.concatenate([re.astype(BF16), im.astype(BF16)], axis=1))
        spectrum = dot(jnp.concatenate(lines, axis=0), inner_ref[...])
        other = spec_ref[pl.ds(base, group)].reshape(group * n1, 2 * LANES)
        sig_re, sig_im = spectrum[:, :LANES], spectrum[:, LANES:]
        ker_re, ker_im = other[:, :LANES], other[:, LANES:]
        product = jnp.concatenate(
            [
                (sig_re * ker_re - sig_im * ker_im).astype(BF16),
                (sig_re * ker_im + sig_im * ker_re).astype(BF16),
            ],
            axis=1,
        )
        turned = dot(product, back_ref[...])
        for pair in range(group // 2):
            stacks = []
            for c in range(2):
                at_row = (2 * pair + c) * n1
                re = turned[at_row : at_row + n1, :LANES]
                im = turned[at_row : at_row + n1, LANES:]
                top = (re * twist_ref[0] + im * twist_ref[1]).astype(BF16)
                low = (im * twist_ref[0] - re * twist_ref[1]).astype(BF16)
                stacks.append(jnp.concatenate([top, low, top, low], axis=0))
            result = dot(rear_ref[0], jnp.concatenate(stacks, axis=1))
            for c in range(2):
                done_ref[pl.ds(base + 2 * pair + c, n1, stride=block), :] = result[
                    :, c * LANES : (c + 1) * LANES
                ]
        return carry

    lax.fori_loop(0, block // group, body, 0)
    half = per // 2 * block
    for s in range(2 * groups):
        part = done_ref[s * half : (s + 1) * half, :]
        outs[s][...] = part.reshape(per // 2, block, LANES).astype(BF16)


def long_conv(ids, pieces, spec, tables, block):
    groups = len(pieces)
    per, channels, _ = pieces[0].shape
    n1 = groups * per
    piece = pl.BlockSpec((per, block, LANES), lambda i, ids: (0, i, 0))
    part = pl.BlockSpec((per // 2, block, LANES), lambda i, ids: (0, i, 0))
    mine = lambda shape: pl.BlockSpec((1,) + shape[1:], lambda i, ids: (ids[0], 0, 0))
    return pl.pallas_call(
        functools.partial(conv_kernel, groups),
        out_shape=[jax.ShapeDtypeStruct((per // 2, channels, LANES), BF16)] * (2 * groups),
        grid_spec=pltpu.PrefetchScalarGridSpec(
            num_scalar_prefetch=1,
            grid=(channels // block,),
            in_specs=[piece] * groups
            + [
                pl.BlockSpec((block, n1, 2 * LANES), lambda i, ids: (i, 0, 0)),
                mine(tables["fore"].shape),
                mine(tables["rear"].shape),
                whole(tables["twist"].shape),
                whole(tables["inner"].shape),
                whole(tables["inner_back"].shape),
            ],
            out_specs=[part] * (2 * groups),
            scratch_shapes=[pltpu.VMEM((n1 * block, LANES), F32)] * 2,
        ),
        compiler_params=grant(24),
        name="conv",
    )(
        ids,
        *pieces,
        spec,
        tables["fore"],
        tables["rear"],
        tables["twist"],
        tables["inner"],
        tables["inner_back"],
    )


def query_kernel(query_ref, aux_ref, out_ref):
    aux = aux_ref[...]
    query = short_conv(query_ref[...].astype(F32), aux[:, 9:11], aux[:, 0:3])
    for j in range(out_ref.shape[0]):
        out_ref[j] = query[:, j * LANES : (j + 1) * LANES]


def query_conv(query_proj, aux):
    channels, tokens = query_proj.shape
    block = min(channels, 128)
    count = tokens // LANES
    return pl.pallas_call(
        query_kernel,
        out_shape=jax.ShapeDtypeStruct((count, channels, LANES), F32),
        grid=(channels // block,),
        in_specs=[
            pl.BlockSpec((block, tokens), lambda i: (i, 0)),
            pl.BlockSpec((block, aux.shape[1]), lambda i: (i, 0)),
        ],
        out_specs=pl.BlockSpec((count, block, LANES), lambda i: (0, i, 0)),
        compiler_params=grant(12),
        name="query",
    )(query_proj, aux)


def gate_kernel(groups, ids_ref, *refs):
    pieces = refs[:groups]
    query_ref, left_ref, right_ref = refs[groups:]
    rows = pieces[0].shape[1]
    half = pl.num_programs(0) // 2
    for side, out_ref in enumerate((left_ref, right_ref)):

        @pl.when(pl.program_id(0) // half == side)
        def _():
            for s in range(groups):
                group = lax.rem(ids_ref[0] + groups - s, groups)
                at = pl.ds(pl.multiple_of(group * rows, rows), rows)
                out_ref[at, :] = (query_ref[0, at, :] * pieces[s][0].astype(F32)).astype(BF16)


def gate(ids, pieces, query, start):
    groups = len(pieces)
    per, rows, _ = pieces[0].shape
    channels = query.shape[1]
    half = per // 2
    shape = jax.ShapeDtypeStruct((channels, half * LANES), BF16)
    return pl.pallas_call(
        functools.partial(gate_kernel, groups),
        out_shape=[shape] * 2,
        grid_spec=pltpu.PrefetchScalarGridSpec(
            num_scalar_prefetch=1,
            grid=(per,),
            in_specs=[pl.BlockSpec((1, rows, LANES), lambda j, ids: (j, 0, 0))] * groups
            + [pl.BlockSpec((1, channels, LANES), lambda j, ids: (start + j, 0, 0))],
            out_specs=[
                pl.BlockSpec((channels, LANES), lambda j, ids: (0, jnp.minimum(j, half - 1))),
                pl.BlockSpec((channels, LANES), lambda j, ids: (0, jnp.maximum(j - half, 0))),
            ],
        ),
        compiler_params=grant(12),
        name="gate",
    )(ids, *pieces, query)


def turn_kernel(ids_ref, weight_ref, *out_refs):
    for at, out_ref in enumerate(out_refs):

        @pl.when(pl.program_id(0) == at)
        def _():
            out_ref[...] = weight_ref[...].T


def turned(ids, out_weight, width, shards_of):
    channels = out_weight.shape[0]
    step = min(width, 256)
    inner = width // step
    count = len(shards_of)

    def from_at(k, h, ids):
        shard = shards_of[0](ids)
        for at in range(1, count):
            shard = jnp.where(k == at, shards_of[at](ids), shard)
        return (0, shard * inner + h)

    def out_at(mine):
        return lambda k, h, ids: (
            jnp.where(k == mine, h, jnp.where(k < mine, 0, inner - 1)),
            0,
        )

    return pl.pallas_call(
        turn_kernel,
        out_shape=[jax.ShapeDtypeStruct((width, channels), BF16)] * count,
        grid_spec=pltpu.PrefetchScalarGridSpec(
            num_scalar_prefetch=1,
            grid=(count, inner),
            in_specs=[pl.BlockSpec((channels, step), from_at)],
            out_specs=[pl.BlockSpec((step, channels), out_at(at)) for at in range(count)],
        ),
        compiler_params=grant(12),
        name="turn",
    )(ids, out_weight)


def project_kernel(slot, ids_ref, *refs):
    sources, weights = refs[0:4], refs[4:6]
    sides = refs[6:8], refs[8:10]
    outs = refs[10:12]
    for colour in range(2):
        for partner in range(2):

            @pl.when((pl.program_id(0) == colour) & (((ids_ref[0] & 1) ^ slot) == partner))
            def _():
                out = dot(weights[colour][...], sources[colour][...]) + dot(
                    sides[colour][partner][...], sources[2 + colour][...]
                )
                outs[colour][...] = out.astype(BF16)


def project(ids, own, near, weights, sides, slot):
    width, channels = weights[0].shape
    tokens = own[0].shape[1]
    step = min(width, 512)
    inner = width // step

    def when(active, mine, colour, h):
        return (jnp.where(active, h, jnp.where(colour > mine, inner - 1, 0)), 0)

    def side_at(mine, partner):
        def at(colour, h, ids):
            chosen = ((ids[0] & 1) ^ slot) == partner
            return when((colour == mine) & chosen, mine, jnp.where(chosen, colour, mine), h)

        return at

    def colour_at(mine):
        return lambda colour, h, ids: when(colour == mine, mine, colour, h)

    return pl.pallas_call(
        functools.partial(project_kernel, slot),
        out_shape=[jax.ShapeDtypeStruct((width, tokens), BF16)] * 2,
        grid_spec=pltpu.PrefetchScalarGridSpec(
            num_scalar_prefetch=1,
            grid=(2, inner),
            in_specs=[whole((channels, tokens))] * 4
            + [pl.BlockSpec((step, channels), colour_at(colour)) for colour in range(2)]
            + [
                pl.BlockSpec((step, channels), side_at(colour, partner))
                for colour in range(2)
                for partner in range(2)
            ],
            out_specs=[pl.BlockSpec((step, tokens), colour_at(colour)) for colour in range(2)],
        ),
        compiler_params=grant(20),
        name="project",
    )(ids, *own, *near, *weights, *sides[0], *sides[1])


def medium_spectrum(taps, fore_ref, low_ref):
    width = taps.shape[0]
    over_taps = (((0,), (0,)), ((), ()))
    spec = lax.dot_general(taps, fore_ref[:width], over_taps, preferred_element_type=F32)
    spec = spec + lax.dot_general(taps, low_ref[:width], over_taps, preferred_element_type=F32)
    return spec[:, :width], spec[:, width:]


def medium_blocks(wide, ker_re, ker_im, fore_ref, low_ref, back_ref):
    width = ker_re.shape[1]
    out = []
    for b in range(wide.shape[1] // width - 1):
        window = wide[:, b * width : (b + 2) * width]
        sig = dot(window, fore_ref[...]) + dot(window, low_ref[...])
        sig_re, sig_im = sig[:, :width], sig[:, width:]
        product = jnp.concatenate(
            [
                (sig_re * ker_re - sig_im * ker_im).astype(BF16),
                (sig_re * ker_im + sig_im * ker_re).astype(BF16),
            ],
            axis=1,
        )
        out.append(dot(product, back_ref[...]).astype(BF16))
    return jnp.concatenate(out, axis=1)


def joined(parts, counts):
    refs, out = list(parts), []
    for count in counts:
        total = refs.pop(0)[...].astype(F32)
        for _ in range(count - 1):
            total = total + refs.pop(0)[...].astype(F32)
        out.append(total.astype(BF16))
    return jnp.concatenate(out, axis=1)


def late_kernel(counts, *refs):
    n = sum(counts)
    taps_ref, fore_ref, low_ref, back_ref, oper_ref, edge_ref, out_ref = refs[n:]
    value = joined(refs[:n], counts)
    oper_ref[...] = value
    edge_ref[...] = value[:, -edge_ref.shape[1] :]
    ker_re, ker_im = medium_spectrum(taps_ref[...], fore_ref, low_ref)
    out_ref[...] = medium_blocks(value, ker_re, ker_im, fore_ref, low_ref, back_ref)


def early_kernel(counts, *refs):
    n = sum(counts)
    edge_ref, later_ref, tail_ref, taps_ref, fore_ref, low_ref, back_ref, oper_ref, out_ref = refs[
        n:
    ]
    value = joined(refs[:n], counts)
    later = later_ref[...]
    half = value.shape[1]
    oper_ref[:, :half] = value
    oper_ref[:, half:] = later
    ker_re, ker_im = medium_spectrum(taps_ref[...], fore_ref, low_ref)
    width = ker_re.shape[1]
    wide = jnp.concatenate([edge_ref[...], value, later[:, :width]], axis=1)
    out_ref[:, : half + width] = medium_blocks(wide, ker_re, ker_im, fore_ref, low_ref, back_ref)
    out_ref[:, half + width :] = tail_ref[...]


def medium_call(kernel, parts, extra, taps, tables, widths):
    counts = tuple(len(p) for p in parts)
    arrays = [array for part in parts for array in part] + list(extra)
    channels = arrays[0].shape[0]
    width = taps.shape[0]
    block = min(channels, 256)
    row = lambda n: pl.BlockSpec((block, n), lambda i: (i, 0))
    return pl.pallas_call(
        functools.partial(kernel, counts),
        out_shape=[jax.ShapeDtypeStruct((channels, n), BF16) for n in widths],
        grid=(channels // block,),
        in_specs=[row(array.shape[1]) for array in arrays]
        + [pl.BlockSpec((width, block), lambda i: (0, i))]
        + [whole(t.shape) for t in tables],
        out_specs=[row(n) for n in widths],
        compiler_params=grant(16),
    )(*arrays, taps, *tables)


def ring(block, axis, distance):
    count = lax.axis_size(axis)
    return lax.ppermute(block, axis, [(i, (i + distance) % count) for i in range(count)])


def forward(block, axis):
    count = lax.axis_size(axis)
    return lax.ppermute(block, axis, [(i, i + 1) for i in range(count - 1)])


def swapped(block, axis, bit):
    return lax.ppermute(block, axis, [(i, i ^ bit) for i in range(lax.axis_size(axis))])


def neighbour_weights(ids, out_weight, width):
    slabs = turned(
        ids,
        out_weight,
        width,
        (lambda ids: ids[1] ^ 1 ^ ((ids[0] & 1) * 2), lambda ids: ids[1] ^ 2 ^ (ids[0] & 1)),
    )
    return [swapped(slabs[0], "tp", 1), swapped(slabs[1], "tp", 2)]


def both_cores(sides, after):
    held = lax.optimization_barrier((*sides, after))
    out = []
    for straight in held[:2]:
        out.append((straight, swapped(straight, "ctx", 1)))
    return out, held[2]


def operator_parts(ids, gated, out_weight, weights, sides):
    if sides is None:
        source = jnp.concatenate(gated, axis=1)
        partial = lax.dot_general(
            out_weight, source, (((0,), (0,)), ((), ())), preferred_element_type=F32
        ).astype(BF16)
        return [[lax.psum_scatter(partial, "tp", scatter_dimension=0, tiled=True)]]
    near = [swapped(gated[0], "tp", 1), swapped(gated[1], "tp", 2)]
    send = project(ids, gated, near, (weights[2], weights[1]), sides, 1)
    got = [swapped(send[0], "tp", 2), swapped(send[1], "tp", 1)]
    keep = project(ids, gated, near, (weights[0], weights[0]), sides, 0)
    return [[keep[0], got[0]], [keep[1], got[1]]]


def shards(query_proj, key_proj, value_proj, short_taps, long_filter, out_weight, medium_taps):
    channels, tokens = query_proj.shape
    groups = lax.axis_size("ctx")
    length = long_filter.shape[1]
    tables = long_tables(length, groups)
    ids = jnp.stack([lax.axis_index("ctx"), lax.axis_index("tp")]).astype(jnp.int32)
    tails = [x[:, -2:] for x in (query_proj, key_proj, value_proj)]
    edges = forward(jnp.concatenate(tails, axis=1), "ctx").astype(F32)
    flat_taps = short_taps.reshape(9, channels).T
    aux = jnp.concatenate([flat_taps, edges, jnp.zeros((channels, 1), F32)], axis=1)
    owned = long_filter.shape[0]
    spec = spectra(long_filter, tables, min(owned, 16))
    batch = groups // 2
    far = mix(ids, key_proj, value_proj, aux, batch, batch, groups)
    near = mix(ids, key_proj, value_proj, aux, 0, batch, groups)
    sent = list(near) + list(far)
    sides, weights = None, None
    if lax.axis_size("tp") == 4:
        part = out_weight.shape[1] // 4
        held = lax.optimization_barrier((out_weight, near[0]))
        sent[0] = held[1]
        sides = neighbour_weights(ids, held[0], part)
        weights = turned(
            ids,
            held[0],
            part,
            (lambda ids: ids[1], lambda ids: ids[1] ^ 1, lambda ids: ids[1] ^ 2),
        )
    query = query_conv(query_proj, aux)
    pieces = [sent[0]]
    for s in range(1, groups):
        pieces.append(ring(sent[s], "ctx", s))
    results = list(long_conv(ids, pieces, spec, tables, min(owned, 32)))
    if sides is not None:
        sides, results[0] = both_cores(sides, results[0])
    width = medium_taps.shape[0]
    half = tokens // 2
    done = []
    for h in (1, 0):
        mine = results[h::2]
        back = [mine[0]] + [ring(mine[s], "ctx", s) for s in range(1, groups)]
        gated = gate(ids, back, query, h * half // LANES)
        parts = operator_parts(ids, gated, out_weight, weights, sides)
        if h == 1:
            later, edge, tail = medium_call(
                late_kernel,
                parts,
                (),
                medium_taps,
                medium_tables(width),
                (half, width, half - width),
            )
            edge = forward(edge, "ctx")
        else:
            done = medium_call(
                early_kernel,
                parts,
                (edge, later, tail),
                medium_taps,
                medium_tables(width),
                (tokens, tokens),
            )
    return tuple(done)


def solution(mesh):
    in_specs = (
        P("tp", "ctx"),
        P("tp", "ctx"),
        P("tp", "ctx"),
        P(None, None, "tp"),
        P(("tp", "ctx"), None),
        P("tp", None),
        P(None, "tp"),
    )
    out_specs = (P("tp", "ctx"), P("tp", "ctx"))
    return jax.shard_map(shards, mesh=mesh, in_specs=in_specs, out_specs=out_specs, check_vma=False)
```

profile of v0, /device:TPU:0, one launch (start us, length us, event | category | flops | bytes accessed | tf_op | source)
XLA Modules:
  0.0 200.4 jit_solution(2640098272193213855)
XLA Ops:
  0.7 1.2 slice.9
  4.5 2.4 %collective-permute-start = (bf16[1024,6]{0,1:T(8,128)(2,1)S(1)}, bf16[1024,6]{0,1:T(8,128)(2,1)S(1)}, u32[]{:S(2)}, u32[]{:S(2)}) collective-permute-start(bf16[1024,6]{0,1:T(8,128)(2,1)S(1)} %pad_maximum_fusion), channel_id=1, source_target_pairs={{0,4},{4,8},{8,12},{12,16},{16,20},{20,24},{24,28},{1,5},{5,9},{9,... | collective-permute-start | bytes 36872 | tf_op jit(solution)/shard_map/ppermute | solution.py:538
  8.1 1.6 copy-done.2
  9.7 3.8 %mix.2 = (bf16[8,128,128]{2,1,0:T(8,128)(2,1)S(1)}, bf16[8,128,128]{2,1,0:T(8,128)(2,1)S(1)}, bf16[8,128,128]{2,1,0:T(8,128)(2,1)S(1)}, bf16[8,128,128]{2,1,0:T(8,128)(2,1)S(1)}) custom-call(s32[2]{0:T(128)S(1)} %pad_add_fusion.ids_ref, bf16[1024,1024]{1,0:T(8,128)(2,1)S(1)} %copy-done.1, bf16[1024,1024]{1,0:T(8,128)(2,1)S(1)} %copy-done.2, ...), custom_call_target="tpu_custom_call" | custom-call | tf_op jit(solution)/shard_map/mix/pallas_call | solution.py:109
  13.5 3.4 %copy-done = bf16[1024,4096]{1,0:T(8,128)(2,1)S(1)} copy-done((bf16[1024,4096]{1,0:T(8,128)(2,1)S(1)}, bf16[1024,4096]{1,0:T(8,128)(2,1)}, u32[]{:S(2)}) %copy-start) | copy-done | bytes 8388632
  16.8 2.9 %turn.2 = (bf16[1024,1024]{1,0:T(8,128)(2,1)S(1)}, bf16[1024,1024]{1,0:T(8,128)(2,1)S(1)}) custom-call(s32[2]{0:T(128)S(1)} %pad_add_fusion.ids_ref, bf16[1024,4096]{1,0:T(8,128)(2,1)S(1)} %copy-done), custom_call_target="tpu_custom_call" | custom-call | tf_op jit(solution)/shard_map/turn/pallas_call | solution.py:381
  19.8 2.4 %collective-permute-start.1 = (bf16[1024,1024]{1,0:T(8,128)(2,1)S(1)}, bf16[1024,1024]{1,0:T(8,128)(2,1)S(1)}, u32[]{:S(2)}, u32[]{:S(2)}) collective-permute-start(bf16[1024,1024]{1,0:T(8,128)(2,1)S(1)} %get-tuple-element.53), channel_id=1, source_target_pairs={{0,1},{1,0},{2,3},{3,2},{4,5},{5,4},{6,7},{7,6},{8,9},{9,8},{10,11... | collective-permute-start | bytes 6291464 | tf_op jit(solution)/shard_map/ppermute | solution.py:542
  22.2 1.5 collective-permute-start.2
  23.7 1.3 collective-permute-start.3
  25.0 2.8 %collective-permute-start.4 = (bf16[8,128,128]{2,1,0:T(8,128)(2,1)S(1)}, bf16[8,128,128]{2,1,0:T(8,128)(2,1)S(1)}, u32[]{:S(2)}, u32[]{:S(2)}) collective-permute-start(bf16[8,128,128]{2,1,0:T(8,128)(2,1)S(1)} %get-tuple-element.57), channel_id=1, source_target_pairs={{0,8},{4,12},{8,16},{12,20},{16,24},{20,28},{24,0},{28,4},{1,9},{5... | collective-permute-start | bytes 786440 | tf_op jit(solution)/shard_map/ppermute | solution.py:533
  27.8 3.8 %mix.3 = (bf16[8,128,128]{2,1,0:T(8,128)(2,1)S(1)}, bf16[8,128,128]{2,1,0:T(8,128)(2,1)S(1)}, bf16[8,128,128]{2,1,0:T(8,128)(2,1)S(1)}, bf16[8,128,128]{2,1,0:T(8,128)(2,1)S(1)}) custom-call(s32[2]{0:T(128)S(1)} %pad_add_fusion.ids_ref, bf16[1024,1024]{1,0:T(8,128)(2,1)S(1)} %copy-done.1, bf16[1024,1024]{1,0:T(8,128)(2,1)S(1)} %copy-done.3, ...), custom_call_target="tpu_custom_call" | custom-call | tf_op jit(solution)/shard_map/mix/pallas_call | solution.py:109
  31.7 2.6 %collective-permute-start.5 = (bf16[8,128,128]{2,1,0:T(8,128)(2,1)S(1)}, bf16[8,128,128]{2,1,0:T(8,128)(2,1)S(1)}, u32[]{:S(2)}, u32[]{:S(2)}) collective-permute-start(bf16[8,128,128]{2,1,0:T(8,128)(2,1)S(1)} %get-tuple-element.58), channel_id=1, source_target_pairs={{0,12},{4,16},{8,20},{12,24},{16,28},{20,0},{24,4},{28,8},{1,13},{... | collective-permute-start | bytes 786440 | tf_op jit(solution)/shard_map/ppermute | solution.py:533
  34.3 2.4 %collective-permute-start.6 = (bf16[8,128,128]{2,1,0:T(8,128)(2,1)S(1)}, bf16[8,128,128]{2,1,0:T(8,128)(2,1)S(1)}, u32[]{:S(2)}, u32[]{:S(2)}) collective-permute-start(bf16[8,128,128]{2,1,0:T(8,128)(2,1)S(1)} %get-tuple-element.59), channel_id=1, source_target_pairs={{0,16},{4,20},{8,24},{12,28},{16,0},{20,4},{24,8},{28,12},{1,17},{... | collective-permute-start | bytes 786440 | tf_op jit(solution)/shard_map/ppermute | solution.py:533
  36.7 6.3 %collective-permute-start.7 = (bf16[8,128,128]{2,1,0:T(8,128)(2,1)S(1)}, bf16[8,128,128]{2,1,0:T(8,128)(2,1)S(1)}, u32[]{:S(2)}, u32[]{:S(2)}) collective-permute-start(bf16[8,128,128]{2,1,0:T(8,128)(2,1)S(1)} %get-tuple-element.60), channel_id=1, source_target_pairs={{0,20},{4,24},{8,28},{12,0},{16,4},{20,8},{24,12},{28,16},{1,21},{... | collective-permute-start | bytes 786440 | tf_op jit(solution)/shard_map/ppermute | solution.py:533
  43.0 13.6 %collective-permute-done.5.refs_3_ = bf16[8,128,128]{2,1,0:T(8,128)(2,1)S(1)} collective-permute-done((bf16[8,128,128]{2,1,0:T(8,128)(2,1)S(1)}, bf16[8,128,128]{2,1,0:T(8,128)(2,1)S(1)}, u32[]{:S(2)}, u32[]{:S(2)}) %collective-permute-start.5) | collective-permute-done | bytes 262176 | tf_op jit(solution)/shard_map/ppermute | solution.py:533
  56.6 9.1 %collective-permute-start.8 = (bf16[8,128,128]{2,1,0:T(8,128)(2,1)S(1)}, bf16[8,128,128]{2,1,0:T(8,128)(2,1)S(1)}, u32[]{:S(2)}, u32[]{:S(2)}) collective-permute-start(bf16[8,128,128]{2,1,0:T(8,128)(2,1)S(1)} %get-tuple-element.61), channel_id=1, source_target_pairs={{0,24},{4,28},{8,0},{12,4},{16,8},{20,12},{24,16},{28,20},{1,25},{... | collective-permute-start | bytes 786440 | tf_op jit(solution)/shard_map/ppermute | solution.py:533
  65.7 7.9 %collective-permute-start.9 = (bf16[8,128,128]{2,1,0:T(8,128)(2,1)S(1)}, bf16[8,128,128]{2,1,0:T(8,128)(2,1)S(1)}, u32[]{:S(2)}, u32[]{:S(2)}) collective-permute-start(bf16[8,128,128]{2,1,0:T(8,128)(2,1)S(1)} %get-tuple-element.62), channel_id=1, source_target_pairs={{0,28},{4,0},{8,4},{12,8},{16,12},{20,16},{24,20},{28,24},{1,29},{... | collective-permute-start | bytes 786440 | tf_op jit(solution)/shard_map/ppermute | solution.py:533
  73.7 8.9 %spectra.1.refs_8_ = f32[128,64,256]{2,1,0:T(8,128)S(1)} custom-call(f32[128,8192]{1,0:T(8,128)S(1)} %copy-done.4, bf16[128,192]{1,0:T(8,128)(2,1)S(1)} %copy-done.16, f32[2,64,128]{2,1,0:T(8,128)S(1)} %copy-done.10, bf16[256,256]{1,0:T(8,128)(2,1)S(1)} %copy-done.7, bf16[256,256]{1,0:T(8,128)(2,1)S(1)} %copy-done.15), custom_call_target="tpu_custom_call" | custom-call | tf_op jit(solution)/shard_map/spectra/pallas_call | solution.py:180
  82.6 14.9 %conv.1 = (bf16[4,128,128]{2,1,0:T(8,128)(2,1)S(1)}, bf16[4,128,128]{2,1,0:T(8,128)(2,1)S(1)}, bf16[4,128,128]{2,1,0:T(8,128)(2,1)S(1)}, bf16[4,128,128]{2,1,0:T...) custom-call(s32[2]{0:T(128)S(1)} %pad_add_fusion.ids_ref, ...), custom_call_target="tpu_custom_call" | custom-call | tf_op jit(solution)/shard_map/conv/pallas_call | solution.py:259
  98.7 6.5 %collective-permute-done.23.refs_1_ = bf16[4,128,128]{2,1,0:T(8,128)(2,1)S(1)} collective-permute-done((bf16[4,128,128]{2,1,0:T(8,128)(2,1)S(1)}, bf16[4,128,128]{2,1,0:T(8,128)(2,1)S(1)}, u32[]{:S(2)}, u32[]{:S(2)}) %collective-permute-start.23) | collective-permute-done | bytes 131104 | tf_op jit(solution)/shard_map/ppermute | solution.py:533
  105.2 1.3 collective-permute-done.24.refs_2_
  107.2 9.6 %collective-permute-done.25.refs_3_ = bf16[4,128,128]{2,1,0:T(8,128)(2,1)S(1)} collective-permute-done((bf16[4,128,128]{2,1,0:T(8,128)(2,1)S(1)}, bf16[4,128,128]{2,1,0:T(8,128)(2,1)S(1)}, u32[]{:S(2)}, u32[]{:S(2)}) %collective-permute-start.25) | collective-permute-done | bytes 131104 | tf_op jit(solution)/shard_map/ppermute | solution.py:533
  117.1 2.2 %collective-permute-start.29 = (bf16[4,128,128]{2,1,0:T(8,128)(2,1)S(1)}, bf16[4,128,128]{2,1,0:T(8,128)(2,1)S(1)}, u32[]{:S(2)}, u32[]{:S(2)}) collective-permute-start(bf16[4,128,128]{2,1,0:T(8,128)(2,1)S(1)} %get-tuple-element.90), channel_id=1, source_target_pairs={{0,28},{4,0},{8,4},{12,8},{16,12},{20,16},{24,20},{28,24},{1,29},{... | collective-permute-start | bytes 393224 | tf_op jit(solution)/shard_map/ppermute | solution.py:533
  119.7 2.1 %collective-permute-done.28.refs_6_ = bf16[4,128,128]{2,1,0:T(8,128)(2,1)S(1)} collective-permute-done((bf16[4,128,128]{2,1,0:T(8,128)(2,1)S(1)}, bf16[4,128,128]{2,1,0:T(8,128)(2,1)S(1)}, u32[]{:S(2)}, u32[]{:S(2)}) %collective-permute-start.28) | collective-permute-done | bytes 131104 | tf_op jit(solution)/shard_map/ppermute | solution.py:533
  121.8 1.4 collective-permute-start.11
  123.3 3.8 %collective-permute-start.12 = (bf16[4,128,128]{2,1,0:T(8,128)(2,1)S(1)}, bf16[4,128,128]{2,1,0:T(8,128)(2,1)S(1)}, u32[]{:S(2)}, u32[]{:S(2)}) collective-permute-start(bf16[4,128,128]{2,1,0:T(8,128)(2,1)S(1)} %get-tuple-element.67), channel_id=1, source_target_pairs={{0,12},{4,16},{8,20},{12,24},{16,28},{20,0},{24,4},{28,8},{1,13},{... | collective-permute-start | bytes 393224 | tf_op jit(solution)/shard_map/ppermute | solution.py:533
  127.1 3.6 %query.1.refs_8_ = f32[8,1024,128]{2,1,0:T(8,128)S(1)} custom-call(bf16[1024,1024]{1,0:T(8,128)(2,1)S(1)} %copy-done.5, f32[1024,16]{1,0:T(8,128)S(1)} %copy.24.aux_ref), custom_call_target="tpu_custom_call" | custom-call | tf_op jit(solution)/shard_map/query/pallas_call | solution.py:302
  130.8 1.1 gate.3
  132.5 1.7 collective-permute-done.12.refs_3_
  134.6 8.2 %collective-permute-done.13.refs_4_ = bf16[4,128,128]{2,1,0:T(8,128)(2,1)S(1)} collective-permute-done((bf16[4,128,128]{2,1,0:T(8,128)(2,1)S(1)}, bf16[4,128,128]{2,1,0:T(8,128)(2,1)S(1)}, u32[]{:S(2)}, u32[]{:S(2)}) %collective-permute-start.13) | collective-permute-done | bytes 131104 | tf_op jit(solution)/shard_map/ppermute | solution.py:533
  143.2 1.8 collective-permute-start.15
  145.0 4.8 %collective-permute-done.15.refs_6_ = bf16[4,128,128]{2,1,0:T(8,128)(2,1)S(1)} collective-permute-done((bf16[4,128,128]{2,1,0:T(8,128)(2,1)S(1)}, bf16[4,128,128]{2,1,0:T(8,128)(2,1)S(1)}, u32[]{:S(2)}, u32[]{:S(2)}) %collective-permute-start.15) | collective-permute-done | bytes 131104 | tf_op jit(solution)/shard_map/ppermute | solution.py:533
  149.8 2.6 %collective-permute-start.16 = (bf16[4,128,128]{2,1,0:T(8,128)(2,1)S(1)}, bf16[4,128,128]{2,1,0:T(8,128)(2,1)S(1)}, u32[]{:S(2)}, u32[]{:S(2)}) collective-permute-start(bf16[4,128,128]{2,1,0:T(8,128)(2,1)S(1)} %get-tuple-element.71), channel_id=1, source_target_pairs={{0,28},{4,0},{8,4},{12,8},{16,12},{20,16},{24,20},{28,24},{1,29},{... | collective-permute-start | bytes 393224 | tf_op jit(solution)/shard_map/ppermute | solution.py:533
  152.4 2.5 %collective-permute-done.16.refs_7_ = bf16[4,128,128]{2,1,0:T(8,128)(2,1)S(1)} collective-permute-done((bf16[4,128,128]{2,1,0:T(8,128)(2,1)S(1)}, bf16[4,128,128]{2,1,0:T(8,128)(2,1)S(1)}, u32[]{:S(2)}, u32[]{:S(2)}) %collective-permute-start.16) | collective-permute-done | bytes 131104 | tf_op jit(solution)/shard_map/ppermute | solution.py:533
  156.0 1.4 collective-permute-start.17
  157.4 4.2 %turn.3 = (bf16[1024,1024]{1,0:T(8,128)(2,1)S(1)}, bf16[1024,1024]{1,0:T(8,128)(2,1)S(1)}, bf16[1024,1024]{1,0:T(8,128)(2,1)S(1)}) custom-call(s32[2]{0:T(128)S(1)} %pad_add_fusion.ids_ref, bf16[1024,4096]{1,0:T(8,128)(2,1)S(1)} %bitcast.5), custom_call_target="tpu_custom_call" | custom-call | tf_op jit(solution)/shard_map/turn/pallas_call | solution.py:381
  161.7 3.7 %project.7 = (bf16[1024,256]{1,0:T(8,128)(2,1)S(1)}, bf16[1024,256]{1,0:T(8,128)(2,1)S(1)}) custom-call(s32[2]{0:T(128)S(1)} %pad_add_fusion.ids_ref, bf16[1024,256]{1,0:T(8,128)(2,1)S(1)} %get-tuple-element.91.refs_0_, bf16[1024,256]{1,0:T(8,128)(2,1)S(1)} %get-tuple-element.92.refs_1_, bf16[1024,256]{1,0:T(8,128)(2,1)S(1)} %collective-permute-done.30.refs_2_, ...), custom_call_target="tpu_custom_call" | custom-call | tf_op jit(solution)/shard_map/project/pallas_call | solution.py:429
  165.4 2.1 %collective-permute-start.32 = (bf16[1024,256]{1,0:T(8,128)(2,1)S(1)}, bf16[1024,256]{1,0:T(8,128)(2,1)S(1)}, u32[]{:S(2)}, u32[]{:S(2)}) collective-permute-start(bf16[1024,256]{1,0:T(8,128)(2,1)S(1)} %get-tuple-element.94), channel_id=1, source_target_pairs={{0,2},{1,3},{2,0},{3,1},{4,6},{5,7},{6,4},{7,5},{8,10},{9,11},{10,... | collective-permute-start | bytes 1572872 | tf_op jit(solution)/shard_map/ppermute | solution.py:542
  168.2 2.4 %collective-permute-done.17.refs_2_ = bf16[1024,256]{1,0:T(8,128)(2,1)S(1)} collective-permute-done((bf16[1024,256]{1,0:T(8,128)(2,1)S(1)}, bf16[1024,256]{1,0:T(8,128)(2,1)S(1)}, u32[]{:S(2)}, u32[]{:S(2)}) %collective-permute-start.17) | collective-permute-done | bytes 524320 | tf_op jit(solution)/shard_map/ppermute | solution.py:542
  170.6 1.6 collective-permute-done.18.refs_3_
  172.2 3.7 %project.5 = (bf16[1024,256]{1,0:T(8,128)(2,1)S(1)}, bf16[1024,256]{1,0:T(8,128)(2,1)S(1)}) custom-call(s32[2]{0:T(128)S(1)} %pad_add_fusion.ids_ref, bf16[1024,256]{1,0:T(8,128)(2,1)S(1)} %get-tuple-element.72.refs_0_, bf16[1024,256]{1,0:T(8,128)(2,1)S(1)} %get-tuple-element.73.refs_1_, bf16[1024,256]{1,0:T(8,128)(2,1)S(1)} %collective-permute-done.17.refs_2_, ...), custom_call_target="tpu_custom_call" | custom-call | tf_op jit(solution)/shard_map/project/pallas_call | solution.py:429
  176.8 3.7 %project.6 = (bf16[1024,256]{1,0:T(8,128)(2,1)S(1)}, bf16[1024,256]{1,0:T(8,128)(2,1)S(1)}) custom-call(s32[2]{0:T(128)S(1)} %pad_add_fusion.ids_ref, bf16[1024,256]{1,0:T(8,128)(2,1)S(1)} %get-tuple-element.91.refs_0_, bf16[1024,256]{1,0:T(8,128)(2,1)S(1)} %get-tuple-element.92.refs_1_, bf16[1024,256]{1,0:T(8,128)(2,1)S(1)} %collective-permute-done.30.refs_2_, ...), custom_call_target="tpu_custom_call" | custom-call | tf_op jit(solution)/shard_map/project/pallas_call | solution.py:429
  180.5 3.0 %collective-permute-done.32.refs_1_ = bf16[1024,256]{1,0:T(8,128)(2,1)S(1)} collective-permute-done((bf16[1024,256]{1,0:T(8,128)(2,1)S(1)}, bf16[1024,256]{1,0:T(8,128)(2,1)S(1)}, u32[]{:S(2)}, u32[]{:S(2)}) %collective-permute-start.32) | collective-permute-done | bytes 524320 | tf_op jit(solution)/shard_map/ppermute | solution.py:542
  183.5 3.6 %shard_map.176 = (bf16[1024,512]{1,0:T(8,128)(2,1)S(1)}, bf16[1024,128]{1,0:T(8,128)(2,1)S(1)}, bf16[1024,384]{1,0:T(8,128)(2,1)S(1)}) custom-call(bf16[1024,256]{1,0:T(8,128)(2,1)S(1)} %get-tuple-element.93.refs_0_, bf16[1024,256]{1,0:T(8,128)(2,1)S(1)} %collective-permute-done.32.refs_1_, bf16[1024,256]{1,0:T(8,128)(2,1)S(1)} %get-tuple-element.95.refs_2_, ...), custom_call_target="tpu_custom_call" | custom-call | tf_op jit(solution)/shard_map/pallas_call | solution.py:519
  187.1 1.3 collective-permute-start.34
  188.4 3.7 %project.4 = (bf16[1024,256]{1,0:T(8,128)(2,1)S(1)}, bf16[1024,256]{1,0:T(8,128)(2,1)S(1)}) custom-call(s32[2]{0:T(128)S(1)} %pad_add_fusion.ids_ref, bf16[1024,256]{1,0:T(8,128)(2,1)S(1)} %get-tuple-element.72.refs_0_, bf16[1024,256]{1,0:T(8,128)(2,1)S(1)} %get-tuple-element.73.refs_1_, bf16[1024,256]{1,0:T(8,128)(2,1)S(1)} %collective-permute-done.17.refs_2_, ...), custom_call_target="tpu_custom_call" | custom-call | tf_op jit(solution)/shard_map/project/pallas_call | solution.py:429
  192.1 1.6 collective-permute-done.21.refs_1_
  193.8 6.6 %shard_map.177 = (bf16[1024,1024]{1,0:T(8,128)(2,1)}, bf16[1024,1024]{1,0:T(8,128)(2,1)}) custom-call(bf16[1024,256]{1,0:T(8,128)(2,1)S(1)} %get-tuple-element.77.refs_0_, bf16[1024,256]{1,0:T(8,128)(2,1)S(1)} %collective-permute-done.21.refs_1_, bf16[1024,256]{1,0:T(8,128)(2,1)S(1)} %get-tuple-element.81.refs_2_, ...), custom_call_target="tpu_custom_call" | custom-call | tf_op jit(solution)/shard_map/pallas_call | solution.py:519
  (91 shorter events, 10.4 us)
Async XLA Ops:
  0.6 7.4 %copy-start.1 = (bf16[1024,1024]{1,0:T(8,128)(2,1)S(1)}, bf16[1024,1024]{1,0:T(8,128)(2,1)}, u32[]{:S(2)}) copy-start(bf16[1024,1024]{1,0:T(8,128)(2,1)} %key_ref.3) | copy-start | bytes 6291460
  4.5 3.2 %collective-permute-start = (bf16[1024,6]{0,1:T(8,128)(2,1)S(1)}, bf16[1024,6]{0,1:T(8,128)(2,1)S(1)}, u32[]{:S(2)}, u32[]{:S(2)}) collective-permute-start(bf16[1024,6]{0,1:T(8,128)(2,1)S(1)} %pad_maximum_fusion), channel_id=1, source_target_pairs={{0,4},{4,8},{8,12},{12,16},{16,20},{20,24},{24,28},{1,5},{5,9},{9,... | collective-permute-start | bytes 36872 | tf_op jit(solution)/shard_map/ppermute | solution.py:538
  16.8 11.0 %copy-start.3 = (bf16[1024,1024]{1,0:T(8,128)(2,1)S(1)}, bf16[1024,1024]{1,0:T(8,128)(2,1)}, u32[]{:S(2)}) copy-start(bf16[1024,1024]{1,0:T(8,128)(2,1)} %value_ref.3) | copy-start | bytes 6291460
  19.8 77.8 %collective-permute-start.1 = (bf16[1024,1024]{1,0:T(8,128)(2,1)S(1)}, bf16[1024,1024]{1,0:T(8,128)(2,1)S(1)}, u32[]{:S(2)}, u32[]{:S(2)}) collective-permute-start(bf16[1024,1024]{1,0:T(8,128)(2,1)S(1)} %get-tuple-element.53), channel_id=1, source_target_pairs={{0,1},{1,0},{2,3},{3,2},{4,5},{5,4},{6,7},{7,6},{8,9},{9,8},{10,11... | collective-permute-start | bytes 6291464 | tf_op jit(solution)/shard_map/ppermute | solution.py:542
  22.2 75.4 %collective-permute-start.2 = (bf16[1024,1024]{1,0:T(8,128)(2,1)S(1)}, bf16[1024,1024]{1,0:T(8,128)(2,1)S(1)}, u32[]{:S(2)}, u32[]{:S(2)}) collective-permute-start(bf16[1024,1024]{1,0:T(8,128)(2,1)S(1)} %get-tuple-element.54), channel_id=1, source_target_pairs={{0,2},{1,3},{2,0},{3,1},{4,6},{5,7},{6,4},{7,5},{8,10},{9,11},{10,... | collective-permute-start | bytes 6291464 | tf_op jit(solution)/shard_map/ppermute | solution.py:542
  23.7 10.6 %collective-permute-start.3 = (bf16[8,128,128]{2,1,0:T(8,128)(2,1)S(1)}, bf16[8,128,128]{2,1,0:T(8,128)(2,1)S(1)}, u32[]{:S(2)}, u32[]{:S(2)}) collective-permute-start(bf16[8,128,128]{2,1,0:T(8,128)(2,1)S(1)} %get-tuple-element.56), channel_id=1, source_target_pairs={{0,4},{4,8},{8,12},{12,16},{16,20},{20,24},{24,28},{28,0},{1,5},{5... | collective-permute-start | bytes 786440 | tf_op jit(solution)/shard_map/ppermute | solution.py:533
  25.0 48.6 %copy-start.4 = (f32[128,8192]{1,0:T(8,128)S(1)}, f32[128,8192]{1,0:T(8,128)}, u32[]{:S(2)}) copy-start(f32[128,8192]{1,0:T(8,128)} %filter_ref.1) | copy-start | bytes 12582916
  25.0 48.6 %copy-start.7 = (bf16[256,256]{1,0:T(8,128)(2,1)S(1)}, bf16[256,256]{1,0:T(8,128)(2,1)}, u32[]{:S(2)}) copy-start(bf16[256,256]{1,0:T(8,128)(2,1)} %constant.33.clone.inner_ref.refs_12_) | copy-start | bytes 393220
  25.0 48.6 %copy-start.10 = (f32[2,64,128]{2,1,0:T(8,128)S(1)}, f32[2,64,128]{2,1,0:T(8,128)}, u32[]{:S(2)}) copy-start(f32[2,64,128]{2,1,0:T(8,128)} %constant.32.clone.twist_ref.refs_11_) | copy-start | bytes 196612
  25.0 48.6 %copy-start.15 = (bf16[256,256]{1,0:T(8,128)(2,1)S(1)}, bf16[256,256]{1,0:T(8,128)(2,1)}, u32[]{:S(2)}) copy-start(bf16[256,256]{1,0:T(8,128)(2,1)} %constant.34.clone.inner_low_ref) | copy-start | bytes 393220
  25.0 48.6 %copy-start.16 = (bf16[128,192]{1,0:T(8,128)(2,1)S(1)}, bf16[128,192]{1,0:T(8,128)(2,1)}, u32[]{:S(2)}) copy-start(bf16[128,192]{1,0:T(8,128)(2,1)} %constant.31.clone.plain_ref) | copy-start | bytes 147460
  25.0 11.7 %collective-permute-start.4 = (bf16[8,128,128]{2,1,0:T(8,128)(2,1)S(1)}, bf16[8,128,128]{2,1,0:T(8,128)(2,1)S(1)}, u32[]{:S(2)}, u32[]{:S(2)}) collective-permute-start(bf16[8,128,128]{2,1,0:T(8,128)(2,1)S(1)} %get-tuple-element.57), channel_id=1, source_target_pairs={{0,8},{4,12},{8,16},{12,20},{16,24},{20,28},{24,0},{28,4},{1,9},{5... | collective-permute-start | bytes 786440 | tf_op jit(solution)/shard_map/ppermute | solution.py:533
  31.7 24.9 %collective-permute-start.5 = (bf16[8,128,128]{2,1,0:T(8,128)(2,1)S(1)}, bf16[8,128,128]{2,1,0:T(8,128)(2,1)S(1)}, u32[]{:S(2)}, u32[]{:S(2)}) collective-permute-start(bf16[8,128,128]{2,1,0:T(8,128)(2,1)S(1)} %get-tuple-element.58), channel_id=1, source_target_pairs={{0,12},{4,16},{8,20},{12,24},{16,28},{20,0},{24,4},{28,8},{1,13},{... | collective-permute-start | bytes 786440 | tf_op jit(solution)/shard_map/ppermute | solution.py:533
  34.3 31.4 %collective-permute-start.6 = (bf16[8,128,128]{2,1,0:T(8,128)(2,1)S(1)}, bf16[8,128,128]{2,1,0:T(8,128)(2,1)S(1)}, u32[]{:S(2)}, u32[]{:S(2)}) collective-permute-start(bf16[8,128,128]{2,1,0:T(8,128)(2,1)S(1)} %get-tuple-element.59), channel_id=1, source_target_pairs={{0,16},{4,20},{8,24},{12,28},{16,0},{20,4},{24,8},{28,12},{1,17},{... | collective-permute-start | bytes 786440 | tf_op jit(solution)/shard_map/ppermute | solution.py:533
  36.7 45.9 %collective-permute-start.7 = (bf16[8,128,128]{2,1,0:T(8,128)(2,1)S(1)}, bf16[8,128,128]{2,1,0:T(8,128)(2,1)S(1)}, u32[]{:S(2)}, u32[]{:S(2)}) collective-permute-start(bf16[8,128,128]{2,1,0:T(8,128)(2,1)S(1)} %get-tuple-element.60), channel_id=1, source_target_pairs={{0,20},{4,24},{8,28},{12,0},{16,4},{20,8},{24,12},{28,16},{1,21},{... | collective-permute-start | bytes 786440 | tf_op jit(solution)/shard_map/ppermute | solution.py:533
  56.6 26.0 %collective-permute-start.8 = (bf16[8,128,128]{2,1,0:T(8,128)(2,1)S(1)}, bf16[8,128,128]{2,1,0:T(8,128)(2,1)S(1)}, u32[]{:S(2)}, u32[]{:S(2)}) collective-permute-start(bf16[8,128,128]{2,1,0:T(8,128)(2,1)S(1)} %get-tuple-element.61), channel_id=1, source_target_pairs={{0,24},{4,28},{8,0},{12,4},{16,8},{20,12},{24,16},{28,20},{1,25},{... | collective-permute-start | bytes 786440 | tf_op jit(solution)/shard_map/ppermute | solution.py:533
  65.7 16.9 %copy-start.11 = (bf16[8,128,128]{2,1,0:T(8,128)(2,1)S(1)}, bf16[8,128,128]{2,1,0:T(8,128)(2,1)}, u32[]{:S(2)}) copy-start(bf16[8,128,128]{2,1,0:T(8,128)(2,1)} %constant.35.clone.refs_9_) | copy-start | bytes 786436
  65.7 16.9 %copy-start.12 = (bf16[8,64,256]{2,1,0:T(8,128)(2,1)S(1)}, bf16[8,64,256]{2,1,0:T(8,128)(2,1)}, u32[]{:S(2)}) copy-start(bf16[8,64,256]{2,1,0:T(8,128)(2,1)} %constant.36.clone.refs_10_) | copy-start | bytes 786436
  65.7 16.9 %copy-start.14 = (bf16[256,256]{1,0:T(8,128)(2,1)S(1)}, bf16[256,256]{1,0:T(8,128)(2,1)}, u32[]{:S(2)}) copy-start(bf16[256,256]{1,0:T(8,128)(2,1)} %constant.37.clone.refs_13_) | copy-start | bytes 393220
  65.7 16.9 %collective-permute-start.9 = (bf16[8,128,128]{2,1,0:T(8,128)(2,1)S(1)}, bf16[8,128,128]{2,1,0:T(8,128)(2,1)S(1)}, u32[]{:S(2)}, u32[]{:S(2)}) collective-permute-start(bf16[8,128,128]{2,1,0:T(8,128)(2,1)S(1)} %get-tuple-element.62), channel_id=1, source_target_pairs={{0,28},{4,0},{8,4},{12,8},{16,12},{20,16},{24,20},{28,24},{1,29},{... | collective-permute-start | bytes 786440 | tf_op jit(solution)/shard_map/ppermute | solution.py:533
  82.6 44.5 %copy-start.5 = (bf16[1024,1024]{1,0:T(8,128)(2,1)S(1)}, bf16[1024,1024]{1,0:T(8,128)(2,1)}, u32[]{:S(2)}) copy-start(bf16[1024,1024]{1,0:T(8,128)(2,1)} %query_ref.1) | copy-start | bytes 6291460
  97.6 64.1 %collective-permute-start.19 = (bf16[1024,1024]{1,0:T(8,128)(2,1)S(1)}, bf16[1024,1024]{1,0:T(8,128)(2,1)S(1)}, u32[]{:S(2)}, u32[]{:S(2)}) collective-permute-start(bf16[1024,1024]{1,0:T(8,128)(2,1)S(1)} %collective-permute-done.1.refs_6_), channel_id=1, source_target_pairs={{0,4},{4,0},{8,12},{12,8},{16,20},{20,16},{24,28},{28,24},{1,5},{5... | collective-permute-start | bytes 6291464 | tf_op jit(solution)/shard_map/ppermute | solution.py:542
  97.6 64.0 %collective-permute-start.20 = (bf16[1024,1024]{1,0:T(8,128)(2,1)S(1)}, bf16[1024,1024]{1,0:T(8,128)(2,1)S(1)}, u32[]{:S(2)}, u32[]{:S(2)}) collective-permute-start(bf16[1024,1024]{1,0:T(8,128)(2,1)S(1)} %collective-permute-done.2.refs_8_), channel_id=1, source_target_pairs={{0,4},{4,0},{8,12},{12,8},{16,20},{20,16},{24,28},{28,24},{1,5},{5... | collective-permute-start | bytes 6291464 | tf_op jit(solution)/shard_map/ppermute | solution.py:542
  98.1 7.0 %collective-permute-start.23 = (bf16[4,128,128]{2,1,0:T(8,128)(2,1)S(1)}, bf16[4,128,128]{2,1,0:T(8,128)(2,1)S(1)}, u32[]{:S(2)}, u32[]{:S(2)}) collective-permute-start(bf16[4,128,128]{2,1,0:T(8,128)(2,1)S(1)} %get-tuple-element.84), channel_id=1, source_target_pairs={{0,4},{4,8},{8,12},{12,16},{16,20},{20,24},{24,28},{28,0},{1,5},{5... | collective-permute-start | bytes 393224 | tf_op jit(solution)/shard_map/ppermute | solution.py:533
  98.2 8.3 %collective-permute-start.24 = (bf16[4,128,128]{2,1,0:T(8,128)(2,1)S(1)}, bf16[4,128,128]{2,1,0:T(8,128)(2,1)S(1)}, u32[]{:S(2)}, u32[]{:S(2)}) collective-permute-start(bf16[4,128,128]{2,1,0:T(8,128)(2,1)S(1)} %get-tuple-element.85), channel_id=1, source_target_pairs={{0,8},{4,12},{8,16},{12,20},{16,24},{20,28},{24,0},{28,4},{1,9},{5... | collective-permute-start | bytes 393224 | tf_op jit(solution)/shard_map/ppermute | solution.py:533
  98.2 18.6 %collective-permute-start.25 = (bf16[4,128,128]{2,1,0:T(8,128)(2,1)S(1)}, bf16[4,128,128]{2,1,0:T(8,128)(2,1)S(1)}, u32[]{:S(2)}, u32[]{:S(2)}) collective-permute-start(bf16[4,128,128]{2,1,0:T(8,128)(2,1)S(1)} %get-tuple-element.86), channel_id=1, source_target_pairs={{0,12},{4,16},{8,20},{12,24},{16,28},{20,0},{24,4},{28,8},{1,13},{... | collective-permute-start | bytes 393224 | tf_op jit(solution)/shard_map/ppermute | solution.py:533
  105.2 11.9 %collective-permute-start.26 = (bf16[4,128,128]{2,1,0:T(8,128)(2,1)S(1)}, bf16[4,128,128]{2,1,0:T(8,128)(2,1)S(1)}, u32[]{:S(2)}, u32[]{:S(2)}) collective-permute-start(bf16[4,128,128]{2,1,0:T(8,128)(2,1)S(1)} %get-tuple-element.87), channel_id=1, source_target_pairs={{0,16},{4,20},{8,24},{12,28},{16,0},{20,4},{24,8},{28,12},{1,17},{... | collective-permute-start | bytes 393224 | tf_op jit(solution)/shard_map/ppermute | solution.py:533
  106.5 12.8 %collective-permute-start.27 = (bf16[4,128,128]{2,1,0:T(8,128)(2,1)S(1)}, bf16[4,128,128]{2,1,0:T(8,128)(2,1)S(1)}, u32[]{:S(2)}, u32[]{:S(2)}) collective-permute-start(bf16[4,128,128]{2,1,0:T(8,128)(2,1)S(1)} %get-tuple-element.88), channel_id=1, source_target_pairs={{0,20},{4,24},{8,28},{12,0},{16,4},{20,8},{24,12},{28,16},{1,21},{... | collective-permute-start | bytes 393224 | tf_op jit(solution)/shard_map/ppermute | solution.py:533
  116.9 5.0 %collective-permute-start.28 = (bf16[4,128,128]{2,1,0:T(8,128)(2,1)S(1)}, bf16[4,128,128]{2,1,0:T(8,128)(2,1)S(1)}, u32[]{:S(2)}, u32[]{:S(2)}) collective-permute-start(bf16[4,128,128]{2,1,0:T(8,128)(2,1)S(1)} %get-tuple-element.89), channel_id=1, source_target_pairs={{0,24},{4,28},{8,0},{12,4},{16,8},{20,12},{24,16},{28,20},{1,25},{... | collective-permute-start | bytes 393224 | tf_op jit(solution)/shard_map/ppermute | solution.py:533
  117.1 6.2 %collective-permute-start.29 = (bf16[4,128,128]{2,1,0:T(8,128)(2,1)S(1)}, bf16[4,128,128]{2,1,0:T(8,128)(2,1)S(1)}, u32[]{:S(2)}, u32[]{:S(2)}) collective-permute-start(bf16[4,128,128]{2,1,0:T(8,128)(2,1)S(1)} %get-tuple-element.90), channel_id=1, source_target_pairs={{0,28},{4,0},{8,4},{12,8},{16,12},{20,16},{24,20},{28,24},{1,29},{... | collective-permute-start | bytes 393224 | tf_op jit(solution)/shard_map/ppermute | solution.py:533
  119.3 12.6 %collective-permute-start.10 = (bf16[4,128,128]{2,1,0:T(8,128)(2,1)S(1)}, bf16[4,128,128]{2,1,0:T(8,128)(2,1)S(1)}, u32[]{:S(2)}, u32[]{:S(2)}) collective-permute-start(bf16[4,128,128]{2,1,0:T(8,128)(2,1)S(1)} %get-tuple-element.65), channel_id=1, source_target_pairs={{0,4},{4,8},{8,12},{12,16},{16,20},{20,24},{24,28},{28,0},{1,5},{5... | collective-permute-start | bytes 393224 | tf_op jit(solution)/shard_map/ppermute | solution.py:533
  121.8 10.7 %collective-permute-start.11 = (bf16[4,128,128]{2,1,0:T(8,128)(2,1)S(1)}, bf16[4,128,128]{2,1,0:T(8,128)(2,1)S(1)}, u32[]{:S(2)}, u32[]{:S(2)}) collective-permute-start(bf16[4,128,128]{2,1,0:T(8,128)(2,1)S(1)} %get-tuple-element.66), channel_id=1, source_target_pairs={{0,8},{4,12},{8,16},{12,20},{16,24},{20,28},{24,0},{28,4},{1,9},{5... | collective-permute-start | bytes 393224 | tf_op jit(solution)/shard_map/ppermute | solution.py:533
  123.3 11.0 %collective-permute-start.12 = (bf16[4,128,128]{2,1,0:T(8,128)(2,1)S(1)}, bf16[4,128,128]{2,1,0:T(8,128)(2,1)S(1)}, u32[]{:S(2)}, u32[]{:S(2)}) collective-permute-start(bf16[4,128,128]{2,1,0:T(8,128)(2,1)S(1)} %get-tuple-element.67), channel_id=1, source_target_pairs={{0,12},{4,16},{8,20},{12,24},{16,28},{20,0},{24,4},{28,8},{1,13},{... | collective-permute-start | bytes 393224 | tf_op jit(solution)/shard_map/ppermute | solution.py:533
  127.1 30.3 %slice-start = ((s8[8388608]{0:T(1024)(128)(4,1)}), s8[4194304]{0:T(1024)(128)(4,1)S(1)}, s32[]{:S(2)}) async-start(s8[8388608]{0:T(1024)(128)(4,1)} %bitcast.4), calls=%async_computation | async-start | bytes 8388608
  130.7 26.7 %slice-start.1 = ((s8[8388608]{0:T(1024)(128)(4,1)}), s8[4194304]{0:T(1024)(128)(4,1)S(1)}, s32[]{:S(2)}) async-start(s8[8388608]{0:T(1024)(128)(4,1)} %bitcast.4), calls=%async_computation.1 | async-start | bytes 8388608
  131.9 25.5 %collective-permute-start.30 = (bf16[1024,256]{1,0:T(8,128)(2,1)S(1)}, bf16[1024,256]{1,0:T(8,128)(2,1)S(1)}, u32[]{:S(2)}, u32[]{:S(2)}) collective-permute-start(bf16[1024,256]{1,0:T(8,128)(2,1)S(1)} %get-tuple-element.91.refs_0_), channel_id=1, source_target_pairs={{0,1},{1,0},{2,3},{3,2},{4,5},{5,4},{6,7},{7,6},{8,9},{9,8},{10,11... | collective-permute-start | bytes 1572872 | tf_op jit(solution)/shard_map/ppermute | solution.py:542
  132.5 10.2 %collective-permute-start.13 = (bf16[4,128,128]{2,1,0:T(8,128)(2,1)S(1)}, bf16[4,128,128]{2,1,0:T(8,128)(2,1)S(1)}, u32[]{:S(2)}, u32[]{:S(2)}) collective-permute-start(bf16[4,128,128]{2,1,0:T(8,128)(2,1)S(1)} %get-tuple-element.68), channel_id=1, source_target_pairs={{0,16},{4,20},{8,24},{12,28},{16,0},{20,4},{24,8},{28,12},{1,17},{... | collective-permute-start | bytes 393224 | tf_op jit(solution)/shard_map/ppermute | solution.py:533
  134.2 9.0 %collective-permute-start.14 = (bf16[4,128,128]{2,1,0:T(8,128)(2,1)S(1)}, bf16[4,128,128]{2,1,0:T(8,128)(2,1)S(1)}, u32[]{:S(2)}, u32[]{:S(2)}) collective-permute-start(bf16[4,128,128]{2,1,0:T(8,128)(2,1)S(1)} %get-tuple-element.69), channel_id=1, source_target_pairs={{0,20},{4,24},{8,28},{12,0},{16,4},{20,8},{24,12},{28,16},{1,21},{... | collective-permute-start | bytes 393224 | tf_op jit(solution)/shard_map/ppermute | solution.py:533
  142.7 18.9 %collective-permute-start.31 = (bf16[1024,256]{1,0:T(8,128)(2,1)S(1)}, bf16[1024,256]{1,0:T(8,128)(2,1)S(1)}, u32[]{:S(2)}, u32[]{:S(2)}) collective-permute-start(bf16[1024,256]{1,0:T(8,128)(2,1)S(1)} %get-tuple-element.92.refs_1_), channel_id=1, source_target_pairs={{0,2},{1,3},{2,0},{3,1},{4,6},{5,7},{6,4},{7,5},{8,10},{9,11},{10,... | collective-permute-start | bytes 1572872 | tf_op jit(solution)/shard_map/ppermute | solution.py:542
  143.2 6.6 %collective-permute-start.15 = (bf16[4,128,128]{2,1,0:T(8,128)(2,1)S(1)}, bf16[4,128,128]{2,1,0:T(8,128)(2,1)S(1)}, u32[]{:S(2)}, u32[]{:S(2)}) collective-permute-start(bf16[4,128,128]{2,1,0:T(8,128)(2,1)S(1)} %get-tuple-element.70), channel_id=1, source_target_pairs={{0,24},{4,28},{8,0},{12,4},{16,8},{20,12},{24,16},{28,20},{1,25},{... | collective-permute-start | bytes 393224 | tf_op jit(solution)/shard_map/ppermute | solution.py:533
  149.8 5.1 %collective-permute-start.16 = (bf16[4,128,128]{2,1,0:T(8,128)(2,1)S(1)}, bf16[4,128,128]{2,1,0:T(8,128)(2,1)S(1)}, u32[]{:S(2)}, u32[]{:S(2)}) collective-permute-start(bf16[4,128,128]{2,1,0:T(8,128)(2,1)S(1)} %get-tuple-element.71), channel_id=1, source_target_pairs={{0,28},{4,0},{8,4},{12,8},{16,12},{20,16},{24,20},{28,24},{1,29},{... | collective-permute-start | bytes 393224 | tf_op jit(solution)/shard_map/ppermute | solution.py:533
  156.0 14.6 %collective-permute-start.17 = (bf16[1024,256]{1,0:T(8,128)(2,1)S(1)}, bf16[1024,256]{1,0:T(8,128)(2,1)S(1)}, u32[]{:S(2)}, u32[]{:S(2)}) collective-permute-start(bf16[1024,256]{1,0:T(8,128)(2,1)S(1)} %get-tuple-element.72.refs_0_), channel_id=1, source_target_pairs={{0,1},{1,0},{2,3},{3,2},{4,5},{5,4},{6,7},{7,6},{8,9},{9,8},{10,11... | collective-permute-start | bytes 1572872 | tf_op jit(solution)/shard_map/ppermute | solution.py:542
  157.4 14.8 %collective-permute-start.18 = (bf16[1024,256]{1,0:T(8,128)(2,1)S(1)}, bf16[1024,256]{1,0:T(8,128)(2,1)S(1)}, u32[]{:S(2)}, u32[]{:S(2)}) collective-permute-start(bf16[1024,256]{1,0:T(8,128)(2,1)S(1)} %get-tuple-element.73.refs_1_), channel_id=1, source_target_pairs={{0,2},{1,3},{2,0},{3,1},{4,6},{5,7},{6,4},{7,5},{8,10},{9,11},{10,... | collective-permute-start | bytes 1572872 | tf_op jit(solution)/shard_map/ppermute | solution.py:542
  165.4 18.0 %collective-permute-start.32 = (bf16[1024,256]{1,0:T(8,128)(2,1)S(1)}, bf16[1024,256]{1,0:T(8,128)(2,1)S(1)}, u32[]{:S(2)}, u32[]{:S(2)}) collective-permute-start(bf16[1024,256]{1,0:T(8,128)(2,1)S(1)} %get-tuple-element.94), channel_id=1, source_target_pairs={{0,2},{1,3},{2,0},{3,1},{4,6},{5,7},{6,4},{7,5},{8,10},{9,11},{10,... | collective-permute-start | bytes 1572872 | tf_op jit(solution)/shard_map/ppermute | solution.py:542
  167.5 16.0 %collective-permute-start.33 = (bf16[1024,256]{1,0:T(8,128)(2,1)S(1)}, bf16[1024,256]{1,0:T(8,128)(2,1)S(1)}, u32[]{:S(2)}, u32[]{:S(2)}) collective-permute-start(bf16[1024,256]{1,0:T(8,128)(2,1)S(1)} %get-tuple-element.96), channel_id=1, source_target_pairs={{0,1},{1,0},{2,3},{3,2},{4,5},{5,4},{6,7},{7,6},{8,9},{9,8},{10,11... | collective-permute-start | bytes 1572872 | tf_op jit(solution)/shard_map/ppermute | solution.py:542
  175.9 17.8 %collective-permute-start.21 = (bf16[1024,256]{1,0:T(8,128)(2,1)S(1)}, bf16[1024,256]{1,0:T(8,128)(2,1)S(1)}, u32[]{:S(2)}, u32[]{:S(2)}) collective-permute-start(bf16[1024,256]{1,0:T(8,128)(2,1)S(1)} %get-tuple-element.80), channel_id=1, source_target_pairs={{0,2},{1,3},{2,0},{3,1},{4,6},{5,7},{6,4},{7,5},{8,10},{9,11},{10,... | collective-permute-start | bytes 1572872 | tf_op jit(solution)/shard_map/ppermute | solution.py:542
  176.0 17.8 %collective-permute-start.22 = (bf16[1024,256]{1,0:T(8,128)(2,1)S(1)}, bf16[1024,256]{1,0:T(8,128)(2,1)S(1)}, u32[]{:S(2)}, u32[]{:S(2)}) collective-permute-start(bf16[1024,256]{1,0:T(8,128)(2,1)S(1)} %get-tuple-element.82), channel_id=1, source_target_pairs={{0,1},{1,0},{2,3},{3,2},{4,5},{5,4},{6,7},{7,6},{8,9},{9,8},{10,11... | collective-permute-start | bytes 1572872 | tf_op jit(solution)/shard_map/ppermute | solution.py:542
  187.1 6.6 %collective-permute-start.34 = (bf16[1024,128]{1,0:T(8,128)(2,1)S(1)}, bf16[1024,128]{1,0:T(8,128)(2,1)S(1)}, u32[]{:S(2)}, u32[]{:S(2)}) collective-permute-start(bf16[1024,128]{1,0:T(8,128)(2,1)S(1)} %get-tuple-element.97), channel_id=1, source_target_pairs={{0,4},{4,8},{8,12},{12,16},{16,20},{20,24},{24,28},{1,5},{5,9},{9,... | collective-permute-start | bytes 786440 | tf_op jit(solution)/shard_map/ppermute | solution.py:538
  (7 other events, 38.0 us)
where the time goes:
time: 201 us; the launch traced here: 200 us
  Pallas kernels  69.4 us (35%)
  starting transfers between devices  60.6 us (30%)
  waiting for transfers between devices  59.9 us (30%)
  local copies, waits for them, and re-layouts  9.16 us (5%)
    ppermute x21, waiting for transfers between devices, ring(): lax.ppermute(block, axis, [(i, (i + distance) % count) for i in range(cou...  50.6 us
    ppermute x21, starting transfers between devices, ring(): lax.ppermute(block, axis, [(i, (i + distance) % count) for i in range(cou...  46.3 us
    pallas_call x1, Pallas kernels, long_conv(): pl.pallas_call(functools.partial(conv_kernel, groups), out_shape=[jax.Sha...  14.9 us
    pallas_call x4, Pallas kernels, project(): pl.pallas_call(functools.partial(project_kernel, slot), out_shape=[jax.Sh...  14.7 us
    ppermute x12, starting transfers between devices, swapped(): lax.ppermute(block, axis, [(i, i ^ bit) for i in range(lax.axis_size(axis...  10.6 us
    pallas_call x2, Pallas kernels, medium_call(): pl.pallas_call(functools.partial(kernel, counts), out_shape=[jax.ShapeDty...  10.3 us
    pallas_call x1, Pallas kernels, spectra(): pl.pallas_call(filter_kernel, out_shape=jax.ShapeDtypeStruct((channels, n...  8.89 us
    ppermute x12, waiting for transfers between devices, swapped(): lax.ppermute(block, axis, [(i, i ^ bit) for i in range(lax.axis_size(axis...  8.64 us
  transfers between devices with their start and end apart: 35, of which 15 were waited for; matrix products, arithmetic and copies ran while one was open for 0% of the time, Pallas kernels for 28%

commit v1 on v0

--- a/solution.py
+++ b/solution.py
@@ -41,8 +41,9 @@
     per = n1 // groups
     fore, rear = [], []
     for me in range(groups):
-        ids = np.concatenate([((me - s) % groups) * per + np.arange(per) for s in range(groups)])
-        out = np.concatenate([((me + s) % groups) * per + np.arange(per) for s in range(groups)])
+        ids, out = (me - np.arange(groups)) % groups, (me + np.arange(groups)) % groups
+        ids = (ids[:, None] * per + np.arange(per)).reshape(-1)
+        out = (out[:, None] * per + np.arange(per)).reshape(-1)
         high, low = split_table(outer[:, ids])
         fore.append(np.concatenate([high, low], axis=1))
         high, low = split_table(back[out])
@@ -93,6 +94,7 @@
     keys = short_conv(key_ref[...].astype(F32), aux[:, 11:13], aux[:, 3:6])
     values = short_conv(value_ref[...].astype(F32), aux[:, 13:15], aux[:, 6:9])
     mixed = (keys * values).astype(BF16)
+
     for at, out_ref in enumerate(out_refs):
 
         @pl.when(pl.program_id(0) == at)
@@ -101,25 +103,26 @@
                 out_ref[j] = mixed[:, j * LANES : (j + 1) * LANES]
 
 
-def mix(ids, key_proj, value_proj, aux, first, count, groups):
+def mix(ids, key_proj, value_proj, aux, groups, chunk, chunks):
     channels, tokens = key_proj.shape
-    rows = channels // groups
-    where = lambda i, ids: (lax.rem(ids[0] + first + i, groups), 0)
-    piece = (tokens // LANES, rows, LANES)
+    rows = channels // groups // chunks
+    count = tokens // LANES
+
+    where = lambda g, ids: (lax.rem(ids[0] + g, groups) * chunks + chunk, 0)
     return pl.pallas_call(
         mix_kernel,
-        out_shape=[jax.ShapeDtypeStruct(piece, BF16)] * count,
+        out_shape=[jax.ShapeDtypeStruct((count, rows, LANES), BF16)] * groups,
         grid_spec=pltpu.PrefetchScalarGridSpec(
             num_scalar_prefetch=1,
-            grid=(count,),
+            grid=(groups,),
             in_specs=[
                 pl.BlockSpec((rows, tokens), where),
                 pl.BlockSpec((rows, tokens), where),
                 pl.BlockSpec((rows, aux.shape[1]), where),
             ],
-            out_specs=[whole(piece)] * count,
+            out_specs=[whole((count, rows, LANES))] * groups,
         ),
-        compiler_params=grant(12),
+        compiler_params=grant(6),
         name="mix",
     )(ids, key_proj, value_proj, aux)
 
@@ -185,21 +188,22 @@
         + [whole(tables[name].shape) for name in names],
         out_specs=pl.BlockSpec((block, n1, 2 * LANES), lambda i: (i, 0, 0)),
         scratch_shapes=[pltpu.VMEM((n1 * block, LANES), F32)],
-        compiler_params=grant(20),
+        compiler_params=grant(9),
         name="spectra",
     )(long_filter, *[tables[name] for name in names])
 
 
-def conv_kernel(groups, ids_ref, *refs):
-    pieces = refs[:groups]
-    spec_ref, fore_ref, rear_ref, twist_ref, inner_ref, back_ref = refs[groups : groups + 6]
-    outs = refs[groups + 6 : 3 * groups + 6]
-    rows_ref, done_ref = refs[3 * groups + 6 :]
+def conv_kernel(count, ids_ref, *refs):
+    pieces = refs[:count]
+    spec_ref, fore_ref, rear_ref, twist_ref, inner_ref, back_ref = refs[count : count + 6]
+    outs, (rows_ref, done_ref) = refs[count + 6 : -2], refs[-2:]
     per, block, _ = pieces[0].shape
-    n1 = groups * per
-    for s in range(groups):
-        part = pieces[s][...].astype(F32)
-        rows_ref[s * per * block : (s + 1) * per * block, :] = part.reshape(per * block, LANES)
+    at = 0
+    for piece_ref in pieces:
+        size = per * block
+        rows_ref[at : at + size, :] = piece_ref[...].astype(F32).reshape(size, LANES)
+        at += size
+    n1 = at // block
     group = math.gcd(block, 8)
 
     def body(at, carry):
@@ -243,49 +247,37 @@
         return carry
 
     lax.fori_loop(0, block // group, body, 0)
-    half = per // 2 * block
-    for s in range(2 * groups):
-        part = done_ref[s * half : (s + 1) * half, :]
-        outs[s][...] = part.reshape(per // 2, block, LANES).astype(BF16)
-
-
-def long_conv(ids, pieces, spec, tables, block):
+    at = 0
+    for out_ref in outs:
+        size = math.prod(out_ref.shape[:-1])
+        out_ref[...] = done_ref[at : at + size, :].reshape(out_ref.shape).astype(BF16)
+        at += size
+
+
+def long_conv(ids, pieces, spec, tables, block, tiles, first):
     groups = len(pieces)
     per, channels, _ = pieces[0].shape
     n1 = groups * per
-    piece = pl.BlockSpec((per, block, LANES), lambda i, ids: (0, i, 0))
-    part = pl.BlockSpec((per // 2, block, LANES), lambda i, ids: (0, i, 0))
+    runs = list(tiles) * groups
+    tile = lambda n: pl.BlockSpec((n, block, LANES), lambda i, ids: (0, i, 0))
     mine = lambda shape: pl.BlockSpec((1,) + shape[1:], lambda i, ids: (ids[0], 0, 0))
+    names = ("fore", "rear", "twist", "inner", "inner_back")
     return pl.pallas_call(
         functools.partial(conv_kernel, groups),
-        out_shape=[jax.ShapeDtypeStruct((per // 2, channels, LANES), BF16)] * (2 * groups),
+        out_shape=[jax.ShapeDtypeStruct((n, channels, LANES), BF16) for n in runs],
         grid_spec=pltpu.PrefetchScalarGridSpec(
             num_scalar_prefetch=1,
             grid=(channels // block,),
-            in_specs=[piece] * groups
-            + [
-                pl.BlockSpec((block, n1, 2 * LANES), lambda i, ids: (i, 0, 0)),
-                mine(tables["fore"].shape),
-                mine(tables["rear"].shape),
-                whole(tables["twist"].shape),
-                whole(tables["inner"].shape),
-                whole(tables["inner_back"].shape),
-            ],
-            out_specs=[part] * (2 * groups),
+            in_specs=[tile(per)] * groups
+            + [pl.BlockSpec((block, n1, 2 * LANES), lambda i, ids: (i + first // block, 0, 0))]
+            + [mine(tables[name].shape) for name in names[:2]]
+            + [whole(tables[name].shape) for name in names[2:]],
+            out_specs=[tile(n) for n in runs],
             scratch_shapes=[pltpu.VMEM((n1 * block, LANES), F32)] * 2,
         ),
-        compiler_params=grant(24),
+        compiler_params=grant(14),
         name="conv",
-    )(
-        ids,
-        *pieces,
-        spec,
-        tables["fore"],
-        tables["rear"],
-        tables["twist"],
-        tables["inner"],
-        tables["inner_back"],
-    )
+    )(ids, *pieces, spec, *[tables[name] for name in names])
 
 
 def query_kernel(query_ref, aux_ref, out_ref):
@@ -308,59 +300,66 @@
             pl.BlockSpec((block, aux.shape[1]), lambda i: (i, 0)),
         ],
         out_specs=pl.BlockSpec((count, block, LANES), lambda i: (0, i, 0)),
-        compiler_params=grant(12),
+        compiler_params=grant(4),
         name="query",
     )(query_proj, aux)
 
 
-def gate_kernel(groups, ids_ref, *refs):
-    pieces = refs[:groups]
-    query_ref, left_ref, right_ref = refs[groups:]
+def gate_kernel(chunk, chunks, tiles, ids_ref, *refs):
+    pieces, (query_ref, left_ref, right_ref) = refs[:-3], refs[-3:]
+    groups = len(pieces)
     rows = pieces[0].shape[1]
-    half = pl.num_programs(0) // 2
     for side, out_ref in enumerate((left_ref, right_ref)):
 
-        @pl.when(pl.program_id(0) // half == side)
+        @pl.when(lax.rem(pl.program_id(0), tiles) // (tiles // 2) == side)
         def _():
-            for s in range(groups):
+            for s, piece_ref in enumerate(pieces):
                 group = lax.rem(ids_ref[0] + groups - s, groups)
-                at = pl.ds(pl.multiple_of(group * rows, rows), rows)
-                out_ref[at, :] = (query_ref[0, at, :] * pieces[s][0].astype(F32)).astype(BF16)
-
-
-def gate(ids, pieces, query, start):
+                at = pl.ds(pl.multiple_of((group * chunks + chunk) * rows, rows), rows)
+                to = pl.ds(pl.multiple_of(group * rows, rows), rows)
+                conv = piece_ref[0].astype(F32)
+                out_ref[to, :] = (query_ref[0, at, :] * conv).astype(BF16)
+
+
+def gate(ids, pieces, query, chunk, chunks, start, tiles):
     groups = len(pieces)
     per, rows, _ = pieces[0].shape
     channels = query.shape[1]
-    half = per // 2
-    shape = jax.ShapeDtypeStruct((channels, half * LANES), BF16)
-    return pl.pallas_call(
-        functools.partial(gate_kernel, groups),
-        out_shape=[shape] * 2,
+    half = tiles // 2
+    shape = (groups * rows, per // 2 * LANES)
+    block = (groups * rows, LANES)
+    left = lambda j, ids: (0, j // tiles * half + jnp.minimum(lax.rem(j, tiles), half - 1))
+    right = lambda j, ids: (0, j // tiles * half + jnp.maximum(lax.rem(j, tiles) - half, 0))
+    return pl.pallas_call(
+        functools.partial(gate_kernel, chunk, chunks, tiles),
+        out_shape=[jax.ShapeDtypeStruct(shape, BF16)] * 2,
         grid_spec=pltpu.PrefetchScalarGridSpec(
             num_scalar_prefetch=1,
             grid=(per,),
             in_specs=[pl.BlockSpec((1, rows, LANES), lambda j, ids: (j, 0, 0))] * groups
             + [pl.BlockSpec((1, channels, LANES), lambda j, ids: (start + j, 0, 0))],
-            out_specs=[
-                pl.BlockSpec((channels, LANES), lambda j, ids: (0, jnp.minimum(j, half - 1))),
-                pl.BlockSpec((channels, LANES), lambda j, ids: (0, jnp.maximum(j - half, 0))),
-            ],
+            out_specs=[pl.BlockSpec(block, left), pl.BlockSpec(block, right)],
         ),
-        compiler_params=grant(12),
+        compiler_params=grant(5),
         name="gate",
     )(ids, *pieces, query)
 
 
-def turn_kernel(ids_ref, weight_ref, *out_refs):
+def turn_kernel(groups, chunks, ids_ref, weight_ref, *out_refs):
+    rows = weight_ref.shape[0] // groups // chunks
     for at, out_ref in enumerate(out_refs):
 
         @pl.when(pl.program_id(0) == at)
         def _():
-            out_ref[...] = weight_ref[...].T
-
-
-def turned(ids, out_weight, width, shards_of):
+            parts = [
+                weight_ref[(g * chunks + c) * rows : (g * chunks + c + 1) * rows, :]
+                for c in range(chunks)
+                for g in range(groups)
+            ]
+            out_ref[...] = jnp.concatenate(parts, axis=0).T
+
+
+def turned(ids, out_weight, width, shards_of, groups, chunks):
     channels = out_weight.shape[0]
     step = min(width, 256)
     inner = width // step
@@ -379,7 +378,7 @@
         )
 
     return pl.pallas_call(
-        turn_kernel,
+        functools.partial(turn_kernel, groups, chunks),
         out_shape=[jax.ShapeDtypeStruct((width, channels), BF16)] * count,
         grid_spec=pltpu.PrefetchScalarGridSpec(
             num_scalar_prefetch=1,
@@ -387,31 +386,37 @@
             in_specs=[pl.BlockSpec((channels, step), from_at)],
             out_specs=[pl.BlockSpec((step, channels), out_at(at)) for at in range(count)],
         ),
-        compiler_params=grant(12),
+        compiler_params=grant(7),
         name="turn",
     )(ids, out_weight)
 
 
-def project_kernel(slot, ids_ref, *refs):
-    sources, weights = refs[0:4], refs[4:6]
-    sides = refs[6:8], refs[8:10]
-    outs = refs[10:12]
+def project_kernel(slot, chunks, ids_ref, *refs):
+    sources, refs = refs[: 4 * chunks], refs[4 * chunks :]
+    weights, sides, outs = refs[0:2], (refs[2:4], refs[4:6]), refs[6:8]
     for colour in range(2):
         for partner in range(2):
 
             @pl.when((pl.program_id(0) == colour) & (((ids_ref[0] & 1) ^ slot) == partner))
             def _():
-                out = dot(weights[colour][...], sources[colour][...]) + dot(
-                    sides[colour][partner][...], sources[2 + colour][...]
-                )
-                outs[colour][...] = out.astype(BF16)
-
-
-def project(ids, own, near, weights, sides, slot):
+                total = None
+                for near, table in enumerate((weights[colour], sides[colour][partner])):
+                    stack = [sources[(2 * c + near) * 2 + colour][...] for c in range(chunks)]
+                    term = dot(table[...], jnp.concatenate(stack, axis=0))
+                    total = term if total is None else total + term
+                outs[colour][...] = total.astype(BF16)
+
+
+def project(ids, sources, weights, sides, slot, h):
     width, channels = weights[0].shape
-    tokens = own[0].shape[1]
+    flat = [array for own, near in sources for array in (*own, *near)]
+    tokens = min(array.shape[1] for array in flat)
     step = min(width, 512)
     inner = width // step
+
+    def source(array):
+        at = h if array.shape[1] > tokens else 0
+        return pl.BlockSpec((array.shape[0], tokens), lambda *_: (0, at))
 
     def when(active, mine, colour, h):
         return (jnp.where(active, h, jnp.where(colour > mine, inner - 1, 0)), 0)
@@ -427,12 +432,12 @@
         return lambda colour, h, ids: when(colour == mine, mine, colour, h)
 
     return pl.pallas_call(
-        functools.partial(project_kernel, slot),
+        functools.partial(project_kernel, slot, len(sources)),
         out_shape=[jax.ShapeDtypeStruct((width, tokens), BF16)] * 2,
         grid_spec=pltpu.PrefetchScalarGridSpec(
             num_scalar_prefetch=1,
             grid=(2, inner),
-            in_specs=[whole((channels, tokens))] * 4
+            in_specs=[source(array) for array in flat]
             + [pl.BlockSpec((step, channels), colour_at(colour)) for colour in range(2)]
             + [
                 pl.BlockSpec((step, channels), side_at(colour, partner))
@@ -441,9 +446,9 @@
             ],
             out_specs=[pl.BlockSpec((step, tokens), colour_at(colour)) for colour in range(2)],
         ),
-        compiler_params=grant(20),
+        compiler_params=grant(18),
         name="project",
-    )(ids, *own, *near, *weights, *sides[0], *sides[1])
+    )(ids, *flat, *weights, *sides[0], *sides[1])
 
 
 def medium_spectrum(taps, fore_ref, low_ref):
@@ -524,12 +529,14 @@
         + [pl.BlockSpec((width, block), lambda i: (0, i))]
         + [whole(t.shape) for t in tables],
         out_specs=[row(n) for n in widths],
-        compiler_params=grant(16),
+        compiler_params=grant(10),
     )(*arrays, taps, *tables)
 
 
 def ring(block, axis, distance):
     count = lax.axis_size(axis)
+    if distance == 0:
+        return block
     return lax.ppermute(block, axis, [(i, (i + distance) % count) for i in range(count)])
 
 
@@ -542,12 +549,14 @@
     return lax.ppermute(block, axis, [(i, i ^ bit) for i in range(lax.axis_size(axis))])
 
 
-def neighbour_weights(ids, out_weight, width):
+def neighbour_weights(ids, out_weight, width, groups, chunks):
     slabs = turned(
         ids,
         out_weight,
         width,
         (lambda ids: ids[1] ^ 1 ^ ((ids[0] & 1) * 2), lambda ids: ids[1] ^ 2 ^ (ids[0] & 1)),
+        groups,
+        chunks,
     )
     return [swapped(slabs[0], "tp", 1), swapped(slabs[1], "tp", 2)]
 
@@ -560,18 +569,8 @@
     return out, held[2]
 
 
-def operator_parts(ids, gated, out_weight, weights, sides):
-    if sides is None:
-        source = jnp.concatenate(gated, axis=1)
-        partial = lax.dot_general(
-            out_weight, source, (((0,), (0,)), ((), ())), preferred_element_type=F32
-        ).astype(BF16)
-        return [[lax.psum_scatter(partial, "tp", scatter_dimension=0, tiled=True)]]
-    near = [swapped(gated[0], "tp", 1), swapped(gated[1], "tp", 2)]
-    send = project(ids, gated, near, (weights[2], weights[1]), sides, 1)
-    got = [swapped(send[0], "tp", 2), swapped(send[1], "tp", 1)]
-    keep = project(ids, gated, near, (weights[0], weights[0]), sides, 0)
-    return [[keep[0], got[0]], [keep[1], got[1]]]
+def neighbours(gated):
+    return [swapped(gated[0], "tp", 1), swapped(gated[1], "tp", 2)]
 
 
 def shards(query_proj, key_proj, value_proj, short_taps, long_filter, out_weight, medium_taps):
@@ -585,58 +584,76 @@
     flat_taps = short_taps.reshape(9, channels).T
     aux = jnp.concatenate([flat_taps, edges, jnp.zeros((channels, 1), F32)], axis=1)
     owned = long_filter.shape[0]
+    four = lax.axis_size("tp") == 4
+    chunks = 2 if four and owned % 32 == 0 else 1
+    rows = owned // chunks
     spec = spectra(long_filter, tables, min(owned, 16))
-    batch = groups // 2
-    far = mix(ids, key_proj, value_proj, aux, batch, batch, groups)
-    near = mix(ids, key_proj, value_proj, aux, 0, batch, groups)
-    sent = list(near) + list(far)
+    sent = []
+    for c in range(chunks):
+        sent.append(list(mix(ids, key_proj, value_proj, aux, groups, c, chunks)))
     sides, weights = None, None
-    if lax.axis_size("tp") == 4:
+    if four:
         part = out_weight.shape[1] // 4
-        held = lax.optimization_barrier((out_weight, near[0]))
-        sent[0] = held[1]
-        sides = neighbour_weights(ids, held[0], part)
+        held = lax.optimization_barrier((out_weight, sent[-1][0]))
+        sent[-1][0] = held[1]
+        sides = neighbour_weights(ids, held[0], part, groups, chunks)
         weights = turned(
             ids,
             held[0],
             part,
             (lambda ids: ids[1], lambda ids: ids[1] ^ 1, lambda ids: ids[1] ^ 2),
+            groups,
+            chunks,
         )
     query = query_conv(query_proj, aux)
-    pieces = [sent[0]]
-    for s in range(1, groups):
-        pieces.append(ring(sent[s], "ctx", s))
-    results = list(long_conv(ids, pieces, spec, tables, min(owned, 32)))
-    if sides is not None:
-        sides, results[0] = both_cores(sides, results[0])
+    count = tokens // LANES
+    half_tiles = count // 2
+    own = {0: [], 1: []}
+    near = {0: [], 1: []}
+    for c in range(chunks):
+        last = c == chunks - 1
+        got = [ring(piece, "ctx", s) for s, piece in enumerate(sent[c])]
+        runs = (half_tiles, half_tiles) if last else (count,)
+        results = list(long_conv(ids, got, spec, tables, min(rows, 32), runs, c * rows))
+        for h in (1, 0) if last else (None,):
+            back = [
+                ring(piece, "ctx", s)
+                for s, piece in enumerate(results[h::2] if last else results)
+            ]
+            start = h * half_tiles if last else 0
+            gated = list(gate(ids, back, query, c, chunks, start, half_tiles))
+            if four and c == 0 and h != 0:
+                sides, gated[0] = both_cores(sides, gated[0])
+            beside = neighbours(gated) if four else None
+            for at in (h,) if last else (0, 1):
+                own[at].append(gated)
+                near[at].append(beside)
+    parts = {}
+    for h in (1, 0):
+        if not four:
+            source = jnp.concatenate(own[h][0], axis=1)
+            partial = lax.dot_general(
+                out_weight, source, (((0,), (0,)), ((), ())), preferred_element_type=F32
+            ).astype(BF16)
+            parts[h] = [[lax.psum_scatter(partial, "tp", scatter_dimension=0, tiled=True)]]
+            continue
+        sources = list(zip(own[h], near[h]))
+        send = project(ids, sources, (weights[2], weights[1]), sides, 1, h)
+        got = [swapped(send[0], "tp", 2), swapped(send[1], "tp", 1)]
+        keep = project(ids, sources, (weights[0], weights[0]), sides, 0, h)
+        parts[h] = [[keep[0], got[0]], [keep[1], got[1]]]
     width = medium_taps.shape[0]
     half = tokens // 2
-    done = []
-    for h in (1, 0):
-        mine = results[h::2]
-        back = [mine[0]] + [ring(mine[s], "ctx", s) for s in range(1, groups)]
-        gated = gate(ids, back, query, h * half // LANES)
-        parts = operator_parts(ids, gated, out_weight, weights, sides)
-        if h == 1:
-            later, edge, tail = medium_call(
-                late_kernel,
-                parts,
-                (),
-                medium_taps,
-                medium_tables(width),
-                (half, width, half - width),
-            )
-            edge = forward(edge, "ctx")
-        else:
-            done = medium_call(
-                early_kernel,
-                parts,
-                (edge, later, tail),
-                medium_taps,
-                medium_tables(width),
-                (tokens, tokens),
-            )
-    return tuple(done)
+    tables = medium_tables(width)
+    later, edge, tail = medium_call(
+        late_kernel, parts[1], (), medium_taps, tables, (half, width, half - width)
+    )
+    edge = forward(edge, "ctx")
+    return tuple(
+        medium_call(
+            early_kernel, parts[0], (edge, later, tail), medium_taps, tables, (tokens, tokens)
+        )
+    )
 
 
 def solution(mesh):

time: 201 us -> 231 us (1.15)
  the two profiles are of different devices: /device:TPU:0 before, /device:TPU:15 now
where the time goes in v1:
time: 231 us; the launch traced here: 229 us
  waiting for transfers between devices  76.7 us (33%)
  Pallas kernels  72 us (31%)
  starting transfers between devices  70 us (30%)
  local copies, waits for them, and re-layouts  9.16 us (4%)
    ppermute x35, waiting for transfers between devices, ring(): lax.ppermute(block, axis, [(i, (i + distance) % count) for i in range(cou...  51 us
    ppermute x35, starting transfers between devices, ring(): lax.ppermute(block, axis, [(i, (i + distance) % count) for i in range(cou...  49.1 us
    ppermute x14, waiting for transfers between devices, swapped(): lax.ppermute(block, axis, [(i, i ^ bit) for i in range(lax.axis_size(axis...  25.1 us
    pallas_call x2, Pallas kernels, long_conv(): pl.pallas_call(functools.partial(conv_kernel, groups), out_shape=[jax.Sha...  15.2 us
    pallas_call x4, Pallas kernels, project(): pl.pallas_call(functools.partial(project_kernel, slot, len(sources)), out...  15.1 us
    ppermute x14, starting transfers between devices, swapped(): lax.ppermute(block, axis, [(i, i ^ bit) for i in range(lax.axis_size(axis...  11.6 us
    pallas_call x2, Pallas kernels, medium_call(): pl.pallas_call(functools.partial(kernel, counts), out_shape=[jax.ShapeDty...  10.3 us
    ppermute x2, starting transfers between devices, forward(): return lax.ppermute(block, axis, [(i, i + 1) for i in range(count - 1)])  9.33 us
  transfers between devices with their start and end apart: 51, of which 21 were waited for; matrix products, arithmetic and copies ran while one was open for 0% of the time, Pallas kernels for 24%

profile of v1, /device:TPU:15, one launch (start us, length us, event | category | flops | bytes accessed | tf_op | source)
XLA Modules:
  0.0 229.2 jit_solution(8973157355264019228)
XLA Ops:
  4.5 3.8 %collective-permute-start = (bf16[1024,6]{0,1:T(8,128)(2,1)S(1)}, bf16[1024,6]{0,1:T(8,128)(2,1)S(1)}, u32[]{:S(2)}, u32[]{:S(2)}) collective-permute-start(bf16[1024,6]{0,1:T(8,128)(2,1)S(1)} %pad_maximum_fusion), channel_id=1, source_target_pairs={{0,4},{4,8},{8,12},{12,16},{16,20},{20,24},{24,28},{1,5},{5,9},{9,... | collective-permute-start | bytes 36872 | tf_op jit(solution)/shard_map/ppermute | solution.py:545
  9.5 1.6 copy-done.2
  11.1 4.0 %mix.2 = (bf16[8,64,128]{2,1,0:T(8,128)(2,1)S(1)}, bf16[8,64,128]{2,1,0:T(8,128)(2,1)S(1)}, bf16[8,64,128]{2,1,0:T(8,128)(2,1)S(1)}, bf16[8,64,128]{2,1,0:T(8,12...) custom-call(s32[2]{0:T(128)S(1)} %pad_add_fusion.ids_ref, ...), custom_call_target="tpu_custom_call" | custom-call | tf_op jit(solution)/shard_map/mix/pallas_call | solution.py:112
  15.1 3.4 %copy-done = bf16[1024,4096]{1,0:T(8,128)(2,1)S(1)} copy-done((bf16[1024,4096]{1,0:T(8,128)(2,1)S(1)}, bf16[1024,4096]{1,0:T(8,128)(2,1)}, u32[]{:S(2)}) %copy-start) | copy-done | bytes 8388632
  18.4 2.9 %turn.2 = (bf16[1024,1024]{1,0:T(8,128)(2,1)S(1)}, bf16[1024,1024]{1,0:T(8,128)(2,1)S(1)}) custom-call(s32[2]{0:T(128)S(1)} %pad_add_fusion.ids_ref, bf16[1024,4096]{1,0:T(8,128)(2,1)S(1)} %copy-done), custom_call_target="tpu_custom_call" | custom-call | tf_op jit(solution)/shard_map/turn/pallas_call | solution.py:380
  22.0 4.0 %mix.3 = (bf16[8,64,128]{2,1,0:T(8,128)(2,1)S(1)}, bf16[8,64,128]{2,1,0:T(8,128)(2,1)S(1)}, bf16[8,64,128]{2,1,0:T(8,128)(2,1)S(1)}, bf16[8,64,128]{2,1,0:T(8,12...) custom-call(s32[2]{0:T(128)S(1)} %pad_add_fusion.ids_ref, ...), custom_call_target="tpu_custom_call" | custom-call | tf_op jit(solution)/shard_map/mix/pallas_call | solution.py:112
  26.0 2.9 %collective-permute-start.3 = (bf16[8,64,128]{2,1,0:T(8,128)(2,1)S(1)}, bf16[8,64,128]{2,1,0:T(8,128)(2,1)S(1)}, u32[]{:S(2)}, u32[]{:S(2)}) collective-permute-start(bf16[8,64,128]{2,1,0:T(8,128)(2,1)S(1)} %get-tuple-element.74), channel_id=1, source_target_pairs={{0,4},{4,8},{8,12},{12,16},{16,20},{20,24},{24,28},{28,0},{1,5},{5... | collective-permute-start | bytes 393224 | tf_op jit(solution)/shard_map/ppermute | solution.py:540
  31.6 3.7 %collective-permute-done.4.refs_2_ = bf16[8,64,128]{2,1,0:T(8,128)(2,1)S(1)} collective-permute-done((bf16[8,64,128]{2,1,0:T(8,128)(2,1)S(1)}, bf16[8,64,128]{2,1,0:T(8,128)(2,1)S(1)}, u32[]{:S(2)}, u32[]{:S(2)}) %collective-permute-start.4) | collective-permute-done | bytes 131104 | tf_op jit(solution)/shard_map/ppermute | solution.py:540
  35.5 10.1 %collective-permute-done.5.refs_3_ = bf16[8,64,128]{2,1,0:T(8,128)(2,1)S(1)} collective-permute-done((bf16[8,64,128]{2,1,0:T(8,128)(2,1)S(1)}, bf16[8,64,128]{2,1,0:T(8,128)(2,1)S(1)}, u32[]{:S(2)}, u32[]{:S(2)}) %collective-permute-start.5) | collective-permute-done | bytes 131104 | tf_op jit(solution)/shard_map/ppermute | solution.py:540
  45.6 2.8 %collective-permute-done.6.refs_4_ = bf16[8,64,128]{2,1,0:T(8,128)(2,1)S(1)} collective-permute-done((bf16[8,64,128]{2,1,0:T(8,128)(2,1)S(1)}, bf16[8,64,128]{2,1,0:T(8,128)(2,1)S(1)}, u32[]{:S(2)}, u32[]{:S(2)}) %collective-permute-start.6) | collective-permute-done | bytes 131104 | tf_op jit(solution)/shard_map/ppermute | solution.py:540
  48.5 9.0 %spectra.1.refs_8_ = f32[128,64,256]{2,1,0:T(8,128)S(1)} custom-call(f32[128,8192]{1,0:T(8,128)S(1)} %copy-done.4, bf16[128,192]{1,0:T(8,128)(2,1)S(1)} %copy-done.16, f32[2,64,128]{2,1,0:T(8,128)S(1)} %copy-done.10, bf16[256,256]{1,0:T(8,128)(2,1)S(1)} %copy-done.6, bf16[256,256]{1,0:T(8,128)(2,1)S(1)} %copy-done.15), custom_call_target="tpu_custom_call" | custom-call | tf_op jit(solution)/shard_map/spectra/pallas_call | solution.py:183
  57.6 7.5 %conv.2 = (bf16[8,64,128]{2,1,0:T(8,128)(2,1)S(1)}, bf16[8,64,128]{2,1,0:T(8,128)(2,1)S(1)}, bf16[8,64,128]{2,1,0:T(8,128)(2,1)S(1)}, bf16[8,64,128]{2,1,0:T(8,1...) custom-call(s32[2]{0:T(128)S(1)} %pad_add_fusion.ids_ref, ...), custom_call_target="tpu_custom_call" | custom-call | tf_op jit(solution)/shard_map/conv/pallas_call | solution.py:265
  65.0 1.8 collective-permute-start.10
  67.2 4.5 %collective-permute-start.12 = (bf16[8,64,128]{2,1,0:T(8,128)(2,1)S(1)}, bf16[8,64,128]{2,1,0:T(8,128)(2,1)S(1)}, u32[]{:S(2)}, u32[]{:S(2)}) collective-permute-start(bf16[8,64,128]{2,1,0:T(8,128)(2,1)S(1)} %get-tuple-element.84), channel_id=1, source_target_pairs={{0,12},{4,16},{8,20},{12,24},{16,28},{20,0},{24,4},{28,8},{1,13},{... | collective-permute-start | bytes 393224 | tf_op jit(solution)/shard_map/ppermute | solution.py:540
  71.8 2.3 %collective-permute-start.13 = (bf16[8,64,128]{2,1,0:T(8,128)(2,1)S(1)}, bf16[8,64,128]{2,1,0:T(8,128)(2,1)S(1)}, u32[]{:S(2)}, u32[]{:S(2)}) collective-permute-start(bf16[8,64,128]{2,1,0:T(8,128)(2,1)S(1)} %get-tuple-element.85), channel_id=1, source_target_pairs={{0,16},{4,20},{8,24},{12,28},{16,0},{20,4},{24,8},{28,12},{1,17},{... | collective-permute-start | bytes 393224 | tf_op jit(solution)/shard_map/ppermute | solution.py:540
  74.1 3.5 %collective-permute-start.14 = (bf16[8,64,128]{2,1,0:T(8,128)(2,1)S(1)}, bf16[8,64,128]{2,1,0:T(8,128)(2,1)S(1)}, u32[]{:S(2)}, u32[]{:S(2)}) collective-permute-start(bf16[8,64,128]{2,1,0:T(8,128)(2,1)S(1)} %get-tuple-element.86), channel_id=1, source_target_pairs={{0,20},{4,24},{8,28},{12,0},{16,4},{20,8},{24,12},{28,16},{1,21},{... | collective-permute-start | bytes 393224 | tf_op jit(solution)/shard_map/ppermute | solution.py:540
  77.7 2.2 collective-permute-start.15
  79.9 5.5 %collective-permute-done.13.refs_4_ = bf16[8,64,128]{2,1,0:T(8,128)(2,1)S(1)} collective-permute-done((bf16[8,64,128]{2,1,0:T(8,128)(2,1)S(1)}, bf16[8,64,128]{2,1,0:T(8,128)(2,1)S(1)}, u32[]{:S(2)}, u32[]{:S(2)}) %collective-permute-start.13) | collective-permute-done | bytes 131104 | tf_op jit(solution)/shard_map/ppermute | solution.py:540
  85.4 3.1 %collective-permute-start.16 = (bf16[8,64,128]{2,1,0:T(8,128)(2,1)S(1)}, bf16[8,64,128]{2,1,0:T(8,128)(2,1)S(1)}, u32[]{:S(2)}, u32[]{:S(2)}) collective-permute-start(bf16[8,64,128]{2,1,0:T(8,128)(2,1)S(1)} %get-tuple-element.88), channel_id=1, source_target_pairs={{0,28},{4,0},{8,4},{12,8},{16,12},{20,16},{24,20},{28,24},{1,29},{... | collective-permute-start | bytes 393224 | tf_op jit(solution)/shard_map/ppermute | solution.py:540
  88.5 3.6 %query.1.refs_8_ = f32[8,1024,128]{2,1,0:T(8,128)S(1)} custom-call(bf16[1024,1024]{1,0:T(8,128)(2,1)S(1)} %copy-done.5, f32[1024,16]{1,0:T(8,128)S(1)} %copy.24.aux_ref), custom_call_target="tpu_custom_call" | custom-call | tf_op jit(solution)/shard_map/query/pallas_call | solution.py:294
  92.1 2.6 %collective-permute-done.15.refs_6_ = bf16[8,64,128]{2,1,0:T(8,128)(2,1)S(1)} collective-permute-done((bf16[8,64,128]{2,1,0:T(8,128)(2,1)S(1)}, bf16[8,64,128]{2,1,0:T(8,128)(2,1)S(1)}, u32[]{:S(2)}, u32[]{:S(2)}) %collective-permute-start.15) | collective-permute-done | bytes 131104 | tf_op jit(solution)/shard_map/ppermute | solution.py:540
  97.0 2.6 %collective-permute-start.21 = (bf16[8,64,128]{2,1,0:T(8,128)(2,1)S(1)}, bf16[8,64,128]{2,1,0:T(8,128)(2,1)S(1)}, u32[]{:S(2)}, u32[]{:S(2)}) collective-permute-start(bf16[8,64,128]{2,1,0:T(8,128)(2,1)S(1)} %get-tuple-element.95), channel_id=1, source_target_pairs={{0,12},{4,16},{8,20},{12,24},{16,28},{20,0},{24,4},{28,8},{1,13},{... | collective-permute-start | bytes 393224 | tf_op jit(solution)/shard_map/ppermute | solution.py:540
  99.6 4.2 %collective-permute-done.19.refs_1_ = bf16[8,64,128]{2,1,0:T(8,128)(2,1)S(1)} collective-permute-done((bf16[8,64,128]{2,1,0:T(8,128)(2,1)S(1)}, bf16[8,64,128]{2,1,0:T(8,128)(2,1)S(1)}, u32[]{:S(2)}, u32[]{:S(2)}) %collective-permute-start.19) | collective-permute-done | bytes 131104 | tf_op jit(solution)/shard_map/ppermute | solution.py:540
  104.0 1.5 collective-permute-start.23
  105.5 7.8 %collective-permute-done.21.refs_3_ = bf16[8,64,128]{2,1,0:T(8,128)(2,1)S(1)} collective-permute-done((bf16[8,64,128]{2,1,0:T(8,128)(2,1)S(1)}, bf16[8,64,128]{2,1,0:T(8,128)(2,1)S(1)}, u32[]{:S(2)}, u32[]{:S(2)}) %collective-permute-start.21) | collective-permute-done | bytes 131104 | tf_op jit(solution)/shard_map/ppermute | solution.py:540
  113.3 2.9 %collective-permute-done.22.refs_4_ = bf16[8,64,128]{2,1,0:T(8,128)(2,1)S(1)} collective-permute-done((bf16[8,64,128]{2,1,0:T(8,128)(2,1)S(1)}, bf16[8,64,128]{2,1,0:T(8,128)(2,1)S(1)}, u32[]{:S(2)}, u32[]{:S(2)}) %collective-permute-start.22) | collective-permute-done | bytes 131104 | tf_op jit(solution)/shard_map/ppermute | solution.py:540
  116.3 6.0 %collective-permute-done.24.refs_6_ = bf16[8,64,128]{2,1,0:T(8,128)(2,1)S(1)} collective-permute-done((bf16[8,64,128]{2,1,0:T(8,128)(2,1)S(1)}, bf16[8,64,128]{2,1,0:T(8,128)(2,1)S(1)}, u32[]{:S(2)}, u32[]{:S(2)}) %collective-permute-start.24) | collective-permute-done | bytes 131104 | tf_op jit(solution)/shard_map/ppermute | solution.py:540
  122.3 7.7 %conv.3 = (bf16[4,64,128]{2,1,0:T(8,128)(2,1)S(1)}, bf16[4,64,128]{2,1,0:T(8,128)(2,1)S(1)}, bf16[4,64,128]{2,1,0:T(8,128)(2,1)S(1)}, bf16[4,64,128]{2,1,0:T(8,1...) custom-call(s32[2]{0:T(128)S(1)} %pad_add_fusion.ids_ref, ...), custom_call_target="tpu_custom_call" | custom-call | tf_op jit(solution)/shard_map/conv/pallas_call | solution.py:265
  131.7 1.8 collective-permute-start.28
  134.4 3.6 %collective-permute-start.39 = (bf16[4,64,128]{2,1,0:T(8,128)(2,1)S(1)}, bf16[4,64,128]{2,1,0:T(8,128)(2,1)S(1)}, u32[]{:S(2)}, u32[]{:S(2)}) collective-permute-start(bf16[4,64,128]{2,1,0:T(8,128)(2,1)S(1)} %get-tuple-element.120), channel_id=1, source_target_pairs={{0,4},{4,8},{8,12},{12,16},{16,20},{20,24},{24,28},{28,0},{1,5},{5... | collective-permute-start | bytes 196616 | tf_op jit(solution)/shard_map/ppermute | solution.py:540
  138.0 2.0 collective-permute-start.40
  139.9 4.2 %collective-permute-start.41 = (bf16[4,64,128]{2,1,0:T(8,128)(2,1)S(1)}, bf16[4,64,128]{2,1,0:T(8,128)(2,1)S(1)}, u32[]{:S(2)}, u32[]{:S(2)}) collective-permute-start(bf16[4,64,128]{2,1,0:T(8,128)(2,1)S(1)} %get-tuple-element.122), channel_id=1, source_target_pairs={{0,12},{4,16},{8,20},{12,24},{16,28},{20,0},{24,4},{28,8},{1,13},{... | collective-permute-start | bytes 196616 | tf_op jit(solution)/shard_map/ppermute | solution.py:540
  144.1 3.8 %collective-permute-start.43 = (bf16[4,64,128]{2,1,0:T(8,128)(2,1)S(1)}, bf16[4,64,128]{2,1,0:T(8,128)(2,1)S(1)}, u32[]{:S(2)}, u32[]{:S(2)}) collective-permute-start(bf16[4,64,128]{2,1,0:T(8,128)(2,1)S(1)} %get-tuple-element.124), channel_id=1, source_target_pairs={{0,20},{4,24},{8,28},{12,0},{16,4},{20,8},{24,12},{28,16},{1,21},{... | collective-permute-start | bytes 196616 | tf_op jit(solution)/shard_map/ppermute | solution.py:540
  148.1 2.2 collective-permute-done.42.refs_4_
  150.6 4.1 %collective-permute-start.30 = (bf16[4,64,128]{2,1,0:T(8,128)(2,1)S(1)}, bf16[4,64,128]{2,1,0:T(8,128)(2,1)S(1)}, u32[]{:S(2)}, u32[]{:S(2)}) collective-permute-start(bf16[4,64,128]{2,1,0:T(8,128)(2,1)S(1)} %get-tuple-element.105), channel_id=1, source_target_pairs={{0,20},{4,24},{8,28},{12,0},{16,4},{20,8},{24,12},{28,16},{1,21},{... | collective-permute-start | bytes 196616 | tf_op jit(solution)/shard_map/ppermute | solution.py:540
  160.9 3.2 %collective-permute-done.46.refs_6_ = bf16[512,256]{1,0:T(8,128)(2,1)S(1)} collective-permute-done((bf16[512,256]{1,0:T(8,128)(2,1)S(1)}, bf16[512,256]{1,0:T(8,128)(2,1)S(1)}, u32[]{:S(2)}, u32[]{:S(2)}) %collective-permute-start.46) | collective-permute-done | bytes 262176 | tf_op jit(solution)/shard_map/ppermute | solution.py:549
  165.4 4.2 %turn.3 = (bf16[1024,1024]{1,0:T(8,128)(2,1)S(1)}, bf16[1024,1024]{1,0:T(8,128)(2,1)S(1)}, bf16[1024,1024]{1,0:T(8,128)(2,1)S(1)}) custom-call(s32[2]{0:T(128)S(1)} %pad_add_fusion.ids_ref, bf16[1024,4096]{1,0:T(8,128)(2,1)S(1)} %bitcast.5), custom_call_target="tpu_custom_call" | custom-call | tf_op jit(solution)/shard_map/turn/pallas_call | solution.py:380
  170.7 6.0 %collective-permute-done.47.refs_7_ = bf16[512,256]{1,0:T(8,128)(2,1)S(1)} collective-permute-done((bf16[512,256]{1,0:T(8,128)(2,1)S(1)}, bf16[512,256]{1,0:T(8,128)(2,1)S(1)}, u32[]{:S(2)}, u32[]{:S(2)}) %collective-permute-start.47) | collective-permute-done | bytes 262176 | tf_op jit(solution)/shard_map/ppermute | solution.py:549
  176.7 3.8 %project.7 = (bf16[1024,256]{1,0:T(8,128)(2,1)S(1)}, bf16[1024,256]{1,0:T(8,128)(2,1)S(1)}) custom-call(s32[2]{0:T(128)S(1)} %pad_add_fusion.ids_ref, bf16[512,512]{1,0:T(8,128)(2,1)S(1)} %get-tuple-element.90.refs_0_, bf16[512,512]{1,0:T(8,128)(2,1)S(1)} %get-tuple-element.91.refs_1_, bf16[512,512]{1,0:T(8,128)(2,1)S(1)} %collective-permute-done.17.refs_2_, ...), custom_call_target="tpu_custom_call" | custom-call | tf_op jit(solution)/shard_map/project/pallas_call | solution.py:434
  181.8 1.9 collective-permute-start.49
  184.0 15.8 %collective-permute-done.33.refs_6_ = bf16[512,256]{1,0:T(8,128)(2,1)S(1)} collective-permute-done((bf16[512,256]{1,0:T(8,128)(2,1)S(1)}, bf16[512,256]{1,0:T(8,128)(2,1)S(1)}, u32[]{:S(2)}, u32[]{:S(2)}) %collective-permute-start.33) | collective-permute-done | bytes 262176 | tf_op jit(solution)/shard_map/ppermute | solution.py:549
  199.8 3.8 %project.5 = (bf16[1024,256]{1,0:T(8,128)(2,1)S(1)}, bf16[1024,256]{1,0:T(8,128)(2,1)S(1)}) custom-call(s32[2]{0:T(128)S(1)} %pad_add_fusion.ids_ref, bf16[512,512]{1,0:T(8,128)(2,1)S(1)} %get-tuple-element.90.refs_0_, bf16[512,512]{1,0:T(8,128)(2,1)S(1)} %get-tuple-element.91.refs_1_, bf16[512,512]{1,0:T(8,128)(2,1)S(1)} %collective-permute-done.17.refs_2_, ...), custom_call_target="tpu_custom_call" | custom-call | tf_op jit(solution)/shard_map/project/pallas_call | solution.py:434
  203.9 1.8 collective-permute-start.38
  205.7 3.8 %project.6 = (bf16[1024,256]{1,0:T(8,128)(2,1)S(1)}, bf16[1024,256]{1,0:T(8,128)(2,1)S(1)}) custom-call(s32[2]{0:T(128)S(1)} %pad_add_fusion.ids_ref, bf16[512,512]{1,0:T(8,128)(2,1)S(1)} %get-tuple-element.90.refs_0_, bf16[512,512]{1,0:T(8,128)(2,1)S(1)} %get-tuple-element.91.refs_1_, bf16[512,512]{1,0:T(8,128)(2,1)S(1)} %collective-permute-done.17.refs_2_, ...), custom_call_target="tpu_custom_call" | custom-call | tf_op jit(solution)/shard_map/project/pallas_call | solution.py:434
  209.5 3.6 %shard_map.176 = (bf16[1024,512]{1,0:T(8,128)(2,1)S(1)}, bf16[1024,128]{1,0:T(8,128)(2,1)S(1)}, bf16[1024,384]{1,0:T(8,128)(2,1)S(1)}) custom-call(bf16[1024,256]{1,0:T(8,128)(2,1)S(1)} %get-tuple-element.129.refs_0_, bf16[1024,256]{1,0:T(8,128)(2,1)S(1)} %collective-permute-done.48.refs_1_, bf16[1024,256]{1,0:T(8,128)(2,1)S(1)} %get-tuple-element.131.refs_2_, ...), custom_call_target="tpu_custom_call" | custom-call | tf_op jit(solution)/shard_map/pallas_call | solution.py:524
  213.2 5.6 %collective-permute-start.50 = (bf16[1024,128]{1,0:T(8,128)(2,1)S(1)}, bf16[1024,128]{1,0:T(8,128)(2,1)S(1)}, u32[]{:S(2)}, u32[]{:S(2)}) collective-permute-start(bf16[1024,128]{1,0:T(8,128)(2,1)S(1)} %get-tuple-element.133), channel_id=1, source_target_pairs={{0,4},{4,8},{8,12},{12,16},{16,20},{20,24},{24,28},{1,5},{5,9},{9,... | collective-permute-start | bytes 786440 | tf_op jit(solution)/shard_map/ppermute | solution.py:545
  218.7 3.8 %project.4 = (bf16[1024,256]{1,0:T(8,128)(2,1)S(1)}, bf16[1024,256]{1,0:T(8,128)(2,1)S(1)}) custom-call(s32[2]{0:T(128)S(1)} %pad_add_fusion.ids_ref, bf16[512,512]{1,0:T(8,128)(2,1)S(1)} %get-tuple-element.90.refs_0_, bf16[512,512]{1,0:T(8,128)(2,1)S(1)} %get-tuple-element.91.refs_1_, bf16[512,512]{1,0:T(8,128)(2,1)S(1)} %collective-permute-done.17.refs_2_, ...), custom_call_target="tpu_custom_call" | custom-call | tf_op jit(solution)/shard_map/project/pallas_call | solution.py:434
  222.6 6.6 %shard_map.177 = (bf16[1024,1024]{1,0:T(8,128)(2,1)}, bf16[1024,1024]{1,0:T(8,128)(2,1)}) custom-call(bf16[1024,256]{1,0:T(8,128)(2,1)S(1)} %get-tuple-element.113.refs_0_, bf16[1024,256]{1,0:T(8,128)(2,1)S(1)} %collective-permute-done.37.refs_1_, bf16[1024,256]{1,0:T(8,128)(2,1)S(1)} %get-tuple-element.117.refs_2_, ...), custom_call_target="tpu_custom_call" | custom-call | tf_op jit(solution)/shard_map/pallas_call | solution.py:524
  (125 shorter events, 25.0 us)
Async XLA Ops:
  4.5 4.6 %collective-permute-start = (bf16[1024,6]{0,1:T(8,128)(2,1)S(1)}, bf16[1024,6]{0,1:T(8,128)(2,1)S(1)}, u32[]{:S(2)}, u32[]{:S(2)}) collective-permute-start(bf16[1024,6]{0,1:T(8,128)(2,1)S(1)} %pad_maximum_fusion), channel_id=1, source_target_pairs={{0,4},{4,8},{8,12},{12,16},{16,20},{20,24},{24,28},{1,5},{5,9},{9,... | collective-permute-start | bytes 36872 | tf_op jit(solution)/shard_map/ppermute | solution.py:545
  21.4 75.0 %collective-permute-start.1 = (bf16[1024,1024]{1,0:T(8,128)(2,1)S(1)}, bf16[1024,1024]{1,0:T(8,128)(2,1)S(1)}, u32[]{:S(2)}, u32[]{:S(2)}) collective-permute-start(bf16[1024,1024]{1,0:T(8,128)(2,1)S(1)} %get-tuple-element.71), channel_id=1, source_target_pairs={{0,1},{1,0},{2,3},{3,2},{4,5},{5,4},{6,7},{7,6},{8,9},{9,8},{10,11... | collective-permute-start | bytes 6291464 | tf_op jit(solution)/shard_map/ppermute | solution.py:549
  21.7 74.7 %collective-permute-start.2 = (bf16[1024,1024]{1,0:T(8,128)(2,1)S(1)}, bf16[1024,1024]{1,0:T(8,128)(2,1)S(1)}, u32[]{:S(2)}, u32[]{:S(2)}) collective-permute-start(bf16[1024,1024]{1,0:T(8,128)(2,1)S(1)} %get-tuple-element.72), channel_id=1, source_target_pairs={{0,2},{1,3},{2,0},{3,1},{4,6},{5,7},{6,4},{7,5},{8,10},{9,11},{10,... | collective-permute-start | bytes 6291464 | tf_op jit(solution)/shard_map/ppermute | solution.py:549
  26.0 5.6 %collective-permute-start.3 = (bf16[8,64,128]{2,1,0:T(8,128)(2,1)S(1)}, bf16[8,64,128]{2,1,0:T(8,128)(2,1)S(1)}, u32[]{:S(2)}, u32[]{:S(2)}) collective-permute-start(bf16[8,64,128]{2,1,0:T(8,128)(2,1)S(1)} %get-tuple-element.74), channel_id=1, source_target_pairs={{0,4},{4,8},{8,12},{12,16},{16,20},{20,24},{24,28},{28,0},{1,5},{5... | collective-permute-start | bytes 393224 | tf_op jit(solution)/shard_map/ppermute | solution.py:540
  28.9 6.4 %collective-permute-start.4 = (bf16[8,64,128]{2,1,0:T(8,128)(2,1)S(1)}, bf16[8,64,128]{2,1,0:T(8,128)(2,1)S(1)}, u32[]{:S(2)}, u32[]{:S(2)}) collective-permute-start(bf16[8,64,128]{2,1,0:T(8,128)(2,1)S(1)} %get-tuple-element.75), channel_id=1, source_target_pairs={{0,8},{4,12},{8,16},{12,20},{16,24},{20,28},{24,0},{28,4},{1,9},{5... | collective-permute-start | bytes 393224 | tf_op jit(solution)/shard_map/ppermute | solution.py:540
  30.2 15.4 %collective-permute-start.5 = (bf16[8,64,128]{2,1,0:T(8,128)(2,1)S(1)}, bf16[8,64,128]{2,1,0:T(8,128)(2,1)S(1)}, u32[]{:S(2)}, u32[]{:S(2)}) collective-permute-start(bf16[8,64,128]{2,1,0:T(8,128)(2,1)S(1)} %get-tuple-element.76), channel_id=1, source_target_pairs={{0,12},{4,16},{8,20},{12,24},{16,28},{20,0},{24,4},{28,8},{1,13},{... | collective-permute-start | bytes 393224 | tf_op jit(solution)/shard_map/ppermute | solution.py:540
  31.6 16.9 %collective-permute-start.6 = (bf16[8,64,128]{2,1,0:T(8,128)(2,1)S(1)}, bf16[8,64,128]{2,1,0:T(8,128)(2,1)S(1)}, u32[]{:S(2)}, u32[]{:S(2)}) collective-permute-start(bf16[8,64,128]{2,1,0:T(8,128)(2,1)S(1)} %get-tuple-element.77), channel_id=1, source_target_pairs={{0,16},{4,20},{8,24},{12,28},{16,0},{20,4},{24,8},{28,12},{1,17},{... | collective-permute-start | bytes 393224 | tf_op jit(solution)/shard_map/ppermute | solution.py:540
  35.3 22.2 %collective-permute-start.7 = (bf16[8,64,128]{2,1,0:T(8,128)(2,1)S(1)}, bf16[8,64,128]{2,1,0:T(8,128)(2,1)S(1)}, u32[]{:S(2)}, u32[]{:S(2)}) collective-permute-start(bf16[8,64,128]{2,1,0:T(8,128)(2,1)S(1)} %get-tuple-element.78), channel_id=1, source_target_pairs={{0,20},{4,24},{8,28},{12,0},{16,4},{20,8},{24,12},{28,16},{1,21},{... | collective-permute-start | bytes 393224 | tf_op jit(solution)/shard_map/ppermute | solution.py:540
  45.6 11.9 %collective-permute-start.8 = (bf16[8,64,128]{2,1,0:T(8,128)(2,1)S(1)}, bf16[8,64,128]{2,1,0:T(8,128)(2,1)S(1)}, u32[]{:S(2)}, u32[]{:S(2)}) collective-permute-start(bf16[8,64,128]{2,1,0:T(8,128)(2,1)S(1)} %get-tuple-element.79), channel_id=1, source_target_pairs={{0,24},{4,28},{8,0},{12,4},{16,8},{20,12},{24,16},{28,20},{1,25},{... | collective-permute-start | bytes 393224 | tf_op jit(solution)/shard_map/ppermute | solution.py:540
  48.5 9.0 %collective-permute-start.9 = (bf16[8,64,128]{2,1,0:T(8,128)(2,1)S(1)}, bf16[8,64,128]{2,1,0:T(8,128)(2,1)S(1)}, u32[]{:S(2)}, u32[]{:S(2)}) collective-permute-start(bf16[8,64,128]{2,1,0:T(8,128)(2,1)S(1)} %get-tuple-element.80), channel_id=1, source_target_pairs={{0,28},{4,0},{8,4},{12,8},{16,12},{20,16},{24,20},{28,24},{1,29},{... | collective-permute-start | bytes 393224 | tf_op jit(solution)/shard_map/ppermute | solution.py:540
  65.0 6.7 %collective-permute-start.10 = (bf16[8,64,128]{2,1,0:T(8,128)(2,1)S(1)}, bf16[8,64,128]{2,1,0:T(8,128)(2,1)S(1)}, u32[]{:S(2)}, u32[]{:S(2)}) collective-permute-start(bf16[8,64,128]{2,1,0:T(8,128)(2,1)S(1)} %get-tuple-element.82), channel_id=1, source_target_pairs={{0,4},{4,8},{8,12},{12,16},{16,20},{20,24},{24,28},{28,0},{1,5},{5... | collective-permute-start | bytes 393224 | tf_op jit(solution)/shard_map/ppermute | solution.py:540
  66.8 7.3 %collective-permute-start.11 = (bf16[8,64,128]{2,1,0:T(8,128)(2,1)S(1)}, bf16[8,64,128]{2,1,0:T(8,128)(2,1)S(1)}, u32[]{:S(2)}, u32[]{:S(2)}) collective-permute-start(bf16[8,64,128]{2,1,0:T(8,128)(2,1)S(1)} %get-tuple-element.83), channel_id=1, source_target_pairs={{0,8},{4,12},{8,16},{12,20},{16,24},{20,28},{24,0},{28,4},{1,9},{5... | collective-permute-start | bytes 393224 | tf_op jit(solution)/shard_map/ppermute | solution.py:540
  67.2 10.4 %collective-permute-start.12 = (bf16[8,64,128]{2,1,0:T(8,128)(2,1)S(1)}, bf16[8,64,128]{2,1,0:T(8,128)(2,1)S(1)}, u32[]{:S(2)}, u32[]{:S(2)}) collective-permute-start(bf16[8,64,128]{2,1,0:T(8,128)(2,1)S(1)} %get-tuple-element.84), channel_id=1, source_target_pairs={{0,12},{4,16},{8,20},{12,24},{16,28},{20,0},{24,4},{28,8},{1,13},{... | collective-permute-start | bytes 393224 | tf_op jit(solution)/shard_map/ppermute | solution.py:540
  71.8 13.6 %collective-permute-start.13 = (bf16[8,64,128]{2,1,0:T(8,128)(2,1)S(1)}, bf16[8,64,128]{2,1,0:T(8,128)(2,1)S(1)}, u32[]{:S(2)}, u32[]{:S(2)}) collective-permute-start(bf16[8,64,128]{2,1,0:T(8,128)(2,1)S(1)} %get-tuple-element.85), channel_id=1, source_target_pairs={{0,16},{4,20},{8,24},{12,28},{16,0},{20,4},{24,8},{28,12},{1,17},{... | collective-permute-start | bytes 393224 | tf_op jit(solution)/shard_map/ppermute | solution.py:540
  74.1 18.0 %collective-permute-start.14 = (bf16[8,64,128]{2,1,0:T(8,128)(2,1)S(1)}, bf16[8,64,128]{2,1,0:T(8,128)(2,1)S(1)}, u32[]{:S(2)}, u32[]{:S(2)}) collective-permute-start(bf16[8,64,128]{2,1,0:T(8,128)(2,1)S(1)} %get-tuple-element.86), channel_id=1, source_target_pairs={{0,20},{4,24},{8,28},{12,0},{16,4},{20,8},{24,12},{28,16},{1,21},{... | collective-permute-start | bytes 393224 | tf_op jit(solution)/shard_map/ppermute | solution.py:540
  77.7 17.1 %collective-permute-start.15 = (bf16[8,64,128]{2,1,0:T(8,128)(2,1)S(1)}, bf16[8,64,128]{2,1,0:T(8,128)(2,1)S(1)}, u32[]{:S(2)}, u32[]{:S(2)}) collective-permute-start(bf16[8,64,128]{2,1,0:T(8,128)(2,1)S(1)} %get-tuple-element.87), channel_id=1, source_target_pairs={{0,24},{4,28},{8,0},{12,4},{16,8},{20,12},{24,16},{28,20},{1,25},{... | collective-permute-start | bytes 393224 | tf_op jit(solution)/shard_map/ppermute | solution.py:540
  85.4 9.5 %collective-permute-start.16 = (bf16[8,64,128]{2,1,0:T(8,128)(2,1)S(1)}, bf16[8,64,128]{2,1,0:T(8,128)(2,1)S(1)}, u32[]{:S(2)}, u32[]{:S(2)}) collective-permute-start(bf16[8,64,128]{2,1,0:T(8,128)(2,1)S(1)} %get-tuple-element.88), channel_id=1, source_target_pairs={{0,28},{4,0},{8,4},{12,8},{16,12},{20,16},{24,20},{28,24},{1,29},{... | collective-permute-start | bytes 393224 | tf_op jit(solution)/shard_map/ppermute | solution.py:540
  96.4 80.3 %collective-permute-start.35 = (bf16[1024,1024]{1,0:T(8,128)(2,1)S(1)}, bf16[1024,1024]{1,0:T(8,128)(2,1)S(1)}, u32[]{:S(2)}, u32[]{:S(2)}) collective-permute-start(bf16[1024,1024]{1,0:T(8,128)(2,1)S(1)} %collective-permute-done.1.refs_10_), channel_id=1, source_target_pairs={{0,4},{4,0},{8,12},{12,8},{16,20},{20,16},{24,28},{28,24},{1,5},{5... | collective-permute-start | bytes 6291464 | tf_op jit(solution)/shard_map/ppermute | solution.py:549
  96.5 80.2 %collective-permute-start.36 = (bf16[1024,1024]{1,0:T(8,128)(2,1)S(1)}, bf16[1024,1024]{1,0:T(8,128)(2,1)S(1)}, u32[]{:S(2)}, u32[]{:S(2)}) collective-permute-start(bf16[1024,1024]{1,0:T(8,128)(2,1)S(1)} %collective-permute-done.2.refs_12_), channel_id=1, source_target_pairs={{0,4},{4,0},{8,12},{12,8},{16,20},{20,16},{24,28},{28,24},{1,5},{5... | collective-permute-start | bytes 6291464 | tf_op jit(solution)/shard_map/ppermute | solution.py:549
  97.0 6.8 %collective-permute-start.19 = (bf16[8,64,128]{2,1,0:T(8,128)(2,1)S(1)}, bf16[8,64,128]{2,1,0:T(8,128)(2,1)S(1)}, u32[]{:S(2)}, u32[]{:S(2)}) collective-permute-start(bf16[8,64,128]{2,1,0:T(8,128)(2,1)S(1)} %get-tuple-element.93), channel_id=1, source_target_pairs={{0,4},{4,8},{8,12},{12,16},{16,20},{20,24},{24,28},{28,0},{1,5},{5... | collective-permute-start | bytes 393224 | tf_op jit(solution)/shard_map/ppermute | solution.py:540
  97.0 7.0 %collective-permute-start.20 = (bf16[8,64,128]{2,1,0:T(8,128)(2,1)S(1)}, bf16[8,64,128]{2,1,0:T(8,128)(2,1)S(1)}, u32[]{:S(2)}, u32[]{:S(2)}) collective-permute-start(bf16[8,64,128]{2,1,0:T(8,128)(2,1)S(1)} %get-tuple-element.94), channel_id=1, source_target_pairs={{0,8},{4,12},{8,16},{12,20},{16,24},{20,28},{24,0},{28,4},{1,9},{5... | collective-permute-start | bytes 393224 | tf_op jit(solution)/shard_map/ppermute | solution.py:540
  97.0 16.3 %collective-permute-start.21 = (bf16[8,64,128]{2,1,0:T(8,128)(2,1)S(1)}, bf16[8,64,128]{2,1,0:T(8,128)(2,1)S(1)}, u32[]{:S(2)}, u32[]{:S(2)}) collective-permute-start(bf16[8,64,128]{2,1,0:T(8,128)(2,1)S(1)} %get-tuple-element.95), channel_id=1, source_target_pairs={{0,12},{4,16},{8,20},{12,24},{16,28},{20,0},{24,4},{28,8},{1,13},{... | collective-permute-start | bytes 393224 | tf_op jit(solution)/shard_map/ppermute | solution.py:540
  103.8 12.5 %collective-permute-start.22 = (bf16[8,64,128]{2,1,0:T(8,128)(2,1)S(1)}, bf16[8,64,128]{2,1,0:T(8,128)(2,1)S(1)}, u32[]{:S(2)}, u32[]{:S(2)}) collective-permute-start(bf16[8,64,128]{2,1,0:T(8,128)(2,1)S(1)} %get-tuple-element.96), channel_id=1, source_target_pairs={{0,16},{4,20},{8,24},{12,28},{16,0},{20,4},{24,8},{28,12},{1,17},{... | collective-permute-start | bytes 393224 | tf_op jit(solution)/shard_map/ppermute | solution.py:540
  104.0 12.3 %collective-permute-start.23 = (bf16[8,64,128]{2,1,0:T(8,128)(2,1)S(1)}, bf16[8,64,128]{2,1,0:T(8,128)(2,1)S(1)}, u32[]{:S(2)}, u32[]{:S(2)}) collective-permute-start(bf16[8,64,128]{2,1,0:T(8,128)(2,1)S(1)} %get-tuple-element.97), channel_id=1, source_target_pairs={{0,20},{4,24},{8,28},{12,0},{16,4},{20,8},{24,12},{28,16},{1,21},{... | collective-permute-start | bytes 393224 | tf_op jit(solution)/shard_map/ppermute | solution.py:540
  113.3 8.9 %collective-permute-start.24 = (bf16[8,64,128]{2,1,0:T(8,128)(2,1)S(1)}, bf16[8,64,128]{2,1,0:T(8,128)(2,1)S(1)}, u32[]{:S(2)}, u32[]{:S(2)}) collective-permute-start(bf16[8,64,128]{2,1,0:T(8,128)(2,1)S(1)} %get-tuple-element.98), channel_id=1, source_target_pairs={{0,24},{4,28},{8,0},{12,4},{16,8},{20,12},{24,16},{28,20},{1,25},{... | collective-permute-start | bytes 393224 | tf_op jit(solution)/shard_map/ppermute | solution.py:540
  116.3 6.1 %collective-permute-start.25 = (bf16[8,64,128]{2,1,0:T(8,128)(2,1)S(1)}, bf16[8,64,128]{2,1,0:T(8,128)(2,1)S(1)}, u32[]{:S(2)}, u32[]{:S(2)}) collective-permute-start(bf16[8,64,128]{2,1,0:T(8,128)(2,1)S(1)} %get-tuple-element.99), channel_id=1, source_target_pairs={{0,28},{4,0},{8,4},{12,8},{16,12},{20,16},{24,20},{28,24},{1,29},{... | collective-permute-start | bytes 393224 | tf_op jit(solution)/shard_map/ppermute | solution.py:540
  131.7 6.3 %collective-permute-start.28 = (bf16[4,64,128]{2,1,0:T(8,128)(2,1)S(1)}, bf16[4,64,128]{2,1,0:T(8,128)(2,1)S(1)}, u32[]{:S(2)}, u32[]{:S(2)}) collective-permute-start(bf16[4,64,128]{2,1,0:T(8,128)(2,1)S(1)} %get-tuple-element.103), channel_id=1, source_target_pairs={{0,12},{4,16},{8,20},{12,24},{16,28},{20,0},{24,4},{28,8},{1,13},{... | collective-permute-start | bytes 196616 | tf_op jit(solution)/shard_map/ppermute | solution.py:540
  133.4 6.5 %collective-permute-start.29 = (bf16[4,64,128]{2,1,0:T(8,128)(2,1)S(1)}, bf16[4,64,128]{2,1,0:T(8,128)(2,1)S(1)}, u32[]{:S(2)}, u32[]{:S(2)}) collective-permute-start(bf16[4,64,128]{2,1,0:T(8,128)(2,1)S(1)} %get-tuple-element.104), channel_id=1, source_target_pairs={{0,16},{4,20},{8,24},{12,28},{16,0},{20,4},{24,8},{28,12},{1,17},{... | collective-permute-start | bytes 196616 | tf_op jit(solution)/shard_map/ppermute | solution.py:540
  134.4 9.8 %collective-permute-start.39 = (bf16[4,64,128]{2,1,0:T(8,128)(2,1)S(1)}, bf16[4,64,128]{2,1,0:T(8,128)(2,1)S(1)}, u32[]{:S(2)}, u32[]{:S(2)}) collective-permute-start(bf16[4,64,128]{2,1,0:T(8,128)(2,1)S(1)} %get-tuple-element.120), channel_id=1, source_target_pairs={{0,4},{4,8},{8,12},{12,16},{16,20},{20,24},{24,28},{28,0},{1,5},{5... | collective-permute-start | bytes 196616 | tf_op jit(solution)/shard_map/ppermute | solution.py:540
  138.0 6.2 %collective-permute-start.40 = (bf16[4,64,128]{2,1,0:T(8,128)(2,1)S(1)}, bf16[4,64,128]{2,1,0:T(8,128)(2,1)S(1)}, u32[]{:S(2)}, u32[]{:S(2)}) collective-permute-start(bf16[4,64,128]{2,1,0:T(8,128)(2,1)S(1)} %get-tuple-element.121), channel_id=1, source_target_pairs={{0,8},{4,12},{8,16},{12,20},{16,24},{20,28},{24,0},{28,4},{1,9},{5... | collective-permute-start | bytes 196616 | tf_op jit(solution)/shard_map/ppermute | solution.py:540
  139.9 8.0 %collective-permute-start.41 = (bf16[4,64,128]{2,1,0:T(8,128)(2,1)S(1)}, bf16[4,64,128]{2,1,0:T(8,128)(2,1)S(1)}, u32[]{:S(2)}, u32[]{:S(2)}) collective-permute-start(bf16[4,64,128]{2,1,0:T(8,128)(2,1)S(1)} %get-tuple-element.122), channel_id=1, source_target_pairs={{0,12},{4,16},{8,20},{12,24},{16,28},{20,0},{24,4},{28,8},{1,13},{... | collective-permute-start | bytes 196616 | tf_op jit(solution)/shard_map/ppermute | solution.py:540
  144.1 6.1 %collective-permute-start.42 = (bf16[4,64,128]{2,1,0:T(8,128)(2,1)S(1)}, bf16[4,64,128]{2,1,0:T(8,128)(2,1)S(1)}, u32[]{:S(2)}, u32[]{:S(2)}) collective-permute-start(bf16[4,64,128]{2,1,0:T(8,128)(2,1)S(1)} %get-tuple-element.123), channel_id=1, source_target_pairs={{0,16},{4,20},{8,24},{12,28},{16,0},{20,4},{24,8},{28,12},{1,17},{... | collective-permute-start | bytes 196616 | tf_op jit(solution)/shard_map/ppermute | solution.py:540
  144.1 6.4 %collective-permute-start.43 = (bf16[4,64,128]{2,1,0:T(8,128)(2,1)S(1)}, bf16[4,64,128]{2,1,0:T(8,128)(2,1)S(1)}, u32[]{:S(2)}, u32[]{:S(2)}) collective-permute-start(bf16[4,64,128]{2,1,0:T(8,128)(2,1)S(1)} %get-tuple-element.124), channel_id=1, source_target_pairs={{0,20},{4,24},{8,28},{12,0},{16,4},{20,8},{24,12},{28,16},{1,21},{... | collective-permute-start | bytes 196616 | tf_op jit(solution)/shard_map/ppermute | solution.py:540
  147.9 6.7 %collective-permute-start.44 = (bf16[4,64,128]{2,1,0:T(8,128)(2,1)S(1)}, bf16[4,64,128]{2,1,0:T(8,128)(2,1)S(1)}, u32[]{:S(2)}, u32[]{:S(2)}) collective-permute-start(bf16[4,64,128]{2,1,0:T(8,128)(2,1)S(1)} %get-tuple-element.125), channel_id=1, source_target_pairs={{0,24},{4,28},{8,0},{12,4},{16,8},{20,12},{24,16},{28,20},{1,25},{... | collective-permute-start | bytes 196616 | tf_op jit(solution)/shard_map/ppermute | solution.py:540
  150.2 4.4 %collective-permute-start.45 = (bf16[4,64,128]{2,1,0:T(8,128)(2,1)S(1)}, bf16[4,64,128]{2,1,0:T(8,128)(2,1)S(1)}, u32[]{:S(2)}, u32[]{:S(2)}) collective-permute-start(bf16[4,64,128]{2,1,0:T(8,128)(2,1)S(1)} %get-tuple-element.126), channel_id=1, source_target_pairs={{0,28},{4,0},{8,4},{12,8},{16,12},{20,16},{24,20},{28,24},{1,29},{... | collective-permute-start | bytes 196616 | tf_op jit(solution)/shard_map/ppermute | solution.py:540
  150.6 6.5 %collective-permute-start.30 = (bf16[4,64,128]{2,1,0:T(8,128)(2,1)S(1)}, bf16[4,64,128]{2,1,0:T(8,128)(2,1)S(1)}, u32[]{:S(2)}, u32[]{:S(2)}) collective-permute-start(bf16[4,64,128]{2,1,0:T(8,128)(2,1)S(1)} %get-tuple-element.105), channel_id=1, source_target_pairs={{0,20},{4,24},{8,28},{12,0},{16,4},{20,8},{24,12},{28,16},{1,21},{... | collective-permute-start | bytes 196616 | tf_op jit(solution)/shard_map/ppermute | solution.py:540
  154.7 5.0 %collective-permute-start.32 = (bf16[4,64,128]{2,1,0:T(8,128)(2,1)S(1)}, bf16[4,64,128]{2,1,0:T(8,128)(2,1)S(1)}, u32[]{:S(2)}, u32[]{:S(2)}) collective-permute-start(bf16[4,64,128]{2,1,0:T(8,128)(2,1)S(1)} %get-tuple-element.107), channel_id=1, source_target_pairs={{0,28},{4,0},{8,4},{12,8},{16,12},{20,16},{24,20},{28,24},{1,29},{... | collective-permute-start | bytes 196616 | tf_op jit(solution)/shard_map/ppermute | solution.py:540
  157.1 7.1 %collective-permute-start.46 = (bf16[512,256]{1,0:T(8,128)(2,1)S(1)}, bf16[512,256]{1,0:T(8,128)(2,1)S(1)}, u32[]{:S(2)}, u32[]{:S(2)}) collective-permute-start(bf16[512,256]{1,0:T(8,128)(2,1)S(1)} %get-tuple-element.127.refs_4_), channel_id=1, source_target_pairs={{0,1},{1,0},{2,3},{3,2},{4,5},{5,4},{6,7},{7,6},{8,9},{9,8},{10,11... | collective-permute-start | bytes 786440 | tf_op jit(solution)/shard_map/ppermute | solution.py:549
  158.5 18.2 %collective-permute-start.18 = (bf16[512,512]{1,0:T(8,128)(2,1)S(1)}, bf16[512,512]{1,0:T(8,128)(2,1)S(1)}, u32[]{:S(2)}, u32[]{:S(2)}) collective-permute-start(bf16[512,512]{1,0:T(8,128)(2,1)S(1)} %get-tuple-element.91.refs_1_), channel_id=1, source_target_pairs={{0,2},{1,3},{2,0},{3,1},{4,6},{5,7},{6,4},{7,5},{8,10},{9,11},{10,... | collective-permute-start | bytes 1572872 | tf_op jit(solution)/shard_map/ppermute | solution.py:549
  159.7 17.0 %collective-permute-start.17 = (bf16[512,512]{1,0:T(8,128)(2,1)S(1)}, bf16[512,512]{1,0:T(8,128)(2,1)S(1)}, u32[]{:S(2)}, u32[]{:S(2)}) collective-permute-start(bf16[512,512]{1,0:T(8,128)(2,1)S(1)} %get-tuple-element.90.refs_0_), channel_id=1, source_target_pairs={{0,1},{1,0},{2,3},{3,2},{4,5},{5,4},{6,7},{7,6},{8,9},{9,8},{10,11... | collective-permute-start | bytes 1572872 | tf_op jit(solution)/shard_map/ppermute | solution.py:549
  164.1 12.6 %collective-permute-start.47 = (bf16[512,256]{1,0:T(8,128)(2,1)S(1)}, bf16[512,256]{1,0:T(8,128)(2,1)S(1)}, u32[]{:S(2)}, u32[]{:S(2)}) collective-permute-start(bf16[512,256]{1,0:T(8,128)(2,1)S(1)} %get-tuple-element.128.refs_5_), channel_id=1, source_target_pairs={{0,2},{1,3},{2,0},{3,1},{4,6},{5,7},{6,4},{7,5},{8,10},{9,11},{10,... | collective-permute-start | bytes 786440 | tf_op jit(solution)/shard_map/ppermute | solution.py:549
  180.5 28.9 %collective-permute-start.48 = (bf16[1024,256]{1,0:T(8,128)(2,1)S(1)}, bf16[1024,256]{1,0:T(8,128)(2,1)S(1)}, u32[]{:S(2)}, u32[]{:S(2)}) collective-permute-start(bf16[1024,256]{1,0:T(8,128)(2,1)S(1)} %get-tuple-element.130), channel_id=1, source_target_pairs={{0,2},{1,3},{2,0},{3,1},{4,6},{5,7},{6,4},{7,5},{8,10},{9,11},{10,... | collective-permute-start | bytes 1572872 | tf_op jit(solution)/shard_map/ppermute | solution.py:549
  181.8 27.6 %collective-permute-start.49 = (bf16[1024,256]{1,0:T(8,128)(2,1)S(1)}, bf16[1024,256]{1,0:T(8,128)(2,1)S(1)}, u32[]{:S(2)}, u32[]{:S(2)}) collective-permute-start(bf16[1024,256]{1,0:T(8,128)(2,1)S(1)} %get-tuple-element.132), channel_id=1, source_target_pairs={{0,1},{1,0},{2,3},{3,2},{4,5},{5,4},{6,7},{7,6},{8,9},{9,8},{10,11... | collective-permute-start | bytes 1572872 | tf_op jit(solution)/shard_map/ppermute | solution.py:549
  183.7 16.1 %collective-permute-start.33 = (bf16[512,256]{1,0:T(8,128)(2,1)S(1)}, bf16[512,256]{1,0:T(8,128)(2,1)S(1)}, u32[]{:S(2)}, u32[]{:S(2)}) collective-permute-start(bf16[512,256]{1,0:T(8,128)(2,1)S(1)} %get-tuple-element.108.refs_4_), channel_id=1, source_target_pairs={{0,1},{1,0},{2,3},{3,2},{4,5},{5,4},{6,7},{7,6},{8,9},{9,8},{10,11... | collective-permute-start | bytes 786440 | tf_op jit(solution)/shard_map/ppermute | solution.py:549
  183.8 16.1 %collective-permute-start.34 = (bf16[512,256]{1,0:T(8,128)(2,1)S(1)}, bf16[512,256]{1,0:T(8,128)(2,1)S(1)}, u32[]{:S(2)}, u32[]{:S(2)}) collective-permute-start(bf16[512,256]{1,0:T(8,128)(2,1)S(1)} %get-tuple-element.109.refs_5_), channel_id=1, source_target_pairs={{0,2},{1,3},{2,0},{3,1},{4,6},{5,7},{6,4},{7,5},{8,10},{9,11},{10,... | collective-permute-start | bytes 786440 | tf_op jit(solution)/shard_map/ppermute | solution.py:549
  203.6 18.9 %collective-permute-start.37 = (bf16[1024,256]{1,0:T(8,128)(2,1)S(1)}, bf16[1024,256]{1,0:T(8,128)(2,1)S(1)}, u32[]{:S(2)}, u32[]{:S(2)}) collective-permute-start(bf16[1024,256]{1,0:T(8,128)(2,1)S(1)} %get-tuple-element.116), channel_id=1, source_target_pairs={{0,2},{1,3},{2,0},{3,1},{4,6},{5,7},{6,4},{7,5},{8,10},{9,11},{10,... | collective-permute-start | bytes 1572872 | tf_op jit(solution)/shard_map/ppermute | solution.py:549
  203.9 18.6 %collective-permute-start.38 = (bf16[1024,256]{1,0:T(8,128)(2,1)S(1)}, bf16[1024,256]{1,0:T(8,128)(2,1)S(1)}, u32[]{:S(2)}, u32[]{:S(2)}) collective-permute-start(bf16[1024,256]{1,0:T(8,128)(2,1)S(1)} %get-tuple-element.118), channel_id=1, source_target_pairs={{0,1},{1,0},{2,3},{3,2},{4,5},{5,4},{6,7},{7,6},{8,9},{9,8},{10,11... | collective-permute-start | bytes 1572872 | tf_op jit(solution)/shard_map/ppermute | solution.py:549
  213.2 9.4 %collective-permute-start.50 = (bf16[1024,128]{1,0:T(8,128)(2,1)S(1)}, bf16[1024,128]{1,0:T(8,128)(2,1)S(1)}, u32[]{:S(2)}, u32[]{:S(2)}) collective-permute-start(bf16[1024,128]{1,0:T(8,128)(2,1)S(1)} %get-tuple-element.133), channel_id=1, source_target_pairs={{0,4},{4,8},{8,12},{12,16},{16,20},{20,24},{24,28},{1,5},{5,9},{9,... | collective-permute-start | bytes 786440 | tf_op jit(solution)/shard_map/ppermute | solution.py:545
  (23 other events, 363.6 us)

commit v2 on v1

--- a/solution.py
+++ b/solution.py
@@ -51,14 +51,13 @@
     high, low = split_table(outer)
     plain = np.concatenate([high, high, low], axis=1)
     twist = np.stack([twist_re, -twist_im]).astype(np.float32)
-    inner_high, inner_low = split_table(inner)
+    inner_high = split_table(inner)[0]
     return dict(
         fore=np.stack(fore),
         rear=np.stack(rear),
         plain=plain,
         twist=twist,
         inner=inner_high,
-        inner_low=inner_low,
         inner_back=split_table(inner_back)[0],
     )
 
@@ -67,10 +66,10 @@
 def medium_tables(width):
     span = 2 * width
     cos, sin = rotation(np.arange(span), np.arange(width) + 0.5, span)
-    high, low = split_table(np.concatenate([cos, -sin], axis=1))
+    fore = split_table(np.concatenate([cos, -sin], axis=1))[0]
     last = slice(width, span)
     back = np.concatenate([cos[last].T, -sin[last].T], axis=0) / width
-    return high, low, split_table(back)[0]
+    return fore, split_table(back)[0]
 
 
 def grant(mib):
@@ -137,7 +136,7 @@
     return out
 
 
-def filter_kernel(filter_ref, plain_ref, twist_ref, inner_ref, inner_low_ref, out_ref, rows_ref):
+def filter_kernel(filter_ref, plain_ref, twist_ref, inner_ref, out_ref, rows_ref):
     block = filter_ref.shape[0]
     n1 = filter_ref.shape[1] // LANES
     for n in range(n1):
@@ -147,7 +146,7 @@
 
     def body(at, carry):
         base = at * group
-        highs, lows = [], []
+        lines = []
         for pair in range(group // 2):
             loaded = [
                 rows_ref[pl.ds(base + 2 * pair + c, n1, stride=block), :] for c in range(2)
@@ -157,15 +156,8 @@
             low = (both - high.astype(F32)).astype(BF16)
             wide = dot(plain_ref[...], jnp.concatenate([high, low, high], axis=0))
             for re, im in twisted(wide, twist_ref[0], twist_ref[1], 2):
-                line = jnp.concatenate([re, im], axis=1)
-                high = line.astype(BF16)
-                highs.append(high)
-                lows.append((line - high.astype(F32)).astype(BF16))
-        high = jnp.concatenate(highs, axis=0)
-        low = jnp.concatenate(lows, axis=0)
-        spectrum = (
-            dot(high, inner_ref[...]) + dot(low, inner_ref[...]) + dot(high, inner_low_ref[...])
-        )
+                lines.append(jnp.concatenate([re.astype(BF16), im.astype(BF16)], axis=1))
+        spectrum = dot(jnp.concatenate(lines, axis=0), inner_ref[...])
         out_ref[pl.ds(base, group)] = spectrum.reshape(group, n1, 2 * LANES)
         return carry
 
@@ -179,7 +171,7 @@
 def spectra(long_filter, tables, block):
     channels, length = long_filter.shape
     n1 = length // LANES
-    names = ("plain", "twist", "inner", "inner_low")
+    names = ("plain", "twist", "inner")
     return pl.pallas_call(
         filter_kernel,
         out_shape=jax.ShapeDtypeStruct((channels, n1, 2 * LANES), F32),
@@ -451,20 +443,19 @@
     )(ids, *flat, *weights, *sides[0], *sides[1])
 
 
-def medium_spectrum(taps, fore_ref, low_ref):
+def medium_spectrum(taps, fore_ref):
     width = taps.shape[0]
     over_taps = (((0,), (0,)), ((), ()))
     spec = lax.dot_general(taps, fore_ref[:width], over_taps, preferred_element_type=F32)
-    spec = spec + lax.dot_general(taps, low_ref[:width], over_taps, preferred_element_type=F32)
     return spec[:, :width], spec[:, width:]
 
 
-def medium_blocks(wide, ker_re, ker_im, fore_ref, low_ref, back_ref):
+def medium_blocks(wide, ker_re, ker_im, fore_ref, back_ref):
     width = ker_re.shape[1]
     out = []
     for b in range(wide.shape[1] // width - 1):
         window = wide[:, b * width : (b + 2) * width]
-        sig = dot(window, fore_ref[...]) + dot(window, low_ref[...])
+        sig = dot(window, fore_ref[...])
         sig_re, sig_im = sig[:, :width], sig[:, width:]
         product = jnp.concatenate(
             [
@@ -489,17 +480,17 @@
 
 def late_kernel(counts, *refs):
     n = sum(counts)
-    taps_ref, fore_ref, low_ref, back_ref, oper_ref, edge_ref, out_ref = refs[n:]
+    taps_ref, fore_ref, back_ref, oper_ref, edge_ref, out_ref = refs[n:]
     value = joined(refs[:n], counts)
     oper_ref[...] = value
     edge_ref[...] = value[:, -edge_ref.shape[1] :]
-    ker_re, ker_im = medium_spectrum(taps_ref[...], fore_ref, low_ref)
-    out_ref[...] = medium_blocks(value, ker_re, ker_im, fore_ref, low_ref, back_ref)
+    ker_re, ker_im = medium_spectrum(taps_ref[...], fore_ref)
+    out_ref[...] = medium_blocks(value, ker_re, ker_im, fore_ref, back_ref)
 
 
 def early_kernel(counts, *refs):
     n = sum(counts)
-    edge_ref, later_ref, tail_ref, taps_ref, fore_ref, low_ref, back_ref, oper_ref, out_ref = refs[
+    edge_ref, later_ref, tail_ref, taps_ref, fore_ref, back_ref, oper_ref, out_ref = refs[
         n:
     ]
     value = joined(refs[:n], counts)
@@ -507,10 +498,10 @@
     half = value.shape[1]
     oper_ref[:, :half] = value
     oper_ref[:, half:] = later
-    ker_re, ker_im = medium_spectrum(taps_ref[...], fore_ref, low_ref)
+    ker_re, ker_im = medium_spectrum(taps_ref[...], fore_ref)
     width = ker_re.shape[1]
     wide = jnp.concatenate([edge_ref[...], value, later[:, :width]], axis=1)
-    out_ref[:, : half + width] = medium_blocks(wide, ker_re, ker_im, fore_ref, low_ref, back_ref)
+    out_ref[:, : half + width] = medium_blocks(wide, ker_re, ker_im, fore_ref, back_ref)
     out_ref[:, half + width :] = tail_ref[...]
 
 

time: 231 us -> 225 us (0.974)
  Pallas kernels: 72 us -> 65.7 us
    pallas_call x2, Pallas kernels: 10.3 us -> 6.3 us  [medium_call(): pl.pallas_call(functools.partial(kernel, counts), out_shape=[jax.ShapeDty...]
    unnamed x43 -> x39, local copies, waits for them, and re-layouts: 5.44 us -> 5.43 us
  transfers between devices with their start and end apart: 51 -> 51, of which waited for: 21 -> 21; matrix products, arithmetic and copies ran while one was open for 0% -> 0% of each run, Pallas kernels for 24% -> 25%
where the time goes in v2:
time: 225 us; the launch traced here: 224 us
  waiting for transfers between devices  77 us (34%)
  starting transfers between devices  70.3 us (31%)
  Pallas kernels  65.7 us (29%)
  local copies, waits for them, and re-layouts  9.15 us (4%)
    ppermute x35, waiting for transfers between devices, ring(): lax.ppermute(block, axis, [(i, (i + distance) % count) for i in range(cou...  50.9 us
    ppermute x35, starting transfers between devices, ring(): lax.ppermute(block, axis, [(i, (i + distance) % count) for i in range(cou...  49.1 us
    ppermute x14, waiting for transfers between devices, swapped(): lax.ppermute(block, axis, [(i, i ^ bit) for i in range(lax.axis_size(axis...  25.5 us
    pallas_call x2, Pallas kernels, long_conv(): pl.pallas_call(functools.partial(conv_kernel, groups), out_shape=[jax.Sha...  15.2 us
    pallas_call x4, Pallas kernels, project(): pl.pallas_call(functools.partial(project_kernel, slot, len(sources)), out...  15.1 us
    ppermute x14, starting transfers between devices, swapped(): lax.ppermute(block, axis, [(i, i ^ bit) for i in range(lax.axis_size(axis...  11 us
    ppermute x2, starting transfers between devices, forward(): return lax.ppermute(block, axis, [(i, i + 1) for i in range(count - 1)])  10.2 us
    pallas_call x2, Pallas kernels, mix(): pl.pallas_call(mix_kernel, out_shape=[jax.ShapeDtypeStruct((count, rows,...  7.97 us
  transfers between devices with their start and end apart: 51, of which 21 were waited for; matrix products, arithmetic and copies ran while one was open for 0% of the time, Pallas kernels for 25%

profile of v2, /device:TPU:15, one launch (start us, length us, event | category | flops | bytes accessed | tf_op | source)
XLA Modules:
  0.0 223.6 jit_solution(2727101955135942059)
XLA Ops:
  4.5 3.8 %collective-permute-start = (bf16[1024,6]{0,1:T(8,128)(2,1)S(1)}, bf16[1024,6]{0,1:T(8,128)(2,1)S(1)}, u32[]{:S(2)}, u32[]{:S(2)}) collective-permute-start(bf16[1024,6]{0,1:T(8,128)(2,1)S(1)} %pad_maximum_fusion), channel_id=1, source_target_pairs={{0,4},{4,8},{8,12},{12,16},{16,20},{20,24},{24,28},{1,5},{5,9},{9,... | collective-permute-start | bytes 36872 | tf_op jit(solution)/shard_map/ppermute | solution.py:536
  9.5 1.6 copy-done.2
  11.1 4.0 %mix.2 = (bf16[8,64,128]{2,1,0:T(8,128)(2,1)S(1)}, bf16[8,64,128]{2,1,0:T(8,128)(2,1)S(1)}, bf16[8,64,128]{2,1,0:T(8,128)(2,1)S(1)}, bf16[8,64,128]{2,1,0:T(8,12...) custom-call(s32[2]{0:T(128)S(1)} %pad_add_fusion.ids_ref, ...), custom_call_target="tpu_custom_call" | custom-call | tf_op jit(solution)/shard_map/mix/pallas_call | solution.py:111
  15.1 3.4 %copy-done = bf16[1024,4096]{1,0:T(8,128)(2,1)S(1)} copy-done((bf16[1024,4096]{1,0:T(8,128)(2,1)S(1)}, bf16[1024,4096]{1,0:T(8,128)(2,1)}, u32[]{:S(2)}) %copy-start) | copy-done | bytes 8388632
  18.4 2.9 %turn.2 = (bf16[1024,1024]{1,0:T(8,128)(2,1)S(1)}, bf16[1024,1024]{1,0:T(8,128)(2,1)S(1)}) custom-call(s32[2]{0:T(128)S(1)} %pad_add_fusion.ids_ref, bf16[1024,4096]{1,0:T(8,128)(2,1)S(1)} %copy-done), custom_call_target="tpu_custom_call" | custom-call | tf_op jit(solution)/shard_map/turn/pallas_call | solution.py:372
  22.0 4.0 %mix.3 = (bf16[8,64,128]{2,1,0:T(8,128)(2,1)S(1)}, bf16[8,64,128]{2,1,0:T(8,128)(2,1)S(1)}, bf16[8,64,128]{2,1,0:T(8,128)(2,1)S(1)}, bf16[8,64,128]{2,1,0:T(8,12...) custom-call(s32[2]{0:T(128)S(1)} %pad_add_fusion.ids_ref, ...), custom_call_target="tpu_custom_call" | custom-call | tf_op jit(solution)/shard_map/mix/pallas_call | solution.py:111
  26.0 2.9 %collective-permute-start.3 = (bf16[8,64,128]{2,1,0:T(8,128)(2,1)S(1)}, bf16[8,64,128]{2,1,0:T(8,128)(2,1)S(1)}, u32[]{:S(2)}, u32[]{:S(2)}) collective-permute-start(bf16[8,64,128]{2,1,0:T(8,128)(2,1)S(1)} %get-tuple-element.74), channel_id=1, source_target_pairs={{0,4},{4,8},{8,12},{12,16},{16,20},{20,24},{24,28},{28,0},{1,5},{5... | collective-permute-start | bytes 393224 | tf_op jit(solution)/shard_map/ppermute | solution.py:531
  31.6 3.7 %collective-permute-done.4.refs_2_ = bf16[8,64,128]{2,1,0:T(8,128)(2,1)S(1)} collective-permute-done((bf16[8,64,128]{2,1,0:T(8,128)(2,1)S(1)}, bf16[8,64,128]{2,1,0:T(8,128)(2,1)S(1)}, u32[]{:S(2)}, u32[]{:S(2)}) %collective-permute-start.4) | collective-permute-done | bytes 131104 | tf_op jit(solution)/shard_map/ppermute | solution.py:531
  35.5 10.1 %collective-permute-done.5.refs_3_ = bf16[8,64,128]{2,1,0:T(8,128)(2,1)S(1)} collective-permute-done((bf16[8,64,128]{2,1,0:T(8,128)(2,1)S(1)}, bf16[8,64,128]{2,1,0:T(8,128)(2,1)S(1)}, u32[]{:S(2)}, u32[]{:S(2)}) %collective-permute-start.5) | collective-permute-done | bytes 131104 | tf_op jit(solution)/shard_map/ppermute | solution.py:531
  45.6 2.8 %collective-permute-done.6.refs_4_ = bf16[8,64,128]{2,1,0:T(8,128)(2,1)S(1)} collective-permute-done((bf16[8,64,128]{2,1,0:T(8,128)(2,1)S(1)}, bf16[8,64,128]{2,1,0:T(8,128)(2,1)S(1)}, u32[]{:S(2)}, u32[]{:S(2)}) %collective-permute-start.6) | collective-permute-done | bytes 131104 | tf_op jit(solution)/shard_map/ppermute | solution.py:531
  48.5 6.7 %spectra.1.refs_8_ = f32[128,64,256]{2,1,0:T(8,128)S(1)} custom-call(f32[128,8192]{1,0:T(8,128)S(1)} %copy-done.4, bf16[128,192]{1,0:T(8,128)(2,1)S(1)} %copy-done.14, f32[2,64,128]{2,1,0:T(8,128)S(1)} %copy-done.10, bf16[256,256]{1,0:T(8,128)(2,1)S(1)} %copy-done.6), custom_call_target="tpu_custom_call" | custom-call | tf_op jit(solution)/shard_map/spectra/pallas_call | solution.py:175
  55.3 7.5 %conv.2 = (bf16[8,64,128]{2,1,0:T(8,128)(2,1)S(1)}, bf16[8,64,128]{2,1,0:T(8,128)(2,1)S(1)}, bf16[8,64,128]{2,1,0:T(8,128)(2,1)S(1)}, bf16[8,64,128]{2,1,0:T(8,1...) custom-call(s32[2]{0:T(128)S(1)} %pad_add_fusion.ids_ref, ...), custom_call_target="tpu_custom_call" | custom-call | tf_op jit(solution)/shard_map/conv/pallas_call | solution.py:257
  62.8 1.8 collective-permute-start.10
  65.0 4.5 %collective-permute-start.12 = (bf16[8,64,128]{2,1,0:T(8,128)(2,1)S(1)}, bf16[8,64,128]{2,1,0:T(8,128)(2,1)S(1)}, u32[]{:S(2)}, u32[]{:S(2)}) collective-permute-start(bf16[8,64,128]{2,1,0:T(8,128)(2,1)S(1)} %get-tuple-element.84), channel_id=1, source_target_pairs={{0,12},{4,16},{8,20},{12,24},{16,28},{20,0},{24,4},{28,8},{1,13},{... | collective-permute-start | bytes 393224 | tf_op jit(solution)/shard_map/ppermute | solution.py:531
  69.5 2.3 %collective-permute-start.13 = (bf16[8,64,128]{2,1,0:T(8,128)(2,1)S(1)}, bf16[8,64,128]{2,1,0:T(8,128)(2,1)S(1)}, u32[]{:S(2)}, u32[]{:S(2)}) collective-permute-start(bf16[8,64,128]{2,1,0:T(8,128)(2,1)S(1)} %get-tuple-element.85), channel_id=1, source_target_pairs={{0,16},{4,20},{8,24},{12,28},{16,0},{20,4},{24,8},{28,12},{1,17},{... | collective-permute-start | bytes 393224 | tf_op jit(solution)/shard_map/ppermute | solution.py:531
  71.9 3.5 %collective-permute-start.14 = (bf16[8,64,128]{2,1,0:T(8,128)(2,1)S(1)}, bf16[8,64,128]{2,1,0:T(8,128)(2,1)S(1)}, u32[]{:S(2)}, u32[]{:S(2)}) collective-permute-start(bf16[8,64,128]{2,1,0:T(8,128)(2,1)S(1)} %get-tuple-element.86), channel_id=1, source_target_pairs={{0,20},{4,24},{8,28},{12,0},{16,4},{20,8},{24,12},{28,16},{1,21},{... | collective-permute-start | bytes 393224 | tf_op jit(solution)/shard_map/ppermute | solution.py:531
  75.4 2.2 collective-permute-start.15
  77.6 5.5 %collective-permute-done.13.refs_4_ = bf16[8,64,128]{2,1,0:T(8,128)(2,1)S(1)} collective-permute-done((bf16[8,64,128]{2,1,0:T(8,128)(2,1)S(1)}, bf16[8,64,128]{2,1,0:T(8,128)(2,1)S(1)}, u32[]{:S(2)}, u32[]{:S(2)}) %collective-permute-start.13) | collective-permute-done | bytes 131104 | tf_op jit(solution)/shard_map/ppermute | solution.py:531
  83.1 3.1 %collective-permute-start.16 = (bf16[8,64,128]{2,1,0:T(8,128)(2,1)S(1)}, bf16[8,64,128]{2,1,0:T(8,128)(2,1)S(1)}, u32[]{:S(2)}, u32[]{:S(2)}) collective-permute-start(bf16[8,64,128]{2,1,0:T(8,128)(2,1)S(1)} %get-tuple-element.88), channel_id=1, source_target_pairs={{0,28},{4,0},{8,4},{12,8},{16,12},{20,16},{24,20},{28,24},{1,29},{... | collective-permute-start | bytes 393224 | tf_op jit(solution)/shard_map/ppermute | solution.py:531
  86.2 3.6 %query.1.refs_8_ = f32[8,1024,128]{2,1,0:T(8,128)S(1)} custom-call(bf16[1024,1024]{1,0:T(8,128)(2,1)S(1)} %copy-done.5, f32[1024,16]{1,0:T(8,128)S(1)} %copy.22.aux_ref), custom_call_target="tpu_custom_call" | custom-call | tf_op jit(solution)/shard_map/query/pallas_call | solution.py:286
  89.9 2.6 %collective-permute-done.15.refs_6_ = bf16[8,64,128]{2,1,0:T(8,128)(2,1)S(1)} collective-permute-done((bf16[8,64,128]{2,1,0:T(8,128)(2,1)S(1)}, bf16[8,64,128]{2,1,0:T(8,128)(2,1)S(1)}, u32[]{:S(2)}, u32[]{:S(2)}) %collective-permute-start.15) | collective-permute-done | bytes 131104 | tf_op jit(solution)/shard_map/ppermute | solution.py:531
  92.6 1.5 gate.3
  94.8 2.5 %collective-permute-start.21 = (bf16[8,64,128]{2,1,0:T(8,128)(2,1)S(1)}, bf16[8,64,128]{2,1,0:T(8,128)(2,1)S(1)}, u32[]{:S(2)}, u32[]{:S(2)}) collective-permute-start(bf16[8,64,128]{2,1,0:T(8,128)(2,1)S(1)} %get-tuple-element.95), channel_id=1, source_target_pairs={{0,12},{4,16},{8,20},{12,24},{16,28},{20,0},{24,4},{28,8},{1,13},{... | collective-permute-start | bytes 393224 | tf_op jit(solution)/shard_map/ppermute | solution.py:531
  97.3 4.2 %collective-permute-done.19.refs_1_ = bf16[8,64,128]{2,1,0:T(8,128)(2,1)S(1)} collective-permute-done((bf16[8,64,128]{2,1,0:T(8,128)(2,1)S(1)}, bf16[8,64,128]{2,1,0:T(8,128)(2,1)S(1)}, u32[]{:S(2)}, u32[]{:S(2)}) %collective-permute-start.19) | collective-permute-done | bytes 131104 | tf_op jit(solution)/shard_map/ppermute | solution.py:531
  101.7 1.5 collective-permute-start.23
  103.2 7.8 %collective-permute-done.21.refs_3_ = bf16[8,64,128]{2,1,0:T(8,128)(2,1)S(1)} collective-permute-done((bf16[8,64,128]{2,1,0:T(8,128)(2,1)S(1)}, bf16[8,64,128]{2,1,0:T(8,128)(2,1)S(1)}, u32[]{:S(2)}, u32[]{:S(2)}) %collective-permute-start.21) | collective-permute-done | bytes 131104 | tf_op jit(solution)/shard_map/ppermute | solution.py:531
  111.0 2.9 %collective-permute-done.22.refs_4_ = bf16[8,64,128]{2,1,0:T(8,128)(2,1)S(1)} collective-permute-done((bf16[8,64,128]{2,1,0:T(8,128)(2,1)S(1)}, bf16[8,64,128]{2,1,0:T(8,128)(2,1)S(1)}, u32[]{:S(2)}, u32[]{:S(2)}) %collective-permute-start.22) | collective-permute-done | bytes 131104 | tf_op jit(solution)/shard_map/ppermute | solution.py:531
  114.0 6.0 %collective-permute-done.24.refs_6_ = bf16[8,64,128]{2,1,0:T(8,128)(2,1)S(1)} collective-permute-done((bf16[8,64,128]{2,1,0:T(8,128)(2,1)S(1)}, bf16[8,64,128]{2,1,0:T(8,128)(2,1)S(1)}, u32[]{:S(2)}, u32[]{:S(2)}) %collective-permute-start.24) | collective-permute-done | bytes 131104 | tf_op jit(solution)/shard_map/ppermute | solution.py:531
  120.1 7.7 %conv.3 = (bf16[4,64,128]{2,1,0:T(8,128)(2,1)S(1)}, bf16[4,64,128]{2,1,0:T(8,128)(2,1)S(1)}, bf16[4,64,128]{2,1,0:T(8,128)(2,1)S(1)}, bf16[4,64,128]{2,1,0:T(8,1...) custom-call(s32[2]{0:T(128)S(1)} %pad_add_fusion.ids_ref, ...), custom_call_target="tpu_custom_call" | custom-call | tf_op jit(solution)/shard_map/conv/pallas_call | solution.py:257
  129.4 1.8 collective-permute-start.28
  132.1 3.6 %collective-permute-start.39 = (bf16[4,64,128]{2,1,0:T(8,128)(2,1)S(1)}, bf16[4,64,128]{2,1,0:T(8,128)(2,1)S(1)}, u32[]{:S(2)}, u32[]{:S(2)}) collective-permute-start(bf16[4,64,128]{2,1,0:T(8,128)(2,1)S(1)} %get-tuple-element.120), channel_id=1, source_target_pairs={{0,4},{4,8},{8,12},{12,16},{16,20},{20,24},{24,28},{28,0},{1,5},{5... | collective-permute-start | bytes 196616 | tf_op jit(solution)/shard_map/ppermute | solution.py:531
  135.7 2.0 collective-permute-start.40
  137.6 4.2 %collective-permute-start.41 = (bf16[4,64,128]{2,1,0:T(8,128)(2,1)S(1)}, bf16[4,64,128]{2,1,0:T(8,128)(2,1)S(1)}, u32[]{:S(2)}, u32[]{:S(2)}) collective-permute-start(bf16[4,64,128]{2,1,0:T(8,128)(2,1)S(1)} %get-tuple-element.122), channel_id=1, source_target_pairs={{0,12},{4,16},{8,20},{12,24},{16,28},{20,0},{24,4},{28,8},{1,13},{... | collective-permute-start | bytes 196616 | tf_op jit(solution)/shard_map/ppermute | solution.py:531
  141.9 3.8 %collective-permute-start.43 = (bf16[4,64,128]{2,1,0:T(8,128)(2,1)S(1)}, bf16[4,64,128]{2,1,0:T(8,128)(2,1)S(1)}, u32[]{:S(2)}, u32[]{:S(2)}) collective-permute-start(bf16[4,64,128]{2,1,0:T(8,128)(2,1)S(1)} %get-tuple-element.124), channel_id=1, source_target_pairs={{0,20},{4,24},{8,28},{12,0},{16,4},{20,8},{24,12},{28,16},{1,21},{... | collective-permute-start | bytes 196616 | tf_op jit(solution)/shard_map/ppermute | solution.py:531
  145.8 2.2 collective-permute-done.42.refs_4_
  148.3 4.1 %collective-permute-start.30 = (bf16[4,64,128]{2,1,0:T(8,128)(2,1)S(1)}, bf16[4,64,128]{2,1,0:T(8,128)(2,1)S(1)}, u32[]{:S(2)}, u32[]{:S(2)}) collective-permute-start(bf16[4,64,128]{2,1,0:T(8,128)(2,1)S(1)} %get-tuple-element.105), channel_id=1, source_target_pairs={{0,20},{4,24},{8,28},{12,0},{16,4},{20,8},{24,12},{28,16},{1,21},{... | collective-permute-start | bytes 196616 | tf_op jit(solution)/shard_map/ppermute | solution.py:531
  158.7 3.1 %collective-permute-done.46.refs_6_ = bf16[512,256]{1,0:T(8,128)(2,1)S(1)} collective-permute-done((bf16[512,256]{1,0:T(8,128)(2,1)S(1)}, bf16[512,256]{1,0:T(8,128)(2,1)S(1)}, u32[]{:S(2)}, u32[]{:S(2)}) %collective-permute-start.46) | collective-permute-done | bytes 262176 | tf_op jit(solution)/shard_map/ppermute | solution.py:540
  163.1 4.2 %turn.3 = (bf16[1024,1024]{1,0:T(8,128)(2,1)S(1)}, bf16[1024,1024]{1,0:T(8,128)(2,1)S(1)}, bf16[1024,1024]{1,0:T(8,128)(2,1)S(1)}) custom-call(s32[2]{0:T(128)S(1)} %pad_add_fusion.ids_ref, bf16[1024,4096]{1,0:T(8,128)(2,1)S(1)} %bitcast.5), custom_call_target="tpu_custom_call" | custom-call | tf_op jit(solution)/shard_map/turn/pallas_call | solution.py:372
  168.4 6.0 %collective-permute-done.47.refs_7_ = bf16[512,256]{1,0:T(8,128)(2,1)S(1)} collective-permute-done((bf16[512,256]{1,0:T(8,128)(2,1)S(1)}, bf16[512,256]{1,0:T(8,128)(2,1)S(1)}, u32[]{:S(2)}, u32[]{:S(2)}) %collective-permute-start.47) | collective-permute-done | bytes 262176 | tf_op jit(solution)/shard_map/ppermute | solution.py:540
  174.4 1.9 collective-permute-start.33
  176.4 3.8 %project.7 = (bf16[1024,256]{1,0:T(8,128)(2,1)S(1)}, bf16[1024,256]{1,0:T(8,128)(2,1)S(1)}) custom-call(s32[2]{0:T(128)S(1)} %pad_add_fusion.ids_ref, bf16[512,512]{1,0:T(8,128)(2,1)S(1)} %get-tuple-element.90.refs_0_, bf16[512,512]{1,0:T(8,128)(2,1)S(1)} %get-tuple-element.91.refs_1_, bf16[512,512]{1,0:T(8,128)(2,1)S(1)} %collective-permute-done.17.refs_2_, ...), custom_call_target="tpu_custom_call" | custom-call | tf_op jit(solution)/shard_map/project/pallas_call | solution.py:426
  181.7 16.3 %collective-permute-done.34.refs_7_ = bf16[512,256]{1,0:T(8,128)(2,1)S(1)} collective-permute-done((bf16[512,256]{1,0:T(8,128)(2,1)S(1)}, bf16[512,256]{1,0:T(8,128)(2,1)S(1)}, u32[]{:S(2)}, u32[]{:S(2)}) %collective-permute-start.34) | collective-permute-done | bytes 262176 | tf_op jit(solution)/shard_map/ppermute | solution.py:540
  198.0 3.8 %project.5 = (bf16[1024,256]{1,0:T(8,128)(2,1)S(1)}, bf16[1024,256]{1,0:T(8,128)(2,1)S(1)}) custom-call(s32[2]{0:T(128)S(1)} %pad_add_fusion.ids_ref, bf16[512,512]{1,0:T(8,128)(2,1)S(1)} %get-tuple-element.90.refs_0_, bf16[512,512]{1,0:T(8,128)(2,1)S(1)} %get-tuple-element.91.refs_1_, bf16[512,512]{1,0:T(8,128)(2,1)S(1)} %collective-permute-done.17.refs_2_, ...), custom_call_target="tpu_custom_call" | custom-call | tf_op jit(solution)/shard_map/project/pallas_call | solution.py:426
  203.1 3.8 %project.6 = (bf16[1024,256]{1,0:T(8,128)(2,1)S(1)}, bf16[1024,256]{1,0:T(8,128)(2,1)S(1)}) custom-call(s32[2]{0:T(128)S(1)} %pad_add_fusion.ids_ref, bf16[512,512]{1,0:T(8,128)(2,1)S(1)} %get-tuple-element.90.refs_0_, bf16[512,512]{1,0:T(8,128)(2,1)S(1)} %get-tuple-element.91.refs_1_, bf16[512,512]{1,0:T(8,128)(2,1)S(1)} %collective-permute-done.17.refs_2_, ...), custom_call_target="tpu_custom_call" | custom-call | tf_op jit(solution)/shard_map/project/pallas_call | solution.py:426
  207.0 2.3 %shard_map.158 = (bf16[1024,512]{1,0:T(8,128)(2,1)S(1)}, bf16[1024,128]{1,0:T(8,128)(2,1)S(1)}, bf16[1024,384]{1,0:T(8,128)(2,1)S(1)}) custom-call(bf16[1024,256]{1,0:T(8,128)(2,1)S(1)} %get-tuple-element.129.refs_0_, bf16[1024,256]{1,0:T(8,128)(2,1)S(1)} %collective-permute-done.48.refs_1_, bf16[1024,256]{1,0:T(8,128)(2,1)S(1)} %get-tuple-element.131.refs_2_, ...), custom_call_target="tpu_custom_call" | custom-call | tf_op jit(solution)/shard_map/pallas_call | solution.py:515
  209.3 6.5 %collective-permute-start.50 = (bf16[1024,128]{1,0:T(8,128)(2,1)S(1)}, bf16[1024,128]{1,0:T(8,128)(2,1)S(1)}, u32[]{:S(2)}, u32[]{:S(2)}) collective-permute-start(bf16[1024,128]{1,0:T(8,128)(2,1)S(1)} %get-tuple-element.133), channel_id=1, source_target_pairs={{0,4},{4,8},{8,12},{12,16},{16,20},{20,24},{24,28},{1,5},{5,9},{9,... | collective-permute-start | bytes 786440 | tf_op jit(solution)/shard_map/ppermute | solution.py:536
  215.8 3.8 %project.4 = (bf16[1024,256]{1,0:T(8,128)(2,1)S(1)}, bf16[1024,256]{1,0:T(8,128)(2,1)S(1)}) custom-call(s32[2]{0:T(128)S(1)} %pad_add_fusion.ids_ref, bf16[512,512]{1,0:T(8,128)(2,1)S(1)} %get-tuple-element.90.refs_0_, bf16[512,512]{1,0:T(8,128)(2,1)S(1)} %get-tuple-element.91.refs_1_, bf16[512,512]{1,0:T(8,128)(2,1)S(1)} %collective-permute-done.17.refs_2_, ...), custom_call_target="tpu_custom_call" | custom-call | tf_op jit(solution)/shard_map/project/pallas_call | solution.py:426
  219.6 4.0 %shard_map.159 = (bf16[1024,1024]{1,0:T(8,128)(2,1)}, bf16[1024,1024]{1,0:T(8,128)(2,1)}) custom-call(bf16[1024,256]{1,0:T(8,128)(2,1)S(1)} %get-tuple-element.113.refs_0_, bf16[1024,256]{1,0:T(8,128)(2,1)S(1)} %collective-permute-done.37.refs_1_, bf16[1024,256]{1,0:T(8,128)(2,1)S(1)} %get-tuple-element.117.refs_2_, ...), custom_call_target="tpu_custom_call" | custom-call | tf_op jit(solution)/shard_map/pallas_call | solution.py:515
  (121 shorter events, 24.5 us)
Async XLA Ops:
  4.5 4.6 %collective-permute-start = (bf16[1024,6]{0,1:T(8,128)(2,1)S(1)}, bf16[1024,6]{0,1:T(8,128)(2,1)S(1)}, u32[]{:S(2)}, u32[]{:S(2)}) collective-permute-start(bf16[1024,6]{0,1:T(8,128)(2,1)S(1)} %pad_maximum_fusion), channel_id=1, source_target_pairs={{0,4},{4,8},{8,12},{12,16},{16,20},{20,24},{24,28},{1,5},{5,9},{9,... | collective-permute-start | bytes 36872 | tf_op jit(solution)/shard_map/ppermute | solution.py:536
  21.4 72.7 %collective-permute-start.1 = (bf16[1024,1024]{1,0:T(8,128)(2,1)S(1)}, bf16[1024,1024]{1,0:T(8,128)(2,1)S(1)}, u32[]{:S(2)}, u32[]{:S(2)}) collective-permute-start(bf16[1024,1024]{1,0:T(8,128)(2,1)S(1)} %get-tuple-element.71), channel_id=1, source_target_pairs={{0,1},{1,0},{2,3},{3,2},{4,5},{5,4},{6,7},{7,6},{8,9},{9,8},{10,11... | collective-permute-start | bytes 6291464 | tf_op jit(solution)/shard_map/ppermute | solution.py:540
  21.7 72.4 %collective-permute-start.2 = (bf16[1024,1024]{1,0:T(8,128)(2,1)S(1)}, bf16[1024,1024]{1,0:T(8,128)(2,1)S(1)}, u32[]{:S(2)}, u32[]{:S(2)}) collective-permute-start(bf16[1024,1024]{1,0:T(8,128)(2,1)S(1)} %get-tuple-element.72), channel_id=1, source_target_pairs={{0,2},{1,3},{2,0},{3,1},{4,6},{5,7},{6,4},{7,5},{8,10},{9,11},{10,... | collective-permute-start | bytes 6291464 | tf_op jit(solution)/shard_map/ppermute | solution.py:540
  26.0 5.6 %collective-permute-start.3 = (bf16[8,64,128]{2,1,0:T(8,128)(2,1)S(1)}, bf16[8,64,128]{2,1,0:T(8,128)(2,1)S(1)}, u32[]{:S(2)}, u32[]{:S(2)}) collective-permute-start(bf16[8,64,128]{2,1,0:T(8,128)(2,1)S(1)} %get-tuple-element.74), channel_id=1, source_target_pairs={{0,4},{4,8},{8,12},{12,16},{16,20},{20,24},{24,28},{28,0},{1,5},{5... | collective-permute-start | bytes 393224 | tf_op jit(solution)/shard_map/ppermute | solution.py:531
  28.9 6.4 %collective-permute-start.4 = (bf16[8,64,128]{2,1,0:T(8,128)(2,1)S(1)}, bf16[8,64,128]{2,1,0:T(8,128)(2,1)S(1)}, u32[]{:S(2)}, u32[]{:S(2)}) collective-permute-start(bf16[8,64,128]{2,1,0:T(8,128)(2,1)S(1)} %get-tuple-element.75), channel_id=1, source_target_pairs={{0,8},{4,12},{8,16},{12,20},{16,24},{20,28},{24,0},{28,4},{1,9},{5... | collective-permute-start | bytes 393224 | tf_op jit(solution)/shard_map/ppermute | solution.py:531
  30.2 15.4 %collective-permute-start.5 = (bf16[8,64,128]{2,1,0:T(8,128)(2,1)S(1)}, bf16[8,64,128]{2,1,0:T(8,128)(2,1)S(1)}, u32[]{:S(2)}, u32[]{:S(2)}) collective-permute-start(bf16[8,64,128]{2,1,0:T(8,128)(2,1)S(1)} %get-tuple-element.76), channel_id=1, source_target_pairs={{0,12},{4,16},{8,20},{12,24},{16,28},{20,0},{24,4},{28,8},{1,13},{... | collective-permute-start | bytes 393224 | tf_op jit(solution)/shard_map/ppermute | solution.py:531
  31.6 16.9 %collective-permute-start.6 = (bf16[8,64,128]{2,1,0:T(8,128)(2,1)S(1)}, bf16[8,64,128]{2,1,0:T(8,128)(2,1)S(1)}, u32[]{:S(2)}, u32[]{:S(2)}) collective-permute-start(bf16[8,64,128]{2,1,0:T(8,128)(2,1)S(1)} %get-tuple-element.77), channel_id=1, source_target_pairs={{0,16},{4,20},{8,24},{12,28},{16,0},{20,4},{24,8},{28,12},{1,17},{... | collective-permute-start | bytes 393224 | tf_op jit(solution)/shard_map/ppermute | solution.py:531
  35.3 19.9 %collective-permute-start.7 = (bf16[8,64,128]{2,1,0:T(8,128)(2,1)S(1)}, bf16[8,64,128]{2,1,0:T(8,128)(2,1)S(1)}, u32[]{:S(2)}, u32[]{:S(2)}) collective-permute-start(bf16[8,64,128]{2,1,0:T(8,128)(2,1)S(1)} %get-tuple-element.78), channel_id=1, source_target_pairs={{0,20},{4,24},{8,28},{12,0},{16,4},{20,8},{24,12},{28,16},{1,21},{... | collective-permute-start | bytes 393224 | tf_op jit(solution)/shard_map/ppermute | solution.py:531
  45.6 9.6 %collective-permute-start.8 = (bf16[8,64,128]{2,1,0:T(8,128)(2,1)S(1)}, bf16[8,64,128]{2,1,0:T(8,128)(2,1)S(1)}, u32[]{:S(2)}, u32[]{:S(2)}) collective-permute-start(bf16[8,64,128]{2,1,0:T(8,128)(2,1)S(1)} %get-tuple-element.79), channel_id=1, source_target_pairs={{0,24},{4,28},{8,0},{12,4},{16,8},{20,12},{24,16},{28,20},{1,25},{... | collective-permute-start | bytes 393224 | tf_op jit(solution)/shard_map/ppermute | solution.py:531
  48.4 6.8 %collective-permute-start.9 = (bf16[8,64,128]{2,1,0:T(8,128)(2,1)S(1)}, bf16[8,64,128]{2,1,0:T(8,128)(2,1)S(1)}, u32[]{:S(2)}, u32[]{:S(2)}) collective-permute-start(bf16[8,64,128]{2,1,0:T(8,128)(2,1)S(1)} %get-tuple-element.80), channel_id=1, source_target_pairs={{0,28},{4,0},{8,4},{12,8},{16,12},{20,16},{24,20},{28,24},{1,29},{... | collective-permute-start | bytes 393224 | tf_op jit(solution)/shard_map/ppermute | solution.py:531
  62.8 6.7 %collective-permute-start.10 = (bf16[8,64,128]{2,1,0:T(8,128)(2,1)S(1)}, bf16[8,64,128]{2,1,0:T(8,128)(2,1)S(1)}, u32[]{:S(2)}, u32[]{:S(2)}) collective-permute-start(bf16[8,64,128]{2,1,0:T(8,128)(2,1)S(1)} %get-tuple-element.82), channel_id=1, source_target_pairs={{0,4},{4,8},{8,12},{12,16},{16,20},{20,24},{24,28},{28,0},{1,5},{5... | collective-permute-start | bytes 393224 | tf_op jit(solution)/shard_map/ppermute | solution.py:531
  64.6 7.3 %collective-permute-start.11 = (bf16[8,64,128]{2,1,0:T(8,128)(2,1)S(1)}, bf16[8,64,128]{2,1,0:T(8,128)(2,1)S(1)}, u32[]{:S(2)}, u32[]{:S(2)}) collective-permute-start(bf16[8,64,128]{2,1,0:T(8,128)(2,1)S(1)} %get-tuple-element.83), channel_id=1, source_target_pairs={{0,8},{4,12},{8,16},{12,20},{16,24},{20,28},{24,0},{28,4},{1,9},{5... | collective-permute-start | bytes 393224 | tf_op jit(solution)/shard_map/ppermute | solution.py:531
  65.0 10.4 %collective-permute-start.12 = (bf16[8,64,128]{2,1,0:T(8,128)(2,1)S(1)}, bf16[8,64,128]{2,1,0:T(8,128)(2,1)S(1)}, u32[]{:S(2)}, u32[]{:S(2)}) collective-permute-start(bf16[8,64,128]{2,1,0:T(8,128)(2,1)S(1)} %get-tuple-element.84), channel_id=1, source_target_pairs={{0,12},{4,16},{8,20},{12,24},{16,28},{20,0},{24,4},{28,8},{1,13},{... | collective-permute-start | bytes 393224 | tf_op jit(solution)/shard_map/ppermute | solution.py:531
  69.5 13.6 %collective-permute-start.13 = (bf16[8,64,128]{2,1,0:T(8,128)(2,1)S(1)}, bf16[8,64,128]{2,1,0:T(8,128)(2,1)S(1)}, u32[]{:S(2)}, u32[]{:S(2)}) collective-permute-start(bf16[8,64,128]{2,1,0:T(8,128)(2,1)S(1)} %get-tuple-element.85), channel_id=1, source_target_pairs={{0,16},{4,20},{8,24},{12,28},{16,0},{20,4},{24,8},{28,12},{1,17},{... | collective-permute-start | bytes 393224 | tf_op jit(solution)/shard_map/ppermute | solution.py:531
  71.9 18.0 %collective-permute-start.14 = (bf16[8,64,128]{2,1,0:T(8,128)(2,1)S(1)}, bf16[8,64,128]{2,1,0:T(8,128)(2,1)S(1)}, u32[]{:S(2)}, u32[]{:S(2)}) collective-permute-start(bf16[8,64,128]{2,1,0:T(8,128)(2,1)S(1)} %get-tuple-element.86), channel_id=1, source_target_pairs={{0,20},{4,24},{8,28},{12,0},{16,4},{20,8},{24,12},{28,16},{1,21},{... | collective-permute-start | bytes 393224 | tf_op jit(solution)/shard_map/ppermute | solution.py:531
  75.4 17.1 %collective-permute-start.15 = (bf16[8,64,128]{2,1,0:T(8,128)(2,1)S(1)}, bf16[8,64,128]{2,1,0:T(8,128)(2,1)S(1)}, u32[]{:S(2)}, u32[]{:S(2)}) collective-permute-start(bf16[8,64,128]{2,1,0:T(8,128)(2,1)S(1)} %get-tuple-element.87), channel_id=1, source_target_pairs={{0,24},{4,28},{8,0},{12,4},{16,8},{20,12},{24,16},{28,20},{1,25},{... | collective-permute-start | bytes 393224 | tf_op jit(solution)/shard_map/ppermute | solution.py:531
  83.1 9.5 %collective-permute-start.16 = (bf16[8,64,128]{2,1,0:T(8,128)(2,1)S(1)}, bf16[8,64,128]{2,1,0:T(8,128)(2,1)S(1)}, u32[]{:S(2)}, u32[]{:S(2)}) collective-permute-start(bf16[8,64,128]{2,1,0:T(8,128)(2,1)S(1)} %get-tuple-element.88), channel_id=1, source_target_pairs={{0,28},{4,0},{8,4},{12,8},{16,12},{20,16},{24,20},{28,24},{1,29},{... | collective-permute-start | bytes 393224 | tf_op jit(solution)/shard_map/ppermute | solution.py:531
  94.1 82.2 %collective-permute-start.35 = (bf16[1024,1024]{1,0:T(8,128)(2,1)S(1)}, bf16[1024,1024]{1,0:T(8,128)(2,1)S(1)}, u32[]{:S(2)}, u32[]{:S(2)}) collective-permute-start(bf16[1024,1024]{1,0:T(8,128)(2,1)S(1)} %collective-permute-done.1.refs_10_), channel_id=1, source_target_pairs={{0,4},{4,0},{8,12},{12,8},{16,20},{20,16},{24,28},{28,24},{1,5},{5... | collective-permute-start | bytes 6291464 | tf_op jit(solution)/shard_map/ppermute | solution.py:540
  94.2 82.2 %collective-permute-start.36 = (bf16[1024,1024]{1,0:T(8,128)(2,1)S(1)}, bf16[1024,1024]{1,0:T(8,128)(2,1)S(1)}, u32[]{:S(2)}, u32[]{:S(2)}) collective-permute-start(bf16[1024,1024]{1,0:T(8,128)(2,1)S(1)} %collective-permute-done.2.refs_12_), channel_id=1, source_target_pairs={{0,4},{4,0},{8,12},{12,8},{16,20},{20,16},{24,28},{28,24},{1,5},{5... | collective-permute-start | bytes 6291464 | tf_op jit(solution)/shard_map/ppermute | solution.py:540
  94.7 6.8 %collective-permute-start.19 = (bf16[8,64,128]{2,1,0:T(8,128)(2,1)S(1)}, bf16[8,64,128]{2,1,0:T(8,128)(2,1)S(1)}, u32[]{:S(2)}, u32[]{:S(2)}) collective-permute-start(bf16[8,64,128]{2,1,0:T(8,128)(2,1)S(1)} %get-tuple-element.93), channel_id=1, source_target_pairs={{0,4},{4,8},{8,12},{12,16},{16,20},{20,24},{24,28},{28,0},{1,5},{5... | collective-permute-start | bytes 393224 | tf_op jit(solution)/shard_map/ppermute | solution.py:531
  94.7 7.0 %collective-permute-start.20 = (bf16[8,64,128]{2,1,0:T(8,128)(2,1)S(1)}, bf16[8,64,128]{2,1,0:T(8,128)(2,1)S(1)}, u32[]{:S(2)}, u32[]{:S(2)}) collective-permute-start(bf16[8,64,128]{2,1,0:T(8,128)(2,1)S(1)} %get-tuple-element.94), channel_id=1, source_target_pairs={{0,8},{4,12},{8,16},{12,20},{16,24},{20,28},{24,0},{28,4},{1,9},{5... | collective-permute-start | bytes 393224 | tf_op jit(solution)/shard_map/ppermute | solution.py:531
  94.8 16.2 %collective-permute-start.21 = (bf16[8,64,128]{2,1,0:T(8,128)(2,1)S(1)}, bf16[8,64,128]{2,1,0:T(8,128)(2,1)S(1)}, u32[]{:S(2)}, u32[]{:S(2)}) collective-permute-start(bf16[8,64,128]{2,1,0:T(8,128)(2,1)S(1)} %get-tuple-element.95), channel_id=1, source_target_pairs={{0,12},{4,16},{8,20},{12,24},{16,28},{20,0},{24,4},{28,8},{1,13},{... | collective-permute-start | bytes 393224 | tf_op jit(solution)/shard_map/ppermute | solution.py:531
  101.5 12.4 %collective-permute-start.22 = (bf16[8,64,128]{2,1,0:T(8,128)(2,1)S(1)}, bf16[8,64,128]{2,1,0:T(8,128)(2,1)S(1)}, u32[]{:S(2)}, u32[]{:S(2)}) collective-permute-start(bf16[8,64,128]{2,1,0:T(8,128)(2,1)S(1)} %get-tuple-element.96), channel_id=1, source_target_pairs={{0,16},{4,20},{8,24},{12,28},{16,0},{20,4},{24,8},{28,12},{1,17},{... | collective-permute-start | bytes 393224 | tf_op jit(solution)/shard_map/ppermute | solution.py:531
  101.7 12.3 %collective-permute-start.23 = (bf16[8,64,128]{2,1,0:T(8,128)(2,1)S(1)}, bf16[8,64,128]{2,1,0:T(8,128)(2,1)S(1)}, u32[]{:S(2)}, u32[]{:S(2)}) collective-permute-start(bf16[8,64,128]{2,1,0:T(8,128)(2,1)S(1)} %get-tuple-element.97), channel_id=1, source_target_pairs={{0,20},{4,24},{8,28},{12,0},{16,4},{20,8},{24,12},{28,16},{1,21},{... | collective-permute-start | bytes 393224 | tf_op jit(solution)/shard_map/ppermute | solution.py:531
  111.0 8.9 %collective-permute-start.24 = (bf16[8,64,128]{2,1,0:T(8,128)(2,1)S(1)}, bf16[8,64,128]{2,1,0:T(8,128)(2,1)S(1)}, u32[]{:S(2)}, u32[]{:S(2)}) collective-permute-start(bf16[8,64,128]{2,1,0:T(8,128)(2,1)S(1)} %get-tuple-element.98), channel_id=1, source_target_pairs={{0,24},{4,28},{8,0},{12,4},{16,8},{20,12},{24,16},{28,20},{1,25},{... | collective-permute-start | bytes 393224 | tf_op jit(solution)/shard_map/ppermute | solution.py:531
  114.0 6.1 %collective-permute-start.25 = (bf16[8,64,128]{2,1,0:T(8,128)(2,1)S(1)}, bf16[8,64,128]{2,1,0:T(8,128)(2,1)S(1)}, u32[]{:S(2)}, u32[]{:S(2)}) collective-permute-start(bf16[8,64,128]{2,1,0:T(8,128)(2,1)S(1)} %get-tuple-element.99), channel_id=1, source_target_pairs={{0,28},{4,0},{8,4},{12,8},{16,12},{20,16},{24,20},{28,24},{1,29},{... | collective-permute-start | bytes 393224 | tf_op jit(solution)/shard_map/ppermute | solution.py:531
  129.4 6.3 %collective-permute-start.28 = (bf16[4,64,128]{2,1,0:T(8,128)(2,1)S(1)}, bf16[4,64,128]{2,1,0:T(8,128)(2,1)S(1)}, u32[]{:S(2)}, u32[]{:S(2)}) collective-permute-start(bf16[4,64,128]{2,1,0:T(8,128)(2,1)S(1)} %get-tuple-element.103), channel_id=1, source_target_pairs={{0,12},{4,16},{8,20},{12,24},{16,28},{20,0},{24,4},{28,8},{1,13},{... | collective-permute-start | bytes 196616 | tf_op jit(solution)/shard_map/ppermute | solution.py:531
  131.2 6.5 %collective-permute-start.29 = (bf16[4,64,128]{2,1,0:T(8,128)(2,1)S(1)}, bf16[4,64,128]{2,1,0:T(8,128)(2,1)S(1)}, u32[]{:S(2)}, u32[]{:S(2)}) collective-permute-start(bf16[4,64,128]{2,1,0:T(8,128)(2,1)S(1)} %get-tuple-element.104), channel_id=1, source_target_pairs={{0,16},{4,20},{8,24},{12,28},{16,0},{20,4},{24,8},{28,12},{1,17},{... | collective-permute-start | bytes 196616 | tf_op jit(solution)/shard_map/ppermute | solution.py:531
  132.1 9.8 %collective-permute-start.39 = (bf16[4,64,128]{2,1,0:T(8,128)(2,1)S(1)}, bf16[4,64,128]{2,1,0:T(8,128)(2,1)S(1)}, u32[]{:S(2)}, u32[]{:S(2)}) collective-permute-start(bf16[4,64,128]{2,1,0:T(8,128)(2,1)S(1)} %get-tuple-element.120), channel_id=1, source_target_pairs={{0,4},{4,8},{8,12},{12,16},{16,20},{20,24},{24,28},{28,0},{1,5},{5... | collective-permute-start | bytes 196616 | tf_op jit(solution)/shard_map/ppermute | solution.py:531
  135.7 6.2 %collective-permute-start.40 = (bf16[4,64,128]{2,1,0:T(8,128)(2,1)S(1)}, bf16[4,64,128]{2,1,0:T(8,128)(2,1)S(1)}, u32[]{:S(2)}, u32[]{:S(2)}) collective-permute-start(bf16[4,64,128]{2,1,0:T(8,128)(2,1)S(1)} %get-tuple-element.121), channel_id=1, source_target_pairs={{0,8},{4,12},{8,16},{12,20},{16,24},{20,28},{24,0},{28,4},{1,9},{5... | collective-permute-start | bytes 196616 | tf_op jit(solution)/shard_map/ppermute | solution.py:531
  137.6 8.0 %collective-permute-start.41 = (bf16[4,64,128]{2,1,0:T(8,128)(2,1)S(1)}, bf16[4,64,128]{2,1,0:T(8,128)(2,1)S(1)}, u32[]{:S(2)}, u32[]{:S(2)}) collective-permute-start(bf16[4,64,128]{2,1,0:T(8,128)(2,1)S(1)} %get-tuple-element.122), channel_id=1, source_target_pairs={{0,12},{4,16},{8,20},{12,24},{16,28},{20,0},{24,4},{28,8},{1,13},{... | collective-permute-start | bytes 196616 | tf_op jit(solution)/shard_map/ppermute | solution.py:531
  141.9 6.1 %collective-permute-start.42 = (bf16[4,64,128]{2,1,0:T(8,128)(2,1)S(1)}, bf16[4,64,128]{2,1,0:T(8,128)(2,1)S(1)}, u32[]{:S(2)}, u32[]{:S(2)}) collective-permute-start(bf16[4,64,128]{2,1,0:T(8,128)(2,1)S(1)} %get-tuple-element.123), channel_id=1, source_target_pairs={{0,16},{4,20},{8,24},{12,28},{16,0},{20,4},{24,8},{28,12},{1,17},{... | collective-permute-start | bytes 196616 | tf_op jit(solution)/shard_map/ppermute | solution.py:531
  141.9 6.4 %collective-permute-start.43 = (bf16[4,64,128]{2,1,0:T(8,128)(2,1)S(1)}, bf16[4,64,128]{2,1,0:T(8,128)(2,1)S(1)}, u32[]{:S(2)}, u32[]{:S(2)}) collective-permute-start(bf16[4,64,128]{2,1,0:T(8,128)(2,1)S(1)} %get-tuple-element.124), channel_id=1, source_target_pairs={{0,20},{4,24},{8,28},{12,0},{16,4},{20,8},{24,12},{28,16},{1,21},{... | collective-permute-start | bytes 196616 | tf_op jit(solution)/shard_map/ppermute | solution.py:531
  145.7 6.7 %collective-permute-start.44 = (bf16[4,64,128]{2,1,0:T(8,128)(2,1)S(1)}, bf16[4,64,128]{2,1,0:T(8,128)(2,1)S(1)}, u32[]{:S(2)}, u32[]{:S(2)}) collective-permute-start(bf16[4,64,128]{2,1,0:T(8,128)(2,1)S(1)} %get-tuple-element.125), channel_id=1, source_target_pairs={{0,24},{4,28},{8,0},{12,4},{16,8},{20,12},{24,16},{28,20},{1,25},{... | collective-permute-start | bytes 196616 | tf_op jit(solution)/shard_map/ppermute | solution.py:531
  148.0 4.4 %collective-permute-start.45 = (bf16[4,64,128]{2,1,0:T(8,128)(2,1)S(1)}, bf16[4,64,128]{2,1,0:T(8,128)(2,1)S(1)}, u32[]{:S(2)}, u32[]{:S(2)}) collective-permute-start(bf16[4,64,128]{2,1,0:T(8,128)(2,1)S(1)} %get-tuple-element.126), channel_id=1, source_target_pairs={{0,28},{4,0},{8,4},{12,8},{16,12},{20,16},{24,20},{28,24},{1,29},{... | collective-permute-start | bytes 196616 | tf_op jit(solution)/shard_map/ppermute | solution.py:531
  148.3 6.5 %collective-permute-start.30 = (bf16[4,64,128]{2,1,0:T(8,128)(2,1)S(1)}, bf16[4,64,128]{2,1,0:T(8,128)(2,1)S(1)}, u32[]{:S(2)}, u32[]{:S(2)}) collective-permute-start(bf16[4,64,128]{2,1,0:T(8,128)(2,1)S(1)} %get-tuple-element.105), channel_id=1, source_target_pairs={{0,20},{4,24},{8,28},{12,0},{16,4},{20,8},{24,12},{28,16},{1,21},{... | collective-permute-start | bytes 196616 | tf_op jit(solution)/shard_map/ppermute | solution.py:531
  152.4 5.1 %collective-permute-start.32 = (bf16[4,64,128]{2,1,0:T(8,128)(2,1)S(1)}, bf16[4,64,128]{2,1,0:T(8,128)(2,1)S(1)}, u32[]{:S(2)}, u32[]{:S(2)}) collective-permute-start(bf16[4,64,128]{2,1,0:T(8,128)(2,1)S(1)} %get-tuple-element.107), channel_id=1, source_target_pairs={{0,28},{4,0},{8,4},{12,8},{16,12},{20,16},{24,20},{28,24},{1,29},{... | collective-permute-start | bytes 196616 | tf_op jit(solution)/shard_map/ppermute | solution.py:531
  154.8 7.0 %collective-permute-start.46 = (bf16[512,256]{1,0:T(8,128)(2,1)S(1)}, bf16[512,256]{1,0:T(8,128)(2,1)S(1)}, u32[]{:S(2)}, u32[]{:S(2)}) collective-permute-start(bf16[512,256]{1,0:T(8,128)(2,1)S(1)} %get-tuple-element.127.refs_4_), channel_id=1, source_target_pairs={{0,1},{1,0},{2,3},{3,2},{4,5},{5,4},{6,7},{7,6},{8,9},{9,8},{10,11... | collective-permute-start | bytes 786440 | tf_op jit(solution)/shard_map/ppermute | solution.py:540
  156.2 20.2 %collective-permute-start.18 = (bf16[512,512]{1,0:T(8,128)(2,1)S(1)}, bf16[512,512]{1,0:T(8,128)(2,1)S(1)}, u32[]{:S(2)}, u32[]{:S(2)}) collective-permute-start(bf16[512,512]{1,0:T(8,128)(2,1)S(1)} %get-tuple-element.91.refs_1_), channel_id=1, source_target_pairs={{0,2},{1,3},{2,0},{3,1},{4,6},{5,7},{6,4},{7,5},{8,10},{9,11},{10,... | collective-permute-start | bytes 1572872 | tf_op jit(solution)/shard_map/ppermute | solution.py:540
  157.4 18.9 %collective-permute-start.17 = (bf16[512,512]{1,0:T(8,128)(2,1)S(1)}, bf16[512,512]{1,0:T(8,128)(2,1)S(1)}, u32[]{:S(2)}, u32[]{:S(2)}) collective-permute-start(bf16[512,512]{1,0:T(8,128)(2,1)S(1)} %get-tuple-element.90.refs_0_), channel_id=1, source_target_pairs={{0,1},{1,0},{2,3},{3,2},{4,5},{5,4},{6,7},{7,6},{8,9},{9,8},{10,11... | collective-permute-start | bytes 1572872 | tf_op jit(solution)/shard_map/ppermute | solution.py:540
  161.8 12.6 %collective-permute-start.47 = (bf16[512,256]{1,0:T(8,128)(2,1)S(1)}, bf16[512,256]{1,0:T(8,128)(2,1)S(1)}, u32[]{:S(2)}, u32[]{:S(2)}) collective-permute-start(bf16[512,256]{1,0:T(8,128)(2,1)S(1)} %get-tuple-element.128.refs_5_), channel_id=1, source_target_pairs={{0,2},{1,3},{2,0},{3,1},{4,6},{5,7},{6,4},{7,5},{8,10},{9,11},{10,... | collective-permute-start | bytes 786440 | tf_op jit(solution)/shard_map/ppermute | solution.py:540
  174.4 7.3 %collective-permute-start.33 = (bf16[512,256]{1,0:T(8,128)(2,1)S(1)}, bf16[512,256]{1,0:T(8,128)(2,1)S(1)}, u32[]{:S(2)}, u32[]{:S(2)}) collective-permute-start(bf16[512,256]{1,0:T(8,128)(2,1)S(1)} %get-tuple-element.108.refs_4_), channel_id=1, source_target_pairs={{0,1},{1,0},{2,3},{3,2},{4,5},{5,4},{6,7},{7,6},{8,9},{9,8},{10,11... | collective-permute-start | bytes 786440 | tf_op jit(solution)/shard_map/ppermute | solution.py:540
  180.2 26.7 %collective-permute-start.48 = (bf16[1024,256]{1,0:T(8,128)(2,1)S(1)}, bf16[1024,256]{1,0:T(8,128)(2,1)S(1)}, u32[]{:S(2)}, u32[]{:S(2)}) collective-permute-start(bf16[1024,256]{1,0:T(8,128)(2,1)S(1)} %get-tuple-element.130), channel_id=1, source_target_pairs={{0,2},{1,3},{2,0},{3,1},{4,6},{5,7},{6,4},{7,5},{8,10},{9,11},{10,... | collective-permute-start | bytes 1572872 | tf_op jit(solution)/shard_map/ppermute | solution.py:540
  181.5 25.5 %collective-permute-start.49 = (bf16[1024,256]{1,0:T(8,128)(2,1)S(1)}, bf16[1024,256]{1,0:T(8,128)(2,1)S(1)}, u32[]{:S(2)}, u32[]{:S(2)}) collective-permute-start(bf16[1024,256]{1,0:T(8,128)(2,1)S(1)} %get-tuple-element.132), channel_id=1, source_target_pairs={{0,1},{1,0},{2,3},{3,2},{4,5},{5,4},{6,7},{7,6},{8,9},{9,8},{10,11... | collective-permute-start | bytes 1572872 | tf_op jit(solution)/shard_map/ppermute | solution.py:540
  181.5 16.6 %collective-permute-start.34 = (bf16[512,256]{1,0:T(8,128)(2,1)S(1)}, bf16[512,256]{1,0:T(8,128)(2,1)S(1)}, u32[]{:S(2)}, u32[]{:S(2)}) collective-permute-start(bf16[512,256]{1,0:T(8,128)(2,1)S(1)} %get-tuple-element.109.refs_5_), channel_id=1, source_target_pairs={{0,2},{1,3},{2,0},{3,1},{4,6},{5,7},{6,4},{7,5},{8,10},{9,11},{10,... | collective-permute-start | bytes 786440 | tf_op jit(solution)/shard_map/ppermute | solution.py:540
  201.8 17.7 %collective-permute-start.37 = (bf16[1024,256]{1,0:T(8,128)(2,1)S(1)}, bf16[1024,256]{1,0:T(8,128)(2,1)S(1)}, u32[]{:S(2)}, u32[]{:S(2)}) collective-permute-start(bf16[1024,256]{1,0:T(8,128)(2,1)S(1)} %get-tuple-element.116), channel_id=1, source_target_pairs={{0,2},{1,3},{2,0},{3,1},{4,6},{5,7},{6,4},{7,5},{8,10},{9,11},{10,... | collective-permute-start | bytes 1572872 | tf_op jit(solution)/shard_map/ppermute | solution.py:540
  203.1 16.4 %collective-permute-start.38 = (bf16[1024,256]{1,0:T(8,128)(2,1)S(1)}, bf16[1024,256]{1,0:T(8,128)(2,1)S(1)}, u32[]{:S(2)}, u32[]{:S(2)}) collective-permute-start(bf16[1024,256]{1,0:T(8,128)(2,1)S(1)} %get-tuple-element.118), channel_id=1, source_target_pairs={{0,1},{1,0},{2,3},{3,2},{4,5},{5,4},{6,7},{7,6},{8,9},{9,8},{10,11... | collective-permute-start | bytes 1572872 | tf_op jit(solution)/shard_map/ppermute | solution.py:540
  209.3 10.3 %collective-permute-start.50 = (bf16[1024,128]{1,0:T(8,128)(2,1)S(1)}, bf16[1024,128]{1,0:T(8,128)(2,1)S(1)}, u32[]{:S(2)}, u32[]{:S(2)}) collective-permute-start(bf16[1024,128]{1,0:T(8,128)(2,1)S(1)} %get-tuple-element.133), channel_id=1, source_target_pairs={{0,4},{4,8},{8,12},{12,16},{16,20},{20,24},{24,28},{1,5},{5,9},{9,... | collective-permute-start | bytes 786440 | tf_op jit(solution)/shard_map/ppermute | solution.py:536
  (21 other events, 326.2 us)

commit v3 on v2

--- a/solution.py
+++ b/solution.py
@@ -88,6 +88,26 @@
     return taps[:, 0:1] * block + taps[:, 1:2] * back1 + taps[:, 2:3] * back2
 
 
+def tail_kernel(*refs):
+    *ins, out_ref = refs
+    rows = [ref[...].astype(F32).T[-2:] for ref in ins]
+    rows.append(jnp.zeros((out_ref.shape[0] - 2 * len(ins), out_ref.shape[1]), F32))
+    out_ref[...] = jnp.concatenate(rows, axis=0).astype(BF16)
+
+
+def tails(arrays):
+    channels, tokens = arrays[0].shape
+    last = pl.BlockSpec((channels, LANES), lambda i: (0, tokens // LANES - 1))
+    return pl.pallas_call(
+        tail_kernel,
+        out_shape=jax.ShapeDtypeStruct((8, channels), BF16),
+        grid=(1,),
+        in_specs=[last] * len(arrays),
+        out_specs=whole((8, channels)),
+        name="tails",
+    )(*arrays)
+
+
 def mix_kernel(ids_ref, key_ref, value_ref, aux_ref, *out_refs):
     aux = aux_ref[...]
     keys = short_conv(key_ref[...].astype(F32), aux[:, 11:13], aux[:, 3:6])
@@ -161,7 +181,7 @@
         out_ref[pl.ds(base, group)] = spectrum.reshape(group, n1, 2 * LANES)
         return carry
 
-    lax.fori_loop(0, block // group, body, 0)
+    lax.fori_loop(0, block // group, body, 0, unroll=2)
 
 
 def whole(shape):
@@ -238,7 +258,7 @@
                 ]
         return carry
 
-    lax.fori_loop(0, block // group, body, 0)
+    lax.fori_loop(0, block // group, body, 0, unroll=2)
     at = 0
     for out_ref in outs:
         size = math.prod(out_ref.shape[:-1])
@@ -570,10 +590,8 @@
     length = long_filter.shape[1]
     tables = long_tables(length, groups)
     ids = jnp.stack([lax.axis_index("ctx"), lax.axis_index("tp")]).astype(jnp.int32)
-    tails = [x[:, -2:] for x in (query_proj, key_proj, value_proj)]
-    edges = forward(jnp.concatenate(tails, axis=1), "ctx").astype(F32)
-    flat_taps = short_taps.reshape(9, channels).T
-    aux = jnp.concatenate([flat_taps, edges, jnp.zeros((channels, 1), F32)], axis=1)
+    edges = forward(tails((query_proj, key_proj, value_proj)), "ctx").astype(F32)
+    aux = jnp.concatenate([short_taps.reshape(9, channels), edges[:7]], axis=0).T
     owned = long_filter.shape[0]
     four = lax.axis_size("tp") == 4
     chunks = 2 if four and owned % 32 == 0 else 1

time: 225 us -> 222 us (0.987)
  local copies, waits for them, and re-layouts: 9.15 us -> 5.24 us
    slice x3 -> x0, local copies, waits for them, and re-layouts: 3.43 us -> none  [shards(): tails = [x[:, -2:] for x in (query_proj, key_proj, value_proj)]]
    unnamed x39 -> x36, local copies, waits for them, and re-layouts: 5.43 us -> 5.03 us
  transfers between devices with their start and end apart: 51 -> 51, of which waited for: 21 -> 21; matrix products, arithmetic and copies ran while one was open for 0% -> 0% of each run, Pallas kernels for 25% -> 24%
where the time goes in v3:
time: 222 us; the launch traced here: 220 us
  waiting for transfers between devices  77.5 us (35%)
  starting transfers between devices  70.1 us (32%)
  Pallas kernels  65.9 us (30%)
  local copies, waits for them, and re-layouts  5.24 us (2%)
    ppermute x35, waiting for transfers between devices, ring(): lax.ppermute(block, axis, [(i, (i + distance) % count) for i in range(cou...  50.9 us
    ppermute x35, starting transfers between devices, ring(): lax.ppermute(block, axis, [(i, (i + distance) % count) for i in range(cou...  49.1 us
    ppermute x14, waiting for transfers between devices, swapped(): lax.ppermute(block, axis, [(i, i ^ bit) for i in range(lax.axis_size(axis...  25.7 us
    pallas_call x4, Pallas kernels, project(): pl.pallas_call(functools.partial(project_kernel, slot, len(sources)), out...  15.1 us
    pallas_call x2, Pallas kernels, long_conv(): pl.pallas_call(functools.partial(conv_kernel, groups), out_shape=[jax.Sha...  14.2 us
    ppermute x14, starting transfers between devices, swapped(): lax.ppermute(block, axis, [(i, i ^ bit) for i in range(lax.axis_size(axis...  10.8 us
    ppermute x2, starting transfers between devices, forward(): return lax.ppermute(block, axis, [(i, i + 1) for i in range(count - 1)])  10.2 us
    pallas_call x2, Pallas kernels, mix(): pl.pallas_call(mix_kernel, out_shape=[jax.ShapeDtypeStruct((count, rows,...  7.97 us
  transfers between devices with their start and end apart: 51, of which 21 were waited for; matrix products, arithmetic and copies ran while one was open for 0% of the time, Pallas kernels for 24%

profile of v3, /device:TPU:15, one launch (start us, length us, event | category | flops | bytes accessed | tf_op | source)
XLA Modules:
  0.0 220.0 jit_solution(9512447266897561146)
XLA Ops:
  0.6 2.2 tails.1
  2.8 3.8 %collective-permute-start = (bf16[8,1024]{1,0:T(8,128)(2,1)}, bf16[8,1024]{1,0:T(8,128)(2,1)S(1)}, u32[]{:S(2)}, u32[]{:S(2)}) collective-permute-start(bf16[8,1024]{1,0:T(8,128)(2,1)} %tails.1), channel_id=1, source_target_pairs={{0,4},{4,8},{8,12},{12,16},{16,20},{20,24},{24,28},{1,5},{5,9},{9,... | collective-permute-start | bytes 49160 | tf_op jit(solution)/shard_map/ppermute | solution.py:556
  7.9 1.6 copy-done.2
  9.5 4.0 %mix.2 = (bf16[8,64,128]{2,1,0:T(8,128)(2,1)S(1)}, bf16[8,64,128]{2,1,0:T(8,128)(2,1)S(1)}, bf16[8,64,128]{2,1,0:T(8,128)(2,1)S(1)}, bf16[8,64,128]{2,1,0:T(8,12...) custom-call(s32[2]{0:T(128)S(1)} %pad_add_fusion.ids_ref, ...), custom_call_target="tpu_custom_call" | custom-call | tf_op jit(solution)/shard_map/mix/pallas_call | solution.py:131
  13.5 3.4 %copy-done = bf16[1024,4096]{1,0:T(8,128)(2,1)S(1)} copy-done((bf16[1024,4096]{1,0:T(8,128)(2,1)S(1)}, bf16[1024,4096]{1,0:T(8,128)(2,1)}, u32[]{:S(2)}) %copy-start) | copy-done | bytes 8388632
  16.8 2.9 %turn.2 = (bf16[1024,1024]{1,0:T(8,128)(2,1)S(1)}, bf16[1024,1024]{1,0:T(8,128)(2,1)S(1)}) custom-call(s32[2]{0:T(128)S(1)} %pad_add_fusion.ids_ref, bf16[1024,4096]{1,0:T(8,128)(2,1)S(1)} %copy-done), custom_call_target="tpu_custom_call" | custom-call | tf_op jit(solution)/shard_map/turn/pallas_call | solution.py:392
  20.4 4.0 %mix.3 = (bf16[8,64,128]{2,1,0:T(8,128)(2,1)S(1)}, bf16[8,64,128]{2,1,0:T(8,128)(2,1)S(1)}, bf16[8,64,128]{2,1,0:T(8,128)(2,1)S(1)}, bf16[8,64,128]{2,1,0:T(8,12...) custom-call(s32[2]{0:T(128)S(1)} %pad_add_fusion.ids_ref, ...), custom_call_target="tpu_custom_call" | custom-call | tf_op jit(solution)/shard_map/mix/pallas_call | solution.py:131
  24.4 2.9 %collective-permute-start.3 = (bf16[8,64,128]{2,1,0:T(8,128)(2,1)S(1)}, bf16[8,64,128]{2,1,0:T(8,128)(2,1)S(1)}, u32[]{:S(2)}, u32[]{:S(2)}) collective-permute-start(bf16[8,64,128]{2,1,0:T(8,128)(2,1)S(1)} %get-tuple-element.74), channel_id=1, source_target_pairs={{0,4},{4,8},{8,12},{12,16},{16,20},{20,24},{24,28},{28,0},{1,5},{5... | collective-permute-start | bytes 393224 | tf_op jit(solution)/shard_map/ppermute | solution.py:551
  30.0 3.7 %collective-permute-done.4.refs_2_ = bf16[8,64,128]{2,1,0:T(8,128)(2,1)S(1)} collective-permute-done((bf16[8,64,128]{2,1,0:T(8,128)(2,1)S(1)}, bf16[8,64,128]{2,1,0:T(8,128)(2,1)S(1)}, u32[]{:S(2)}, u32[]{:S(2)}) %collective-permute-start.4) | collective-permute-done | bytes 131104 | tf_op jit(solution)/shard_map/ppermute | solution.py:551
  33.9 10.1 %collective-permute-done.5.refs_3_ = bf16[8,64,128]{2,1,0:T(8,128)(2,1)S(1)} collective-permute-done((bf16[8,64,128]{2,1,0:T(8,128)(2,1)S(1)}, bf16[8,64,128]{2,1,0:T(8,128)(2,1)S(1)}, u32[]{:S(2)}, u32[]{:S(2)}) %collective-permute-start.5) | collective-permute-done | bytes 131104 | tf_op jit(solution)/shard_map/ppermute | solution.py:551
  44.0 2.8 %collective-permute-done.6.refs_4_ = bf16[8,64,128]{2,1,0:T(8,128)(2,1)S(1)} collective-permute-done((bf16[8,64,128]{2,1,0:T(8,128)(2,1)S(1)}, bf16[8,64,128]{2,1,0:T(8,128)(2,1)S(1)}, u32[]{:S(2)}, u32[]{:S(2)}) %collective-permute-start.6) | collective-permute-done | bytes 131104 | tf_op jit(solution)/shard_map/ppermute | solution.py:551
  46.9 5.7 %spectra.1.refs_8_ = f32[128,64,256]{2,1,0:T(8,128)S(1)} custom-call(f32[128,8192]{1,0:T(8,128)S(1)} %copy-done.5, bf16[128,192]{1,0:T(8,128)(2,1)S(1)} %copy-done.14, f32[2,64,128]{2,1,0:T(8,128)S(1)} %copy-done.10, bf16[256,256]{1,0:T(8,128)(2,1)S(1)} %copy-done.6), custom_call_target="tpu_custom_call" | custom-call | tf_op jit(solution)/shard_map/spectra/pallas_call | solution.py:195
  52.7 7.0 %conv.2 = (bf16[8,64,128]{2,1,0:T(8,128)(2,1)S(1)}, bf16[8,64,128]{2,1,0:T(8,128)(2,1)S(1)}, bf16[8,64,128]{2,1,0:T(8,128)(2,1)S(1)}, bf16[8,64,128]{2,1,0:T(8,1...) custom-call(s32[2]{0:T(128)S(1)} %pad_add_fusion.ids_ref, ...), custom_call_target="tpu_custom_call" | custom-call | tf_op jit(solution)/shard_map/conv/pallas_call | solution.py:277
  59.7 1.8 collective-permute-start.10
  61.9 4.5 %collective-permute-start.12 = (bf16[8,64,128]{2,1,0:T(8,128)(2,1)S(1)}, bf16[8,64,128]{2,1,0:T(8,128)(2,1)S(1)}, u32[]{:S(2)}, u32[]{:S(2)}) collective-permute-start(bf16[8,64,128]{2,1,0:T(8,128)(2,1)S(1)} %get-tuple-element.84), channel_id=1, source_target_pairs={{0,12},{4,16},{8,20},{12,24},{16,28},{20,0},{24,4},{28,8},{1,13},{... | collective-permute-start | bytes 393224 | tf_op jit(solution)/shard_map/ppermute | solution.py:551
  66.4 2.3 %collective-permute-start.13 = (bf16[8,64,128]{2,1,0:T(8,128)(2,1)S(1)}, bf16[8,64,128]{2,1,0:T(8,128)(2,1)S(1)}, u32[]{:S(2)}, u32[]{:S(2)}) collective-permute-start(bf16[8,64,128]{2,1,0:T(8,128)(2,1)S(1)} %get-tuple-element.85), channel_id=1, source_target_pairs={{0,16},{4,20},{8,24},{12,28},{16,0},{20,4},{24,8},{28,12},{1,17},{... | collective-permute-start | bytes 393224 | tf_op jit(solution)/shard_map/ppermute | solution.py:551
  68.8 3.5 %collective-permute-start.14 = (bf16[8,64,128]{2,1,0:T(8,128)(2,1)S(1)}, bf16[8,64,128]{2,1,0:T(8,128)(2,1)S(1)}, u32[]{:S(2)}, u32[]{:S(2)}) collective-permute-start(bf16[8,64,128]{2,1,0:T(8,128)(2,1)S(1)} %get-tuple-element.86), channel_id=1, source_target_pairs={{0,20},{4,24},{8,28},{12,0},{16,4},{20,8},{24,12},{28,16},{1,21},{... | collective-permute-start | bytes 393224 | tf_op jit(solution)/shard_map/ppermute | solution.py:551
  72.3 2.2 %collective-permute-start.15 = (bf16[8,64,128]{2,1,0:T(8,128)(2,1)S(1)}, bf16[8,64,128]{2,1,0:T(8,128)(2,1)S(1)}, u32[]{:S(2)}, u32[]{:S(2)}) collective-permute-start(bf16[8,64,128]{2,1,0:T(8,128)(2,1)S(1)} %get-tuple-element.87), channel_id=1, source_target_pairs={{0,24},{4,28},{8,0},{12,4},{16,8},{20,12},{24,16},{28,20},{1,25},{... | collective-permute-start | bytes 393224 | tf_op jit(solution)/shard_map/ppermute | solution.py:551
  74.6 5.5 %collective-permute-done.13.refs_4_ = bf16[8,64,128]{2,1,0:T(8,128)(2,1)S(1)} collective-permute-done((bf16[8,64,128]{2,1,0:T(8,128)(2,1)S(1)}, bf16[8,64,128]{2,1,0:T(8,128)(2,1)S(1)}, u32[]{:S(2)}, u32[]{:S(2)}) %collective-permute-start.13) | collective-permute-done | bytes 131104 | tf_op jit(solution)/shard_map/ppermute | solution.py:551
  80.0 3.1 %collective-permute-start.16 = (bf16[8,64,128]{2,1,0:T(8,128)(2,1)S(1)}, bf16[8,64,128]{2,1,0:T(8,128)(2,1)S(1)}, u32[]{:S(2)}, u32[]{:S(2)}) collective-permute-start(bf16[8,64,128]{2,1,0:T(8,128)(2,1)S(1)} %get-tuple-element.88), channel_id=1, source_target_pairs={{0,28},{4,0},{8,4},{12,8},{16,12},{20,16},{24,20},{28,24},{1,29},{... | collective-permute-start | bytes 393224 | tf_op jit(solution)/shard_map/ppermute | solution.py:551
  83.1 3.6 %query.1.refs_8_ = f32[8,1024,128]{2,1,0:T(8,128)S(1)} custom-call(bf16[1024,1024]{1,0:T(8,128)(2,1)S(1)} %copy-done.4, f32[1024,16]{1,0:T(8,128)S(1)} %bitcast.7), custom_call_target="tpu_custom_call" | custom-call | tf_op jit(solution)/shard_map/query/pallas_call | solution.py:306
  86.8 2.6 %collective-permute-done.15.refs_6_ = bf16[8,64,128]{2,1,0:T(8,128)(2,1)S(1)} collective-permute-done((bf16[8,64,128]{2,1,0:T(8,128)(2,1)S(1)}, bf16[8,64,128]{2,1,0:T(8,128)(2,1)S(1)}, u32[]{:S(2)}, u32[]{:S(2)}) %collective-permute-start.15) | collective-permute-done | bytes 131104 | tf_op jit(solution)/shard_map/ppermute | solution.py:551
  91.7 2.5 %collective-permute-start.21 = (bf16[8,64,128]{2,1,0:T(8,128)(2,1)S(1)}, bf16[8,64,128]{2,1,0:T(8,128)(2,1)S(1)}, u32[]{:S(2)}, u32[]{:S(2)}) collective-permute-start(bf16[8,64,128]{2,1,0:T(8,128)(2,1)S(1)} %get-tuple-element.95), channel_id=1, source_target_pairs={{0,12},{4,16},{8,20},{12,24},{16,28},{20,0},{24,4},{28,8},{1,13},{... | collective-permute-start | bytes 393224 | tf_op jit(solution)/shard_map/ppermute | solution.py:551
  94.2 4.2 %collective-permute-done.19.refs_1_ = bf16[8,64,128]{2,1,0:T(8,128)(2,1)S(1)} collective-permute-done((bf16[8,64,128]{2,1,0:T(8,128)(2,1)S(1)}, bf16[8,64,128]{2,1,0:T(8,128)(2,1)S(1)}, u32[]{:S(2)}, u32[]{:S(2)}) %collective-permute-start.19) | collective-permute-done | bytes 131104 | tf_op jit(solution)/shard_map/ppermute | solution.py:551
  98.6 1.5 collective-permute-start.23
  100.1 7.8 %collective-permute-done.21.refs_3_ = bf16[8,64,128]{2,1,0:T(8,128)(2,1)S(1)} collective-permute-done((bf16[8,64,128]{2,1,0:T(8,128)(2,1)S(1)}, bf16[8,64,128]{2,1,0:T(8,128)(2,1)S(1)}, u32[]{:S(2)}, u32[]{:S(2)}) %collective-permute-start.21) | collective-permute-done | bytes 131104 | tf_op jit(solution)/shard_map/ppermute | solution.py:551
  108.0 2.9 %collective-permute-done.22.refs_4_ = bf16[8,64,128]{2,1,0:T(8,128)(2,1)S(1)} collective-permute-done((bf16[8,64,128]{2,1,0:T(8,128)(2,1)S(1)}, bf16[8,64,128]{2,1,0:T(8,128)(2,1)S(1)}, u32[]{:S(2)}, u32[]{:S(2)}) %collective-permute-start.22) | collective-permute-done | bytes 131104 | tf_op jit(solution)/shard_map/ppermute | solution.py:551
  110.9 6.0 %collective-permute-done.24.refs_6_ = bf16[8,64,128]{2,1,0:T(8,128)(2,1)S(1)} collective-permute-done((bf16[8,64,128]{2,1,0:T(8,128)(2,1)S(1)}, bf16[8,64,128]{2,1,0:T(8,128)(2,1)S(1)}, u32[]{:S(2)}, u32[]{:S(2)}) %collective-permute-start.24) | collective-permute-done | bytes 131104 | tf_op jit(solution)/shard_map/ppermute | solution.py:551
  117.0 7.2 %conv.3 = (bf16[4,64,128]{2,1,0:T(8,128)(2,1)S(1)}, bf16[4,64,128]{2,1,0:T(8,128)(2,1)S(1)}, bf16[4,64,128]{2,1,0:T(8,128)(2,1)S(1)}, bf16[4,64,128]{2,1,0:T(8,1...) custom-call(s32[2]{0:T(128)S(1)} %pad_add_fusion.ids_ref, ...), custom_call_target="tpu_custom_call" | custom-call | tf_op jit(solution)/shard_map/conv/pallas_call | solution.py:277
  125.8 1.8 collective-permute-start.28
  128.5 3.6 %collective-permute-start.39 = (bf16[4,64,128]{2,1,0:T(8,128)(2,1)S(1)}, bf16[4,64,128]{2,1,0:T(8,128)(2,1)S(1)}, u32[]{:S(2)}, u32[]{:S(2)}) collective-permute-start(bf16[4,64,128]{2,1,0:T(8,128)(2,1)S(1)} %get-tuple-element.120), channel_id=1, source_target_pairs={{0,4},{4,8},{8,12},{12,16},{16,20},{20,24},{24,28},{28,0},{1,5},{5... | collective-permute-start | bytes 196616 | tf_op jit(solution)/shard_map/ppermute | solution.py:551
  132.1 2.0 collective-permute-start.40
  134.1 4.2 %collective-permute-start.41 = (bf16[4,64,128]{2,1,0:T(8,128)(2,1)S(1)}, bf16[4,64,128]{2,1,0:T(8,128)(2,1)S(1)}, u32[]{:S(2)}, u32[]{:S(2)}) collective-permute-start(bf16[4,64,128]{2,1,0:T(8,128)(2,1)S(1)} %get-tuple-element.122), channel_id=1, source_target_pairs={{0,12},{4,16},{8,20},{12,24},{16,28},{20,0},{24,4},{28,8},{1,13},{... | collective-permute-start | bytes 196616 | tf_op jit(solution)/shard_map/ppermute | solution.py:551
  138.3 3.8 %collective-permute-start.43 = (bf16[4,64,128]{2,1,0:T(8,128)(2,1)S(1)}, bf16[4,64,128]{2,1,0:T(8,128)(2,1)S(1)}, u32[]{:S(2)}, u32[]{:S(2)}) collective-permute-start(bf16[4,64,128]{2,1,0:T(8,128)(2,1)S(1)} %get-tuple-element.124), channel_id=1, source_target_pairs={{0,20},{4,24},{8,28},{12,0},{16,4},{20,8},{24,12},{28,16},{1,21},{... | collective-permute-start | bytes 196616 | tf_op jit(solution)/shard_map/ppermute | solution.py:551
  142.2 2.2 collective-permute-done.42.refs_4_
  144.7 4.1 %collective-permute-start.30 = (bf16[4,64,128]{2,1,0:T(8,128)(2,1)S(1)}, bf16[4,64,128]{2,1,0:T(8,128)(2,1)S(1)}, u32[]{:S(2)}, u32[]{:S(2)}) collective-permute-start(bf16[4,64,128]{2,1,0:T(8,128)(2,1)S(1)} %get-tuple-element.105), channel_id=1, source_target_pairs={{0,20},{4,24},{8,28},{12,0},{16,4},{20,8},{24,12},{28,16},{1,21},{... | collective-permute-start | bytes 196616 | tf_op jit(solution)/shard_map/ppermute | solution.py:551
  155.1 3.2 %collective-permute-done.46.refs_6_ = bf16[512,256]{1,0:T(8,128)(2,1)S(1)} collective-permute-done((bf16[512,256]{1,0:T(8,128)(2,1)S(1)}, bf16[512,256]{1,0:T(8,128)(2,1)S(1)}, u32[]{:S(2)}, u32[]{:S(2)}) %collective-permute-start.46) | collective-permute-done | bytes 262176 | tf_op jit(solution)/shard_map/ppermute | solution.py:560
  159.5 4.2 %turn.3 = (bf16[1024,1024]{1,0:T(8,128)(2,1)S(1)}, bf16[1024,1024]{1,0:T(8,128)(2,1)S(1)}, bf16[1024,1024]{1,0:T(8,128)(2,1)S(1)}) custom-call(s32[2]{0:T(128)S(1)} %pad_add_fusion.ids_ref, bf16[1024,4096]{1,0:T(8,128)(2,1)S(1)} %bitcast.4), custom_call_target="tpu_custom_call" | custom-call | tf_op jit(solution)/shard_map/turn/pallas_call | solution.py:392
  164.8 6.1 %collective-permute-done.47.refs_7_ = bf16[512,256]{1,0:T(8,128)(2,1)S(1)} collective-permute-done((bf16[512,256]{1,0:T(8,128)(2,1)S(1)}, bf16[512,256]{1,0:T(8,128)(2,1)S(1)}, u32[]{:S(2)}, u32[]{:S(2)}) %collective-permute-start.47) | collective-permute-done | bytes 262176 | tf_op jit(solution)/shard_map/ppermute | solution.py:560
  170.9 1.9 collective-permute-start.33
  172.8 3.8 %project.7 = (bf16[1024,256]{1,0:T(8,128)(2,1)S(1)}, bf16[1024,256]{1,0:T(8,128)(2,1)S(1)}) custom-call(s32[2]{0:T(128)S(1)} %pad_add_fusion.ids_ref, bf16[512,512]{1,0:T(8,128)(2,1)S(1)} %get-tuple-element.90.refs_0_, bf16[512,512]{1,0:T(8,128)(2,1)S(1)} %get-tuple-element.91.refs_1_, bf16[512,512]{1,0:T(8,128)(2,1)S(1)} %collective-permute-done.17.refs_2_, ...), custom_call_target="tpu_custom_call" | custom-call | tf_op jit(solution)/shard_map/project/pallas_call | solution.py:446
  178.1 16.3 %collective-permute-done.34.refs_7_ = bf16[512,256]{1,0:T(8,128)(2,1)S(1)} collective-permute-done((bf16[512,256]{1,0:T(8,128)(2,1)S(1)}, bf16[512,256]{1,0:T(8,128)(2,1)S(1)}, u32[]{:S(2)}, u32[]{:S(2)}) %collective-permute-start.34) | collective-permute-done | bytes 262176 | tf_op jit(solution)/shard_map/ppermute | solution.py:560
  194.5 3.8 %project.5 = (bf16[1024,256]{1,0:T(8,128)(2,1)S(1)}, bf16[1024,256]{1,0:T(8,128)(2,1)S(1)}) custom-call(s32[2]{0:T(128)S(1)} %pad_add_fusion.ids_ref, bf16[512,512]{1,0:T(8,128)(2,1)S(1)} %get-tuple-element.90.refs_0_, bf16[512,512]{1,0:T(8,128)(2,1)S(1)} %get-tuple-element.91.refs_1_, bf16[512,512]{1,0:T(8,128)(2,1)S(1)} %collective-permute-done.17.refs_2_, ...), custom_call_target="tpu_custom_call" | custom-call | tf_op jit(solution)/shard_map/project/pallas_call | solution.py:446
  199.5 3.8 %project.6 = (bf16[1024,256]{1,0:T(8,128)(2,1)S(1)}, bf16[1024,256]{1,0:T(8,128)(2,1)S(1)}) custom-call(s32[2]{0:T(128)S(1)} %pad_add_fusion.ids_ref, bf16[512,512]{1,0:T(8,128)(2,1)S(1)} %get-tuple-element.90.refs_0_, bf16[512,512]{1,0:T(8,128)(2,1)S(1)} %get-tuple-element.91.refs_1_, bf16[512,512]{1,0:T(8,128)(2,1)S(1)} %collective-permute-done.17.refs_2_, ...), custom_call_target="tpu_custom_call" | custom-call | tf_op jit(solution)/shard_map/project/pallas_call | solution.py:446
  203.4 2.3 %shard_map.158 = (bf16[1024,512]{1,0:T(8,128)(2,1)S(1)}, bf16[1024,128]{1,0:T(8,128)(2,1)S(1)}, bf16[1024,384]{1,0:T(8,128)(2,1)S(1)}) custom-call(bf16[1024,256]{1,0:T(8,128)(2,1)S(1)} %get-tuple-element.129.refs_0_, bf16[1024,256]{1,0:T(8,128)(2,1)S(1)} %collective-permute-done.48.refs_1_, bf16[1024,256]{1,0:T(8,128)(2,1)S(1)} %get-tuple-element.131.refs_2_, ...), custom_call_target="tpu_custom_call" | custom-call | tf_op jit(solution)/shard_map/pallas_call | solution.py:535
  205.7 6.5 %collective-permute-start.50 = (bf16[1024,128]{1,0:T(8,128)(2,1)S(1)}, bf16[1024,128]{1,0:T(8,128)(2,1)S(1)}, u32[]{:S(2)}, u32[]{:S(2)}) collective-permute-start(bf16[1024,128]{1,0:T(8,128)(2,1)S(1)} %get-tuple-element.133), channel_id=1, source_target_pairs={{0,4},{4,8},{8,12},{12,16},{16,20},{20,24},{24,28},{1,5},{5,9},{9,... | collective-permute-start | bytes 786440 | tf_op jit(solution)/shard_map/ppermute | solution.py:556
  212.2 3.8 %project.4 = (bf16[1024,256]{1,0:T(8,128)(2,1)S(1)}, bf16[1024,256]{1,0:T(8,128)(2,1)S(1)}) custom-call(s32[2]{0:T(128)S(1)} %pad_add_fusion.ids_ref, bf16[512,512]{1,0:T(8,128)(2,1)S(1)} %get-tuple-element.90.refs_0_, bf16[512,512]{1,0:T(8,128)(2,1)S(1)} %get-tuple-element.91.refs_1_, bf16[512,512]{1,0:T(8,128)(2,1)S(1)} %collective-permute-done.17.refs_2_, ...), custom_call_target="tpu_custom_call" | custom-call | tf_op jit(solution)/shard_map/project/pallas_call | solution.py:446
  216.0 4.0 %shard_map.159 = (bf16[1024,1024]{1,0:T(8,128)(2,1)}, bf16[1024,1024]{1,0:T(8,128)(2,1)}) custom-call(bf16[1024,256]{1,0:T(8,128)(2,1)S(1)} %get-tuple-element.113.refs_0_, bf16[1024,256]{1,0:T(8,128)(2,1)S(1)} %collective-permute-done.37.refs_1_, bf16[1024,256]{1,0:T(8,128)(2,1)S(1)} %get-tuple-element.117.refs_2_, ...), custom_call_target="tpu_custom_call" | custom-call | tf_op jit(solution)/shard_map/pallas_call | solution.py:535
  (114 shorter events, 22.2 us)
Async XLA Ops:
  2.8 4.8 %collective-permute-start = (bf16[8,1024]{1,0:T(8,128)(2,1)}, bf16[8,1024]{1,0:T(8,128)(2,1)S(1)}, u32[]{:S(2)}, u32[]{:S(2)}) collective-permute-start(bf16[8,1024]{1,0:T(8,128)(2,1)} %tails.1), channel_id=1, source_target_pairs={{0,4},{4,8},{8,12},{12,16},{16,20},{20,24},{24,28},{1,5},{5,9},{9,... | collective-permute-start | bytes 49160 | tf_op jit(solution)/shard_map/ppermute | solution.py:556
  19.8 71.2 %collective-permute-start.1 = (bf16[1024,1024]{1,0:T(8,128)(2,1)S(1)}, bf16[1024,1024]{1,0:T(8,128)(2,1)S(1)}, u32[]{:S(2)}, u32[]{:S(2)}) collective-permute-start(bf16[1024,1024]{1,0:T(8,128)(2,1)S(1)} %get-tuple-element.71), channel_id=1, source_target_pairs={{0,1},{1,0},{2,3},{3,2},{4,5},{5,4},{6,7},{7,6},{8,9},{9,8},{10,11... | collective-permute-start | bytes 6291464 | tf_op jit(solution)/shard_map/ppermute | solution.py:560
  20.1 70.9 %collective-permute-start.2 = (bf16[1024,1024]{1,0:T(8,128)(2,1)S(1)}, bf16[1024,1024]{1,0:T(8,128)(2,1)S(1)}, u32[]{:S(2)}, u32[]{:S(2)}) collective-permute-start(bf16[1024,1024]{1,0:T(8,128)(2,1)S(1)} %get-tuple-element.72), channel_id=1, source_target_pairs={{0,2},{1,3},{2,0},{3,1},{4,6},{5,7},{6,4},{7,5},{8,10},{9,11},{10,... | collective-permute-start | bytes 6291464 | tf_op jit(solution)/shard_map/ppermute | solution.py:560
  24.4 5.6 %collective-permute-start.3 = (bf16[8,64,128]{2,1,0:T(8,128)(2,1)S(1)}, bf16[8,64,128]{2,1,0:T(8,128)(2,1)S(1)}, u32[]{:S(2)}, u32[]{:S(2)}) collective-permute-start(bf16[8,64,128]{2,1,0:T(8,128)(2,1)S(1)} %get-tuple-element.74), channel_id=1, source_target_pairs={{0,4},{4,8},{8,12},{12,16},{16,20},{20,24},{24,28},{28,0},{1,5},{5... | collective-permute-start | bytes 393224 | tf_op jit(solution)/shard_map/ppermute | solution.py:551
  27.3 6.4 %collective-permute-start.4 = (bf16[8,64,128]{2,1,0:T(8,128)(2,1)S(1)}, bf16[8,64,128]{2,1,0:T(8,128)(2,1)S(1)}, u32[]{:S(2)}, u32[]{:S(2)}) collective-permute-start(bf16[8,64,128]{2,1,0:T(8,128)(2,1)S(1)} %get-tuple-element.75), channel_id=1, source_target_pairs={{0,8},{4,12},{8,16},{12,20},{16,24},{20,28},{24,0},{28,4},{1,9},{5... | collective-permute-start | bytes 393224 | tf_op jit(solution)/shard_map/ppermute | solution.py:551
  28.6 15.4 %collective-permute-start.5 = (bf16[8,64,128]{2,1,0:T(8,128)(2,1)S(1)}, bf16[8,64,128]{2,1,0:T(8,128)(2,1)S(1)}, u32[]{:S(2)}, u32[]{:S(2)}) collective-permute-start(bf16[8,64,128]{2,1,0:T(8,128)(2,1)S(1)} %get-tuple-element.76), channel_id=1, source_target_pairs={{0,12},{4,16},{8,20},{12,24},{16,28},{20,0},{24,4},{28,8},{1,13},{... | collective-permute-start | bytes 393224 | tf_op jit(solution)/shard_map/ppermute | solution.py:551
  30.0 16.9 %collective-permute-start.6 = (bf16[8,64,128]{2,1,0:T(8,128)(2,1)S(1)}, bf16[8,64,128]{2,1,0:T(8,128)(2,1)S(1)}, u32[]{:S(2)}, u32[]{:S(2)}) collective-permute-start(bf16[8,64,128]{2,1,0:T(8,128)(2,1)S(1)} %get-tuple-element.77), channel_id=1, source_target_pairs={{0,16},{4,20},{8,24},{12,28},{16,0},{20,4},{24,8},{28,12},{1,17},{... | collective-permute-start | bytes 393224 | tf_op jit(solution)/shard_map/ppermute | solution.py:551
  33.7 18.9 %collective-permute-start.7 = (bf16[8,64,128]{2,1,0:T(8,128)(2,1)S(1)}, bf16[8,64,128]{2,1,0:T(8,128)(2,1)S(1)}, u32[]{:S(2)}, u32[]{:S(2)}) collective-permute-start(bf16[8,64,128]{2,1,0:T(8,128)(2,1)S(1)} %get-tuple-element.78), channel_id=1, source_target_pairs={{0,20},{4,24},{8,28},{12,0},{16,4},{20,8},{24,12},{28,16},{1,21},{... | collective-permute-start | bytes 393224 | tf_op jit(solution)/shard_map/ppermute | solution.py:551
  44.0 8.6 %collective-permute-start.8 = (bf16[8,64,128]{2,1,0:T(8,128)(2,1)S(1)}, bf16[8,64,128]{2,1,0:T(8,128)(2,1)S(1)}, u32[]{:S(2)}, u32[]{:S(2)}) collective-permute-start(bf16[8,64,128]{2,1,0:T(8,128)(2,1)S(1)} %get-tuple-element.79), channel_id=1, source_target_pairs={{0,24},{4,28},{8,0},{12,4},{16,8},{20,12},{24,16},{28,20},{1,25},{... | collective-permute-start | bytes 393224 | tf_op jit(solution)/shard_map/ppermute | solution.py:551
  46.9 5.8 %collective-permute-start.9 = (bf16[8,64,128]{2,1,0:T(8,128)(2,1)S(1)}, bf16[8,64,128]{2,1,0:T(8,128)(2,1)S(1)}, u32[]{:S(2)}, u32[]{:S(2)}) collective-permute-start(bf16[8,64,128]{2,1,0:T(8,128)(2,1)S(1)} %get-tuple-element.80), channel_id=1, source_target_pairs={{0,28},{4,0},{8,4},{12,8},{16,12},{20,16},{24,20},{28,24},{1,29},{... | collective-permute-start | bytes 393224 | tf_op jit(solution)/shard_map/ppermute | solution.py:551
  59.7 6.7 %collective-permute-start.10 = (bf16[8,64,128]{2,1,0:T(8,128)(2,1)S(1)}, bf16[8,64,128]{2,1,0:T(8,128)(2,1)S(1)}, u32[]{:S(2)}, u32[]{:S(2)}) collective-permute-start(bf16[8,64,128]{2,1,0:T(8,128)(2,1)S(1)} %get-tuple-element.82), channel_id=1, source_target_pairs={{0,4},{4,8},{8,12},{12,16},{16,20},{20,24},{24,28},{28,0},{1,5},{5... | collective-permute-start | bytes 393224 | tf_op jit(solution)/shard_map/ppermute | solution.py:551
  61.5 7.3 %collective-permute-start.11 = (bf16[8,64,128]{2,1,0:T(8,128)(2,1)S(1)}, bf16[8,64,128]{2,1,0:T(8,128)(2,1)S(1)}, u32[]{:S(2)}, u32[]{:S(2)}) collective-permute-start(bf16[8,64,128]{2,1,0:T(8,128)(2,1)S(1)} %get-tuple-element.83), channel_id=1, source_target_pairs={{0,8},{4,12},{8,16},{12,20},{16,24},{20,28},{24,0},{28,4},{1,9},{5... | collective-permute-start | bytes 393224 | tf_op jit(solution)/shard_map/ppermute | solution.py:551
  61.9 10.4 %collective-permute-start.12 = (bf16[8,64,128]{2,1,0:T(8,128)(2,1)S(1)}, bf16[8,64,128]{2,1,0:T(8,128)(2,1)S(1)}, u32[]{:S(2)}, u32[]{:S(2)}) collective-permute-start(bf16[8,64,128]{2,1,0:T(8,128)(2,1)S(1)} %get-tuple-element.84), channel_id=1, source_target_pairs={{0,12},{4,16},{8,20},{12,24},{16,28},{20,0},{24,4},{28,8},{1,13},{... | collective-permute-start | bytes 393224 | tf_op jit(solution)/shard_map/ppermute | solution.py:551
  66.4 13.6 %collective-permute-start.13 = (bf16[8,64,128]{2,1,0:T(8,128)(2,1)S(1)}, bf16[8,64,128]{2,1,0:T(8,128)(2,1)S(1)}, u32[]{:S(2)}, u32[]{:S(2)}) collective-permute-start(bf16[8,64,128]{2,1,0:T(8,128)(2,1)S(1)} %get-tuple-element.85), channel_id=1, source_target_pairs={{0,16},{4,20},{8,24},{12,28},{16,0},{20,4},{24,8},{28,12},{1,17},{... | collective-permute-start | bytes 393224 | tf_op jit(solution)/shard_map/ppermute | solution.py:551
  68.8 18.0 %collective-permute-start.14 = (bf16[8,64,128]{2,1,0:T(8,128)(2,1)S(1)}, bf16[8,64,128]{2,1,0:T(8,128)(2,1)S(1)}, u32[]{:S(2)}, u32[]{:S(2)}) collective-permute-start(bf16[8,64,128]{2,1,0:T(8,128)(2,1)S(1)} %get-tuple-element.86), channel_id=1, source_target_pairs={{0,20},{4,24},{8,28},{12,0},{16,4},{20,8},{24,12},{28,16},{1,21},{... | collective-permute-start | bytes 393224 | tf_op jit(solution)/shard_map/ppermute | solution.py:551
  72.3 17.1 %collective-permute-start.15 = (bf16[8,64,128]{2,1,0:T(8,128)(2,1)S(1)}, bf16[8,64,128]{2,1,0:T(8,128)(2,1)S(1)}, u32[]{:S(2)}, u32[]{:S(2)}) collective-permute-start(bf16[8,64,128]{2,1,0:T(8,128)(2,1)S(1)} %get-tuple-element.87), channel_id=1, source_target_pairs={{0,24},{4,28},{8,0},{12,4},{16,8},{20,12},{24,16},{28,20},{1,25},{... | collective-permute-start | bytes 393224 | tf_op jit(solution)/shard_map/ppermute | solution.py:551
  80.0 9.5 %collective-permute-start.16 = (bf16[8,64,128]{2,1,0:T(8,128)(2,1)S(1)}, bf16[8,64,128]{2,1,0:T(8,128)(2,1)S(1)}, u32[]{:S(2)}, u32[]{:S(2)}) collective-permute-start(bf16[8,64,128]{2,1,0:T(8,128)(2,1)S(1)} %get-tuple-element.88), channel_id=1, source_target_pairs={{0,28},{4,0},{8,4},{12,8},{16,12},{20,16},{24,20},{28,24},{1,29},{... | collective-permute-start | bytes 393224 | tf_op jit(solution)/shard_map/ppermute | solution.py:551
  91.1 81.7 %collective-permute-start.35 = (bf16[1024,1024]{1,0:T(8,128)(2,1)S(1)}, bf16[1024,1024]{1,0:T(8,128)(2,1)S(1)}, u32[]{:S(2)}, u32[]{:S(2)}) collective-permute-start(bf16[1024,1024]{1,0:T(8,128)(2,1)S(1)} %collective-permute-done.1.refs_10_), channel_id=1, source_target_pairs={{0,4},{4,0},{8,12},{12,8},{16,20},{20,16},{24,28},{28,24},{1,5},{5... | collective-permute-start | bytes 6291464 | tf_op jit(solution)/shard_map/ppermute | solution.py:560
  91.1 81.7 %collective-permute-start.36 = (bf16[1024,1024]{1,0:T(8,128)(2,1)S(1)}, bf16[1024,1024]{1,0:T(8,128)(2,1)S(1)}, u32[]{:S(2)}, u32[]{:S(2)}) collective-permute-start(bf16[1024,1024]{1,0:T(8,128)(2,1)S(1)} %collective-permute-done.2.refs_12_), channel_id=1, source_target_pairs={{0,4},{4,0},{8,12},{12,8},{16,20},{20,16},{24,28},{28,24},{1,5},{5... | collective-permute-start | bytes 6291464 | tf_op jit(solution)/shard_map/ppermute | solution.py:560
  91.6 6.8 %collective-permute-start.19 = (bf16[8,64,128]{2,1,0:T(8,128)(2,1)S(1)}, bf16[8,64,128]{2,1,0:T(8,128)(2,1)S(1)}, u32[]{:S(2)}, u32[]{:S(2)}) collective-permute-start(bf16[8,64,128]{2,1,0:T(8,128)(2,1)S(1)} %get-tuple-element.93), channel_id=1, source_target_pairs={{0,4},{4,8},{8,12},{12,16},{16,20},{20,24},{24,28},{28,0},{1,5},{5... | collective-permute-start | bytes 393224 | tf_op jit(solution)/shard_map/ppermute | solution.py:551
  91.6 7.0 %collective-permute-start.20 = (bf16[8,64,128]{2,1,0:T(8,128)(2,1)S(1)}, bf16[8,64,128]{2,1,0:T(8,128)(2,1)S(1)}, u32[]{:S(2)}, u32[]{:S(2)}) collective-permute-start(bf16[8,64,128]{2,1,0:T(8,128)(2,1)S(1)} %get-tuple-element.94), channel_id=1, source_target_pairs={{0,8},{4,12},{8,16},{12,20},{16,24},{20,28},{24,0},{28,4},{1,9},{5... | collective-permute-start | bytes 393224 | tf_op jit(solution)/shard_map/ppermute | solution.py:551
  91.7 16.3 %collective-permute-start.21 = (bf16[8,64,128]{2,1,0:T(8,128)(2,1)S(1)}, bf16[8,64,128]{2,1,0:T(8,128)(2,1)S(1)}, u32[]{:S(2)}, u32[]{:S(2)}) collective-permute-start(bf16[8,64,128]{2,1,0:T(8,128)(2,1)S(1)} %get-tuple-element.95), channel_id=1, source_target_pairs={{0,12},{4,16},{8,20},{12,24},{16,28},{20,0},{24,4},{28,8},{1,13},{... | collective-permute-start | bytes 393224 | tf_op jit(solution)/shard_map/ppermute | solution.py:551
  98.5 12.4 %collective-permute-start.22 = (bf16[8,64,128]{2,1,0:T(8,128)(2,1)S(1)}, bf16[8,64,128]{2,1,0:T(8,128)(2,1)S(1)}, u32[]{:S(2)}, u32[]{:S(2)}) collective-permute-start(bf16[8,64,128]{2,1,0:T(8,128)(2,1)S(1)} %get-tuple-element.96), channel_id=1, source_target_pairs={{0,16},{4,20},{8,24},{12,28},{16,0},{20,4},{24,8},{28,12},{1,17},{... | collective-permute-start | bytes 393224 | tf_op jit(solution)/shard_map/ppermute | solution.py:551
  98.6 12.3 %collective-permute-start.23 = (bf16[8,64,128]{2,1,0:T(8,128)(2,1)S(1)}, bf16[8,64,128]{2,1,0:T(8,128)(2,1)S(1)}, u32[]{:S(2)}, u32[]{:S(2)}) collective-permute-start(bf16[8,64,128]{2,1,0:T(8,128)(2,1)S(1)} %get-tuple-element.97), channel_id=1, source_target_pairs={{0,20},{4,24},{8,28},{12,0},{16,4},{20,8},{24,12},{28,16},{1,21},{... | collective-permute-start | bytes 393224 | tf_op jit(solution)/shard_map/ppermute | solution.py:551
  108.0 8.9 %collective-permute-start.24 = (bf16[8,64,128]{2,1,0:T(8,128)(2,1)S(1)}, bf16[8,64,128]{2,1,0:T(8,128)(2,1)S(1)}, u32[]{:S(2)}, u32[]{:S(2)}) collective-permute-start(bf16[8,64,128]{2,1,0:T(8,128)(2,1)S(1)} %get-tuple-element.98), channel_id=1, source_target_pairs={{0,24},{4,28},{8,0},{12,4},{16,8},{20,12},{24,16},{28,20},{1,25},{... | collective-permute-start | bytes 393224 | tf_op jit(solution)/shard_map/ppermute | solution.py:551
  110.9 6.1 %collective-permute-start.25 = (bf16[8,64,128]{2,1,0:T(8,128)(2,1)S(1)}, bf16[8,64,128]{2,1,0:T(8,128)(2,1)S(1)}, u32[]{:S(2)}, u32[]{:S(2)}) collective-permute-start(bf16[8,64,128]{2,1,0:T(8,128)(2,1)S(1)} %get-tuple-element.99), channel_id=1, source_target_pairs={{0,28},{4,0},{8,4},{12,8},{16,12},{20,16},{24,20},{28,24},{1,29},{... | collective-permute-start | bytes 393224 | tf_op jit(solution)/shard_map/ppermute | solution.py:551
  125.8 6.3 %collective-permute-start.28 = (bf16[4,64,128]{2,1,0:T(8,128)(2,1)S(1)}, bf16[4,64,128]{2,1,0:T(8,128)(2,1)S(1)}, u32[]{:S(2)}, u32[]{:S(2)}) collective-permute-start(bf16[4,64,128]{2,1,0:T(8,128)(2,1)S(1)} %get-tuple-element.103), channel_id=1, source_target_pairs={{0,12},{4,16},{8,20},{12,24},{16,28},{20,0},{24,4},{28,8},{1,13},{... | collective-permute-start | bytes 196616 | tf_op jit(solution)/shard_map/ppermute | solution.py:551
  127.6 6.5 %collective-permute-start.29 = (bf16[4,64,128]{2,1,0:T(8,128)(2,1)S(1)}, bf16[4,64,128]{2,1,0:T(8,128)(2,1)S(1)}, u32[]{:S(2)}, u32[]{:S(2)}) collective-permute-start(bf16[4,64,128]{2,1,0:T(8,128)(2,1)S(1)} %get-tuple-element.104), channel_id=1, source_target_pairs={{0,16},{4,20},{8,24},{12,28},{16,0},{20,4},{24,8},{28,12},{1,17},{... | collective-permute-start | bytes 196616 | tf_op jit(solution)/shard_map/ppermute | solution.py:551
  128.5 9.8 %collective-permute-start.39 = (bf16[4,64,128]{2,1,0:T(8,128)(2,1)S(1)}, bf16[4,64,128]{2,1,0:T(8,128)(2,1)S(1)}, u32[]{:S(2)}, u32[]{:S(2)}) collective-permute-start(bf16[4,64,128]{2,1,0:T(8,128)(2,1)S(1)} %get-tuple-element.120), channel_id=1, source_target_pairs={{0,4},{4,8},{8,12},{12,16},{16,20},{20,24},{24,28},{28,0},{1,5},{5... | collective-permute-start | bytes 196616 | tf_op jit(solution)/shard_map/ppermute | solution.py:551
  132.1 6.2 %collective-permute-start.40 = (bf16[4,64,128]{2,1,0:T(8,128)(2,1)S(1)}, bf16[4,64,128]{2,1,0:T(8,128)(2,1)S(1)}, u32[]{:S(2)}, u32[]{:S(2)}) collective-permute-start(bf16[4,64,128]{2,1,0:T(8,128)(2,1)S(1)} %get-tuple-element.121), channel_id=1, source_target_pairs={{0,8},{4,12},{8,16},{12,20},{16,24},{20,28},{24,0},{28,4},{1,9},{5... | collective-permute-start | bytes 196616 | tf_op jit(solution)/shard_map/ppermute | solution.py:551
  134.1 8.0 %collective-permute-start.41 = (bf16[4,64,128]{2,1,0:T(8,128)(2,1)S(1)}, bf16[4,64,128]{2,1,0:T(8,128)(2,1)S(1)}, u32[]{:S(2)}, u32[]{:S(2)}) collective-permute-start(bf16[4,64,128]{2,1,0:T(8,128)(2,1)S(1)} %get-tuple-element.122), channel_id=1, source_target_pairs={{0,12},{4,16},{8,20},{12,24},{16,28},{20,0},{24,4},{28,8},{1,13},{... | collective-permute-start | bytes 196616 | tf_op jit(solution)/shard_map/ppermute | solution.py:551
  138.3 6.1 %collective-permute-start.42 = (bf16[4,64,128]{2,1,0:T(8,128)(2,1)S(1)}, bf16[4,64,128]{2,1,0:T(8,128)(2,1)S(1)}, u32[]{:S(2)}, u32[]{:S(2)}) collective-permute-start(bf16[4,64,128]{2,1,0:T(8,128)(2,1)S(1)} %get-tuple-element.123), channel_id=1, source_target_pairs={{0,16},{4,20},{8,24},{12,28},{16,0},{20,4},{24,8},{28,12},{1,17},{... | collective-permute-start | bytes 196616 | tf_op jit(solution)/shard_map/ppermute | solution.py:551
  138.3 6.4 %collective-permute-start.43 = (bf16[4,64,128]{2,1,0:T(8,128)(2,1)S(1)}, bf16[4,64,128]{2,1,0:T(8,128)(2,1)S(1)}, u32[]{:S(2)}, u32[]{:S(2)}) collective-permute-start(bf16[4,64,128]{2,1,0:T(8,128)(2,1)S(1)} %get-tuple-element.124), channel_id=1, source_target_pairs={{0,20},{4,24},{8,28},{12,0},{16,4},{20,8},{24,12},{28,16},{1,21},{... | collective-permute-start | bytes 196616 | tf_op jit(solution)/shard_map/ppermute | solution.py:551
  142.1 6.7 %collective-permute-start.44 = (bf16[4,64,128]{2,1,0:T(8,128)(2,1)S(1)}, bf16[4,64,128]{2,1,0:T(8,128)(2,1)S(1)}, u32[]{:S(2)}, u32[]{:S(2)}) collective-permute-start(bf16[4,64,128]{2,1,0:T(8,128)(2,1)S(1)} %get-tuple-element.125), channel_id=1, source_target_pairs={{0,24},{4,28},{8,0},{12,4},{16,8},{20,12},{24,16},{28,20},{1,25},{... | collective-permute-start | bytes 196616 | tf_op jit(solution)/shard_map/ppermute | solution.py:551
  144.4 4.4 %collective-permute-start.45 = (bf16[4,64,128]{2,1,0:T(8,128)(2,1)S(1)}, bf16[4,64,128]{2,1,0:T(8,128)(2,1)S(1)}, u32[]{:S(2)}, u32[]{:S(2)}) collective-permute-start(bf16[4,64,128]{2,1,0:T(8,128)(2,1)S(1)} %get-tuple-element.126), channel_id=1, source_target_pairs={{0,28},{4,0},{8,4},{12,8},{16,12},{20,16},{24,20},{28,24},{1,29},{... | collective-permute-start | bytes 196616 | tf_op jit(solution)/shard_map/ppermute | solution.py:551
  144.7 6.5 %collective-permute-start.30 = (bf16[4,64,128]{2,1,0:T(8,128)(2,1)S(1)}, bf16[4,64,128]{2,1,0:T(8,128)(2,1)S(1)}, u32[]{:S(2)}, u32[]{:S(2)}) collective-permute-start(bf16[4,64,128]{2,1,0:T(8,128)(2,1)S(1)} %get-tuple-element.105), channel_id=1, source_target_pairs={{0,20},{4,24},{8,28},{12,0},{16,4},{20,8},{24,12},{28,16},{1,21},{... | collective-permute-start | bytes 196616 | tf_op jit(solution)/shard_map/ppermute | solution.py:551
  148.8 5.0 %collective-permute-start.32 = (bf16[4,64,128]{2,1,0:T(8,128)(2,1)S(1)}, bf16[4,64,128]{2,1,0:T(8,128)(2,1)S(1)}, u32[]{:S(2)}, u32[]{:S(2)}) collective-permute-start(bf16[4,64,128]{2,1,0:T(8,128)(2,1)S(1)} %get-tuple-element.107), channel_id=1, source_target_pairs={{0,28},{4,0},{8,4},{12,8},{16,12},{20,16},{24,20},{28,24},{1,29},{... | collective-permute-start | bytes 196616 | tf_op jit(solution)/shard_map/ppermute | solution.py:551
  151.2 7.1 %collective-permute-start.46 = (bf16[512,256]{1,0:T(8,128)(2,1)S(1)}, bf16[512,256]{1,0:T(8,128)(2,1)S(1)}, u32[]{:S(2)}, u32[]{:S(2)}) collective-permute-start(bf16[512,256]{1,0:T(8,128)(2,1)S(1)} %get-tuple-element.127.refs_4_), channel_id=1, source_target_pairs={{0,1},{1,0},{2,3},{3,2},{4,5},{5,4},{6,7},{7,6},{8,9},{9,8},{10,11... | collective-permute-start | bytes 786440 | tf_op jit(solution)/shard_map/ppermute | solution.py:560
  152.6 20.2 %collective-permute-start.18 = (bf16[512,512]{1,0:T(8,128)(2,1)S(1)}, bf16[512,512]{1,0:T(8,128)(2,1)S(1)}, u32[]{:S(2)}, u32[]{:S(2)}) collective-permute-start(bf16[512,512]{1,0:T(8,128)(2,1)S(1)} %get-tuple-element.91.refs_1_), channel_id=1, source_target_pairs={{0,2},{1,3},{2,0},{3,1},{4,6},{5,7},{6,4},{7,5},{8,10},{9,11},{10,... | collective-permute-start | bytes 1572872 | tf_op jit(solution)/shard_map/ppermute | solution.py:560
  153.9 18.9 %collective-permute-start.17 = (bf16[512,512]{1,0:T(8,128)(2,1)S(1)}, bf16[512,512]{1,0:T(8,128)(2,1)S(1)}, u32[]{:S(2)}, u32[]{:S(2)}) collective-permute-start(bf16[512,512]{1,0:T(8,128)(2,1)S(1)} %get-tuple-element.90.refs_0_), channel_id=1, source_target_pairs={{0,1},{1,0},{2,3},{3,2},{4,5},{5,4},{6,7},{7,6},{8,9},{9,8},{10,11... | collective-permute-start | bytes 1572872 | tf_op jit(solution)/shard_map/ppermute | solution.py:560
  158.3 12.6 %collective-permute-start.47 = (bf16[512,256]{1,0:T(8,128)(2,1)S(1)}, bf16[512,256]{1,0:T(8,128)(2,1)S(1)}, u32[]{:S(2)}, u32[]{:S(2)}) collective-permute-start(bf16[512,256]{1,0:T(8,128)(2,1)S(1)} %get-tuple-element.128.refs_5_), channel_id=1, source_target_pairs={{0,2},{1,3},{2,0},{3,1},{4,6},{5,7},{6,4},{7,5},{8,10},{9,11},{10,... | collective-permute-start | bytes 786440 | tf_op jit(solution)/shard_map/ppermute | solution.py:560
  170.9 7.3 %collective-permute-start.33 = (bf16[512,256]{1,0:T(8,128)(2,1)S(1)}, bf16[512,256]{1,0:T(8,128)(2,1)S(1)}, u32[]{:S(2)}, u32[]{:S(2)}) collective-permute-start(bf16[512,256]{1,0:T(8,128)(2,1)S(1)} %get-tuple-element.108.refs_4_), channel_id=1, source_target_pairs={{0,1},{1,0},{2,3},{3,2},{4,5},{5,4},{6,7},{7,6},{8,9},{9,8},{10,11... | collective-permute-start | bytes 786440 | tf_op jit(solution)/shard_map/ppermute | solution.py:560
  176.6 26.7 %collective-permute-start.48 = (bf16[1024,256]{1,0:T(8,128)(2,1)S(1)}, bf16[1024,256]{1,0:T(8,128)(2,1)S(1)}, u32[]{:S(2)}, u32[]{:S(2)}) collective-permute-start(bf16[1024,256]{1,0:T(8,128)(2,1)S(1)} %get-tuple-element.130), channel_id=1, source_target_pairs={{0,2},{1,3},{2,0},{3,1},{4,6},{5,7},{6,4},{7,5},{8,10},{9,11},{10,... | collective-permute-start | bytes 1572872 | tf_op jit(solution)/shard_map/ppermute | solution.py:560
  177.9 25.5 %collective-permute-start.49 = (bf16[1024,256]{1,0:T(8,128)(2,1)S(1)}, bf16[1024,256]{1,0:T(8,128)(2,1)S(1)}, u32[]{:S(2)}, u32[]{:S(2)}) collective-permute-start(bf16[1024,256]{1,0:T(8,128)(2,1)S(1)} %get-tuple-element.132), channel_id=1, source_target_pairs={{0,1},{1,0},{2,3},{3,2},{4,5},{5,4},{6,7},{7,6},{8,9},{9,8},{10,11... | collective-permute-start | bytes 1572872 | tf_op jit(solution)/shard_map/ppermute | solution.py:560
  177.9 16.6 %collective-permute-start.34 = (bf16[512,256]{1,0:T(8,128)(2,1)S(1)}, bf16[512,256]{1,0:T(8,128)(2,1)S(1)}, u32[]{:S(2)}, u32[]{:S(2)}) collective-permute-start(bf16[512,256]{1,0:T(8,128)(2,1)S(1)} %get-tuple-element.109.refs_5_), channel_id=1, source_target_pairs={{0,2},{1,3},{2,0},{3,1},{4,6},{5,7},{6,4},{7,5},{8,10},{9,11},{10,... | collective-permute-start | bytes 786440 | tf_op jit(solution)/shard_map/ppermute | solution.py:560
  198.2 17.7 %collective-permute-start.37 = (bf16[1024,256]{1,0:T(8,128)(2,1)S(1)}, bf16[1024,256]{1,0:T(8,128)(2,1)S(1)}, u32[]{:S(2)}, u32[]{:S(2)}) collective-permute-start(bf16[1024,256]{1,0:T(8,128)(2,1)S(1)} %get-tuple-element.116), channel_id=1, source_target_pairs={{0,2},{1,3},{2,0},{3,1},{4,6},{5,7},{6,4},{7,5},{8,10},{9,11},{10,... | collective-permute-start | bytes 1572872 | tf_op jit(solution)/shard_map/ppermute | solution.py:560
  199.5 16.4 %collective-permute-start.38 = (bf16[1024,256]{1,0:T(8,128)(2,1)S(1)}, bf16[1024,256]{1,0:T(8,128)(2,1)S(1)}, u32[]{:S(2)}, u32[]{:S(2)}) collective-permute-start(bf16[1024,256]{1,0:T(8,128)(2,1)S(1)} %get-tuple-element.118), channel_id=1, source_target_pairs={{0,1},{1,0},{2,3},{3,2},{4,5},{5,4},{6,7},{7,6},{8,9},{9,8},{10,11... | collective-permute-start | bytes 1572872 | tf_op jit(solution)/shard_map/ppermute | solution.py:560
  205.7 10.3 %collective-permute-start.50 = (bf16[1024,128]{1,0:T(8,128)(2,1)S(1)}, bf16[1024,128]{1,0:T(8,128)(2,1)S(1)}, u32[]{:S(2)}, u32[]{:S(2)}) collective-permute-start(bf16[1024,128]{1,0:T(8,128)(2,1)S(1)} %get-tuple-element.133), channel_id=1, source_target_pairs={{0,4},{4,8},{8,12},{12,16},{16,20},{20,24},{24,28},{1,5},{5,9},{9,... | collective-permute-start | bytes 786440 | tf_op jit(solution)/shard_map/ppermute | solution.py:556
  (21 other events, 318.2 us)

commit v4 on v3

--- a/solution.py
+++ b/solution.py
@@ -122,24 +122,24 @@
                 out_ref[j] = mixed[:, j * LANES : (j + 1) * LANES]
 
 
-def mix(ids, key_proj, value_proj, aux, groups, chunk, chunks):
+def mix(ids, key_proj, value_proj, aux, groups, chunk, chunks, first, number):
     channels, tokens = key_proj.shape
     rows = channels // groups // chunks
     count = tokens // LANES
 
-    where = lambda g, ids: (lax.rem(ids[0] + g, groups) * chunks + chunk, 0)
+    where = lambda g, ids: (lax.rem(ids[0] + first + g, groups) * chunks + chunk, 0)
     return pl.pallas_call(
         mix_kernel,
-        out_shape=[jax.ShapeDtypeStruct((count, rows, LANES), BF16)] * groups,
+        out_shape=[jax.ShapeDtypeStruct((count, rows, LANES), BF16)] * number,
         grid_spec=pltpu.PrefetchScalarGridSpec(
             num_scalar_prefetch=1,
-            grid=(groups,),
+            grid=(number,),
             in_specs=[
                 pl.BlockSpec((rows, tokens), where),
                 pl.BlockSpec((rows, tokens), where),
                 pl.BlockSpec((rows, aux.shape[1]), where),
             ],
-            out_specs=[whole((count, rows, LANES))] * groups,
+            out_specs=[whole((count, rows, LANES))] * number,
         ),
         compiler_params=grant(6),
         name="mix",
@@ -599,7 +599,11 @@
     spec = spectra(long_filter, tables, min(owned, 16))
     sent = []
     for c in range(chunks):
-        sent.append(list(mix(ids, key_proj, value_proj, aux, groups, c, chunks)))
+        cuts = (0, groups // 2, groups) if c == 0 else (0, groups)
+        made = []
+        for first, end in zip(cuts, cuts[1:]):
+            made += mix(ids, key_proj, value_proj, aux, groups, c, chunks, first, end - first)
+        sent.append(made)
     sides, weights = None, None
     if four:
         part = out_weight.shape[1] // 4
@@ -621,7 +625,9 @@
     near = {0: [], 1: []}
     for c in range(chunks):
         last = c == chunks - 1
-        got = [ring(piece, "ctx", s) for s, piece in enumerate(sent[c])]
+        got = []
+        for s, piece in enumerate(sent[c]):
+            got.append(ring(piece, "ctx", s))
         runs = (half_tiles, half_tiles) if last else (count,)
         results = list(long_conv(ids, got, spec, tables, min(rows, 32), runs, c * rows))
         for h in (1, 0) if last else (None,):

time: 222 us -> 219 us (0.986)
  waiting for transfers between devices: 77.5 us -> 72.2 us
  starting transfers between devices: 70.1 us -> 72.7 us
    ppermute x35, waiting for transfers between devices: 50.9 us -> 45.6 us  [ring(): lax.ppermute(block, axis, [(i, (i + distance) % count) for i in range(cou...]
    ppermute x35, starting transfers between devices: 49.1 us -> 51.8 us  [ring(): lax.ppermute(block, axis, [(i, (i + distance) % count) for i in range(cou...]
    pallas_call x2 -> x3, Pallas kernels: 7.97 us -> 8.39 us  [mix(): pl.pallas_call(mix_kernel, out_shape=[jax.ShapeDtypeStruct((count, rows,...]
  transfers between devices with their start and end apart: 51 -> 51, of which waited for: 21 -> 20; matrix products, arithmetic and copies ran while one was open for 0% -> 0% of each run, Pallas kernels for 24% -> 24%
where the time goes in v4:
time: 219 us; the launch traced here: 218 us
  starting transfers between devices  72.7 us (33%)
  waiting for transfers between devices  72.2 us (33%)
  Pallas kernels  66.3 us (30%)
  local copies, waits for them, and re-layouts  5.24 us (2%)
    ppermute x35, starting transfers between devices, ring(): lax.ppermute(block, axis, [(i, (i + distance) % count) for i in range(cou...  51.8 us
    ppermute x35, waiting for transfers between devices, ring(): lax.ppermute(block, axis, [(i, (i + distance) % count) for i in range(cou...  45.6 us
    ppermute x14, waiting for transfers between devices, swapped(): lax.ppermute(block, axis, [(i, i ^ bit) for i in range(lax.axis_size(axis...  25.6 us
    pallas_call x4, Pallas kernels, project(): pl.pallas_call(functools.partial(project_kernel, slot, len(sources)), out...  15.1 us
    pallas_call x2, Pallas kernels, long_conv(): pl.pallas_call(functools.partial(conv_kernel, groups), out_shape=[jax.Sha...  14.2 us
    ppermute x14, starting transfers between devices, swapped(): lax.ppermute(block, axis, [(i, i ^ bit) for i in range(lax.axis_size(axis...  10.8 us
    ppermute x2, starting transfers between devices, forward(): return lax.ppermute(block, axis, [(i, i + 1) for i in range(count - 1)])  10.1 us
    pallas_call x3, Pallas kernels, mix(): pl.pallas_call(mix_kernel, out_shape=[jax.ShapeDtypeStruct((count, rows,...  8.39 us
  transfers between devices with their start and end apart: 51, of which 20 were waited for; matrix products, arithmetic and copies ran while one was open for 0% of the time, Pallas kernels for 24%

profile of v4, /device:TPU:15, one launch (start us, length us, event | category | flops | bytes accessed | tf_op | source)
XLA Modules:
  0.0 217.7 jit_solution(6983820472747407220)
XLA Ops:
  0.6 2.2 tails.1
  2.8 3.8 %collective-permute-start = (bf16[8,1024]{1,0:T(8,128)(2,1)}, bf16[8,1024]{1,0:T(8,128)(2,1)S(1)}, u32[]{:S(2)}, u32[]{:S(2)}) collective-permute-start(bf16[8,1024]{1,0:T(8,128)(2,1)} %tails.1), channel_id=1, source_target_pairs={{0,4},{4,8},{8,12},{12,16},{16,20},{20,24},{24,28},{1,5},{5,9},{9,... | collective-permute-start | bytes 49160 | tf_op jit(solution)/shard_map/ppermute | solution.py:556
  7.9 1.6 copy-done.1
  9.5 4.0 %mix.3 = (bf16[8,64,128]{2,1,0:T(8,128)(2,1)S(1)}, bf16[8,64,128]{2,1,0:T(8,128)(2,1)S(1)}, bf16[8,64,128]{2,1,0:T(8,128)(2,1)S(1)}, bf16[8,64,128]{2,1,0:T(8,12...) custom-call(s32[2]{0:T(128)S(1)} %pad_add_fusion.ids_ref, ...), custom_call_target="tpu_custom_call" | custom-call | tf_op jit(solution)/shard_map/mix/pallas_call | solution.py:131
  13.5 3.4 %copy-done.3 = bf16[1024,4096]{1,0:T(8,128)(2,1)S(1)} copy-done((bf16[1024,4096]{1,0:T(8,128)(2,1)S(1)}, bf16[1024,4096]{1,0:T(8,128)(2,1)}, u32[]{:S(2)}) %copy-start.3) | copy-done | bytes 8388632
  16.8 2.9 %turn.2 = (bf16[1024,1024]{1,0:T(8,128)(2,1)S(1)}, bf16[1024,1024]{1,0:T(8,128)(2,1)S(1)}) custom-call(s32[2]{0:T(128)S(1)} %pad_add_fusion.ids_ref, bf16[1024,4096]{1,0:T(8,128)(2,1)S(1)} %copy-done.3), custom_call_target="tpu_custom_call" | custom-call | tf_op jit(solution)/shard_map/turn/pallas_call | solution.py:392
  20.3 2.2 %mix.4 = (bf16[8,64,128]{2,1,0:T(8,128)(2,1)S(1)}, bf16[8,64,128]{2,1,0:T(8,128)(2,1)S(1)}, bf16[8,64,128]{2,1,0:T(8,128)(2,1)S(1)}, bf16[8,64,128]{2,1,0:T(8,128)(2,1)S(1)}) custom-call(s32[2]{0:T(128)S(1)} %pad_add_fusion.ids_ref, bf16[1024,1024]{1,0:T(8,128)(2,1)S(1)} %copy-done, bf16[1024,1024]{1,0:T(8,128)(2,1)S(1)} %copy-done.2, f32[1024,16]{1,0:T(8,128)S(1)} %bitcast.6), custom_call_target="tpu_custom_call" | custom-call | tf_op jit(solution)/shard_map/mix/pallas_call | solution.py:131
  22.5 2.9 %collective-permute-start.3 = (bf16[8,64,128]{2,1,0:T(8,128)(2,1)S(1)}, bf16[8,64,128]{2,1,0:T(8,128)(2,1)S(1)}, u32[]{:S(2)}, u32[]{:S(2)}) collective-permute-start(bf16[8,64,128]{2,1,0:T(8,128)(2,1)S(1)} %get-tuple-element.74), channel_id=1, source_target_pairs={{0,4},{4,8},{8,12},{12,16},{16,20},{20,24},{24,28},{28,0},{1,5},{5... | collective-permute-start | bytes 393224 | tf_op jit(solution)/shard_map/ppermute | solution.py:551
  26.8 2.2 %mix.5 = (bf16[8,64,128]{2,1,0:T(8,128)(2,1)S(1)}, bf16[8,64,128]{2,1,0:T(8,128)(2,1)S(1)}, bf16[8,64,128]{2,1,0:T(8,128)(2,1)S(1)}, bf16[8,64,128]{2,1,0:T(8,128)(2,1)S(1)}) custom-call(s32[2]{0:T(128)S(1)} %pad_add_fusion.ids_ref, bf16[1024,1024]{1,0:T(8,128)(2,1)S(1)} %copy-done, bf16[1024,1024]{1,0:T(8,128)(2,1)S(1)} %copy-done.2, f32[1024,16]{1,0:T(8,128)S(1)} %bitcast.7), custom_call_target="tpu_custom_call" | custom-call | tf_op jit(solution)/shard_map/mix/pallas_call | solution.py:131
  32.1 9.2 %collective-permute-done.5.refs_3_ = bf16[8,64,128]{2,1,0:T(8,128)(2,1)S(1)} collective-permute-done((bf16[8,64,128]{2,1,0:T(8,128)(2,1)S(1)}, bf16[8,64,128]{2,1,0:T(8,128)(2,1)S(1)}, u32[]{:S(2)}, u32[]{:S(2)}) %collective-permute-start.5) | collective-permute-done | bytes 131104 | tf_op jit(solution)/shard_map/ppermute | solution.py:551
  41.3 2.9 %collective-permute-done.6.refs_4_ = bf16[8,64,128]{2,1,0:T(8,128)(2,1)S(1)} collective-permute-done((bf16[8,64,128]{2,1,0:T(8,128)(2,1)S(1)}, bf16[8,64,128]{2,1,0:T(8,128)(2,1)S(1)}, u32[]{:S(2)}, u32[]{:S(2)}) %collective-permute-start.6) | collective-permute-done | bytes 131104 | tf_op jit(solution)/shard_map/ppermute | solution.py:551
  44.6 5.7 %spectra.1.refs_8_ = f32[128,64,256]{2,1,0:T(8,128)S(1)} custom-call(f32[128,8192]{1,0:T(8,128)S(1)} %copy-done.5, bf16[128,192]{1,0:T(8,128)(2,1)S(1)} %copy-done.14, f32[2,64,128]{2,1,0:T(8,128)S(1)} %copy-done.10, bf16[256,256]{1,0:T(8,128)(2,1)S(1)} %copy-done.6), custom_call_target="tpu_custom_call" | custom-call | tf_op jit(solution)/shard_map/spectra/pallas_call | solution.py:195
  50.4 7.0 %conv.2 = (bf16[8,64,128]{2,1,0:T(8,128)(2,1)S(1)}, bf16[8,64,128]{2,1,0:T(8,128)(2,1)S(1)}, bf16[8,64,128]{2,1,0:T(8,128)(2,1)S(1)}, bf16[8,64,128]{2,1,0:T(8,1...) custom-call(s32[2]{0:T(128)S(1)} %pad_add_fusion.ids_ref, ...), custom_call_target="tpu_custom_call" | custom-call | tf_op jit(solution)/shard_map/conv/pallas_call | solution.py:277
  58.8 2.0 collective-permute-start.11
  60.8 3.3 %collective-permute-start.12 = (bf16[8,64,128]{2,1,0:T(8,128)(2,1)S(1)}, bf16[8,64,128]{2,1,0:T(8,128)(2,1)S(1)}, u32[]{:S(2)}, u32[]{:S(2)}) collective-permute-start(bf16[8,64,128]{2,1,0:T(8,128)(2,1)S(1)} %get-tuple-element.84), channel_id=1, source_target_pairs={{0,12},{4,16},{8,20},{12,24},{16,28},{20,0},{24,4},{28,8},{1,13},{... | collective-permute-start | bytes 393224 | tf_op jit(solution)/shard_map/ppermute | solution.py:551
  64.1 2.3 %collective-permute-start.13 = (bf16[8,64,128]{2,1,0:T(8,128)(2,1)S(1)}, bf16[8,64,128]{2,1,0:T(8,128)(2,1)S(1)}, u32[]{:S(2)}, u32[]{:S(2)}) collective-permute-start(bf16[8,64,128]{2,1,0:T(8,128)(2,1)S(1)} %get-tuple-element.85), channel_id=1, source_target_pairs={{0,16},{4,20},{8,24},{12,28},{16,0},{20,4},{24,8},{28,12},{1,17},{... | collective-permute-start | bytes 393224 | tf_op jit(solution)/shard_map/ppermute | solution.py:551
  66.4 3.5 %collective-permute-start.14 = (bf16[8,64,128]{2,1,0:T(8,128)(2,1)S(1)}, bf16[8,64,128]{2,1,0:T(8,128)(2,1)S(1)}, u32[]{:S(2)}, u32[]{:S(2)}) collective-permute-start(bf16[8,64,128]{2,1,0:T(8,128)(2,1)S(1)} %get-tuple-element.86), channel_id=1, source_target_pairs={{0,20},{4,24},{8,28},{12,0},{16,4},{20,8},{24,12},{28,16},{1,21},{... | collective-permute-start | bytes 393224 | tf_op jit(solution)/shard_map/ppermute | solution.py:551
  70.0 2.2 %collective-permute-start.15 = (bf16[8,64,128]{2,1,0:T(8,128)(2,1)S(1)}, bf16[8,64,128]{2,1,0:T(8,128)(2,1)S(1)}, u32[]{:S(2)}, u32[]{:S(2)}) collective-permute-start(bf16[8,64,128]{2,1,0:T(8,128)(2,1)S(1)} %get-tuple-element.87), channel_id=1, source_target_pairs={{0,24},{4,28},{8,0},{12,4},{16,8},{20,12},{24,16},{28,20},{1,25},{... | collective-permute-start | bytes 393224 | tf_op jit(solution)/shard_map/ppermute | solution.py:551
  72.2 5.3 %collective-permute-done.13.refs_4_ = bf16[8,64,128]{2,1,0:T(8,128)(2,1)S(1)} collective-permute-done((bf16[8,64,128]{2,1,0:T(8,128)(2,1)S(1)}, bf16[8,64,128]{2,1,0:T(8,128)(2,1)S(1)}, u32[]{:S(2)}, u32[]{:S(2)}) %collective-permute-start.13) | collective-permute-done | bytes 131104 | tf_op jit(solution)/shard_map/ppermute | solution.py:551
  77.6 3.2 %collective-permute-start.16 = (bf16[8,64,128]{2,1,0:T(8,128)(2,1)S(1)}, bf16[8,64,128]{2,1,0:T(8,128)(2,1)S(1)}, u32[]{:S(2)}, u32[]{:S(2)}) collective-permute-start(bf16[8,64,128]{2,1,0:T(8,128)(2,1)S(1)} %get-tuple-element.88), channel_id=1, source_target_pairs={{0,28},{4,0},{8,4},{12,8},{16,12},{20,16},{24,20},{28,24},{1,29},{... | collective-permute-start | bytes 393224 | tf_op jit(solution)/shard_map/ppermute | solution.py:551
  80.8 3.6 %query.1.refs_8_ = f32[8,1024,128]{2,1,0:T(8,128)S(1)} custom-call(bf16[1024,1024]{1,0:T(8,128)(2,1)S(1)} %copy-done.4, f32[1024,16]{1,0:T(8,128)S(1)} %bitcast.8), custom_call_target="tpu_custom_call" | custom-call | tf_op jit(solution)/shard_map/query/pallas_call | solution.py:306
  84.5 2.6 %collective-permute-done.15.refs_6_ = bf16[8,64,128]{2,1,0:T(8,128)(2,1)S(1)} collective-permute-done((bf16[8,64,128]{2,1,0:T(8,128)(2,1)S(1)}, bf16[8,64,128]{2,1,0:T(8,128)(2,1)S(1)}, u32[]{:S(2)}, u32[]{:S(2)}) %collective-permute-start.15) | collective-permute-done | bytes 131104 | tf_op jit(solution)/shard_map/ppermute | solution.py:551
  89.3 2.6 %collective-permute-start.21 = (bf16[8,64,128]{2,1,0:T(8,128)(2,1)S(1)}, bf16[8,64,128]{2,1,0:T(8,128)(2,1)S(1)}, u32[]{:S(2)}, u32[]{:S(2)}) collective-permute-start(bf16[8,64,128]{2,1,0:T(8,128)(2,1)S(1)} %get-tuple-element.95), channel_id=1, source_target_pairs={{0,12},{4,16},{8,20},{12,24},{16,28},{20,0},{24,4},{28,8},{1,13},{... | collective-permute-start | bytes 393224 | tf_op jit(solution)/shard_map/ppermute | solution.py:551
  91.9 4.2 %collective-permute-done.19.refs_1_ = bf16[8,64,128]{2,1,0:T(8,128)(2,1)S(1)} collective-permute-done((bf16[8,64,128]{2,1,0:T(8,128)(2,1)S(1)}, bf16[8,64,128]{2,1,0:T(8,128)(2,1)S(1)}, u32[]{:S(2)}, u32[]{:S(2)}) %collective-permute-start.19) | collective-permute-done | bytes 131104 | tf_op jit(solution)/shard_map/ppermute | solution.py:551
  97.8 7.9 %collective-permute-done.21.refs_3_ = bf16[8,64,128]{2,1,0:T(8,128)(2,1)S(1)} collective-permute-done((bf16[8,64,128]{2,1,0:T(8,128)(2,1)S(1)}, bf16[8,64,128]{2,1,0:T(8,128)(2,1)S(1)}, u32[]{:S(2)}, u32[]{:S(2)}) %collective-permute-start.21) | collective-permute-done | bytes 131104 | tf_op jit(solution)/shard_map/ppermute | solution.py:551
  105.7 2.9 %collective-permute-done.22.refs_4_ = bf16[8,64,128]{2,1,0:T(8,128)(2,1)S(1)} collective-permute-done((bf16[8,64,128]{2,1,0:T(8,128)(2,1)S(1)}, bf16[8,64,128]{2,1,0:T(8,128)(2,1)S(1)}, u32[]{:S(2)}, u32[]{:S(2)}) %collective-permute-start.22) | collective-permute-done | bytes 131104 | tf_op jit(solution)/shard_map/ppermute | solution.py:551
  108.6 5.9 %collective-permute-done.24.refs_6_ = bf16[8,64,128]{2,1,0:T(8,128)(2,1)S(1)} collective-permute-done((bf16[8,64,128]{2,1,0:T(8,128)(2,1)S(1)}, bf16[8,64,128]{2,1,0:T(8,128)(2,1)S(1)}, u32[]{:S(2)}, u32[]{:S(2)}) %collective-permute-start.24) | collective-permute-done | bytes 131104 | tf_op jit(solution)/shard_map/ppermute | solution.py:551
  114.7 7.2 %conv.3 = (bf16[4,64,128]{2,1,0:T(8,128)(2,1)S(1)}, bf16[4,64,128]{2,1,0:T(8,128)(2,1)S(1)}, bf16[4,64,128]{2,1,0:T(8,128)(2,1)S(1)}, bf16[4,64,128]{2,1,0:T(8,1...) custom-call(s32[2]{0:T(128)S(1)} %pad_add_fusion.ids_ref, ...), custom_call_target="tpu_custom_call" | custom-call | tf_op jit(solution)/shard_map/conv/pallas_call | solution.py:277
  121.9 1.6 collective-permute-start.27
  123.5 1.8 collective-permute-start.28
  126.2 3.6 %collective-permute-start.39 = (bf16[4,64,128]{2,1,0:T(8,128)(2,1)S(1)}, bf16[4,64,128]{2,1,0:T(8,128)(2,1)S(1)}, u32[]{:S(2)}, u32[]{:S(2)}) collective-permute-start(bf16[4,64,128]{2,1,0:T(8,128)(2,1)S(1)} %get-tuple-element.120), channel_id=1, source_target_pairs={{0,4},{4,8},{8,12},{12,16},{16,20},{20,24},{24,28},{28,0},{1,5},{5... | collective-permute-start | bytes 196616 | tf_op jit(solution)/shard_map/ppermute | solution.py:551
  129.8 2.0 collective-permute-start.40
  131.8 4.2 %collective-permute-start.41 = (bf16[4,64,128]{2,1,0:T(8,128)(2,1)S(1)}, bf16[4,64,128]{2,1,0:T(8,128)(2,1)S(1)}, u32[]{:S(2)}, u32[]{:S(2)}) collective-permute-start(bf16[4,64,128]{2,1,0:T(8,128)(2,1)S(1)} %get-tuple-element.122), channel_id=1, source_target_pairs={{0,12},{4,16},{8,20},{12,24},{16,28},{20,0},{24,4},{28,8},{1,13},{... | collective-permute-start | bytes 196616 | tf_op jit(solution)/shard_map/ppermute | solution.py:551
  136.0 3.8 %collective-permute-start.43 = (bf16[4,64,128]{2,1,0:T(8,128)(2,1)S(1)}, bf16[4,64,128]{2,1,0:T(8,128)(2,1)S(1)}, u32[]{:S(2)}, u32[]{:S(2)}) collective-permute-start(bf16[4,64,128]{2,1,0:T(8,128)(2,1)S(1)} %get-tuple-element.124), channel_id=1, source_target_pairs={{0,20},{4,24},{8,28},{12,0},{16,4},{20,8},{24,12},{28,16},{1,21},{... | collective-permute-start | bytes 196616 | tf_op jit(solution)/shard_map/ppermute | solution.py:551
  139.9 2.2 collective-permute-done.42.refs_4_
  142.4 4.1 %collective-permute-start.30 = (bf16[4,64,128]{2,1,0:T(8,128)(2,1)S(1)}, bf16[4,64,128]{2,1,0:T(8,128)(2,1)S(1)}, u32[]{:S(2)}, u32[]{:S(2)}) collective-permute-start(bf16[4,64,128]{2,1,0:T(8,128)(2,1)S(1)} %get-tuple-element.105), channel_id=1, source_target_pairs={{0,20},{4,24},{8,28},{12,0},{16,4},{20,8},{24,12},{28,16},{1,21},{... | collective-permute-start | bytes 196616 | tf_op jit(solution)/shard_map/ppermute | solution.py:551
  152.8 3.3 %collective-permute-done.46.refs_6_ = bf16[512,256]{1,0:T(8,128)(2,1)S(1)} collective-permute-done((bf16[512,256]{1,0:T(8,128)(2,1)S(1)}, bf16[512,256]{1,0:T(8,128)(2,1)S(1)}, u32[]{:S(2)}, u32[]{:S(2)}) %collective-permute-start.46) | collective-permute-done | bytes 262176 | tf_op jit(solution)/shard_map/ppermute | solution.py:560
  157.3 4.2 %turn.3 = (bf16[1024,1024]{1,0:T(8,128)(2,1)S(1)}, bf16[1024,1024]{1,0:T(8,128)(2,1)S(1)}, bf16[1024,1024]{1,0:T(8,128)(2,1)S(1)}) custom-call(s32[2]{0:T(128)S(1)} %pad_add_fusion.ids_ref, bf16[1024,4096]{1,0:T(8,128)(2,1)S(1)} %bitcast.4), custom_call_target="tpu_custom_call" | custom-call | tf_op jit(solution)/shard_map/turn/pallas_call | solution.py:392
  162.6 6.0 %collective-permute-done.47.refs_7_ = bf16[512,256]{1,0:T(8,128)(2,1)S(1)} collective-permute-done((bf16[512,256]{1,0:T(8,128)(2,1)S(1)}, bf16[512,256]{1,0:T(8,128)(2,1)S(1)}, u32[]{:S(2)}, u32[]{:S(2)}) %collective-permute-start.47) | collective-permute-done | bytes 262176 | tf_op jit(solution)/shard_map/ppermute | solution.py:560
  168.6 1.9 collective-permute-start.33
  170.6 3.8 %project.7 = (bf16[1024,256]{1,0:T(8,128)(2,1)S(1)}, bf16[1024,256]{1,0:T(8,128)(2,1)S(1)}) custom-call(s32[2]{0:T(128)S(1)} %pad_add_fusion.ids_ref, bf16[512,512]{1,0:T(8,128)(2,1)S(1)} %get-tuple-element.90.refs_0_, bf16[512,512]{1,0:T(8,128)(2,1)S(1)} %get-tuple-element.91.refs_1_, bf16[512,512]{1,0:T(8,128)(2,1)S(1)} %collective-permute-done.17.refs_2_, ...), custom_call_target="tpu_custom_call" | custom-call | tf_op jit(solution)/shard_map/project/pallas_call | solution.py:446
  175.9 16.3 %collective-permute-done.34.refs_7_ = bf16[512,256]{1,0:T(8,128)(2,1)S(1)} collective-permute-done((bf16[512,256]{1,0:T(8,128)(2,1)S(1)}, bf16[512,256]{1,0:T(8,128)(2,1)S(1)}, u32[]{:S(2)}, u32[]{:S(2)}) %collective-permute-start.34) | collective-permute-done | bytes 262176 | tf_op jit(solution)/shard_map/ppermute | solution.py:560
  192.2 3.8 %project.5 = (bf16[1024,256]{1,0:T(8,128)(2,1)S(1)}, bf16[1024,256]{1,0:T(8,128)(2,1)S(1)}) custom-call(s32[2]{0:T(128)S(1)} %pad_add_fusion.ids_ref, bf16[512,512]{1,0:T(8,128)(2,1)S(1)} %get-tuple-element.90.refs_0_, bf16[512,512]{1,0:T(8,128)(2,1)S(1)} %get-tuple-element.91.refs_1_, bf16[512,512]{1,0:T(8,128)(2,1)S(1)} %collective-permute-done.17.refs_2_, ...), custom_call_target="tpu_custom_call" | custom-call | tf_op jit(solution)/shard_map/project/pallas_call | solution.py:446
  197.3 3.8 %project.6 = (bf16[1024,256]{1,0:T(8,128)(2,1)S(1)}, bf16[1024,256]{1,0:T(8,128)(2,1)S(1)}) custom-call(s32[2]{0:T(128)S(1)} %pad_add_fusion.ids_ref, bf16[512,512]{1,0:T(8,128)(2,1)S(1)} %get-tuple-element.90.refs_0_, bf16[512,512]{1,0:T(8,128)(2,1)S(1)} %get-tuple-element.91.refs_1_, bf16[512,512]{1,0:T(8,128)(2,1)S(1)} %collective-permute-done.17.refs_2_, ...), custom_call_target="tpu_custom_call" | custom-call | tf_op jit(solution)/shard_map/project/pallas_call | solution.py:446
  201.2 2.3 %shard_map.158 = (bf16[1024,512]{1,0:T(8,128)(2,1)S(1)}, bf16[1024,128]{1,0:T(8,128)(2,1)S(1)}, bf16[1024,384]{1,0:T(8,128)(2,1)S(1)}) custom-call(bf16[1024,256]{1,0:T(8,128)(2,1)S(1)} %get-tuple-element.129.refs_0_, bf16[1024,256]{1,0:T(8,128)(2,1)S(1)} %collective-permute-done.48.refs_1_, bf16[1024,256]{1,0:T(8,128)(2,1)S(1)} %get-tuple-element.131.refs_2_, ...), custom_call_target="tpu_custom_call" | custom-call | tf_op jit(solution)/shard_map/pallas_call | solution.py:535
  203.5 6.4 %collective-permute-start.50 = (bf16[1024,128]{1,0:T(8,128)(2,1)S(1)}, bf16[1024,128]{1,0:T(8,128)(2,1)S(1)}, u32[]{:S(2)}, u32[]{:S(2)}) collective-permute-start(bf16[1024,128]{1,0:T(8,128)(2,1)S(1)} %get-tuple-element.133), channel_id=1, source_target_pairs={{0,4},{4,8},{8,12},{12,16},{16,20},{20,24},{24,28},{1,5},{5,9},{9,... | collective-permute-start | bytes 786440 | tf_op jit(solution)/shard_map/ppermute | solution.py:556
  209.9 3.8 %project.4 = (bf16[1024,256]{1,0:T(8,128)(2,1)S(1)}, bf16[1024,256]{1,0:T(8,128)(2,1)S(1)}) custom-call(s32[2]{0:T(128)S(1)} %pad_add_fusion.ids_ref, bf16[512,512]{1,0:T(8,128)(2,1)S(1)} %get-tuple-element.90.refs_0_, bf16[512,512]{1,0:T(8,128)(2,1)S(1)} %get-tuple-element.91.refs_1_, bf16[512,512]{1,0:T(8,128)(2,1)S(1)} %collective-permute-done.17.refs_2_, ...), custom_call_target="tpu_custom_call" | custom-call | tf_op jit(solution)/shard_map/project/pallas_call | solution.py:446
  213.7 4.0 %shard_map.159 = (bf16[1024,1024]{1,0:T(8,128)(2,1)}, bf16[1024,1024]{1,0:T(8,128)(2,1)}) custom-call(bf16[1024,256]{1,0:T(8,128)(2,1)S(1)} %get-tuple-element.113.refs_0_, bf16[1024,256]{1,0:T(8,128)(2,1)S(1)} %collective-permute-done.37.refs_1_, bf16[1024,256]{1,0:T(8,128)(2,1)S(1)} %get-tuple-element.117.refs_2_, ...), custom_call_target="tpu_custom_call" | custom-call | tf_op jit(solution)/shard_map/pallas_call | solution.py:535
  (115 shorter events, 25.0 us)
Async XLA Ops:
  2.8 4.8 %collective-permute-start = (bf16[8,1024]{1,0:T(8,128)(2,1)}, bf16[8,1024]{1,0:T(8,128)(2,1)S(1)}, u32[]{:S(2)}, u32[]{:S(2)}) collective-permute-start(bf16[8,1024]{1,0:T(8,128)(2,1)} %tails.1), channel_id=1, source_target_pairs={{0,4},{4,8},{8,12},{12,16},{16,20},{20,24},{24,28},{1,5},{5,9},{9,... | collective-permute-start | bytes 49160 | tf_op jit(solution)/shard_map/ppermute | solution.py:556
  19.8 68.9 %collective-permute-start.1 = (bf16[1024,1024]{1,0:T(8,128)(2,1)S(1)}, bf16[1024,1024]{1,0:T(8,128)(2,1)S(1)}, u32[]{:S(2)}, u32[]{:S(2)}) collective-permute-start(bf16[1024,1024]{1,0:T(8,128)(2,1)S(1)} %get-tuple-element.71), channel_id=1, source_target_pairs={{0,1},{1,0},{2,3},{3,2},{4,5},{5,4},{6,7},{7,6},{8,9},{9,8},{10,11... | collective-permute-start | bytes 6291464 | tf_op jit(solution)/shard_map/ppermute | solution.py:560
  20.1 68.6 %collective-permute-start.2 = (bf16[1024,1024]{1,0:T(8,128)(2,1)S(1)}, bf16[1024,1024]{1,0:T(8,128)(2,1)S(1)}, u32[]{:S(2)}, u32[]{:S(2)}) collective-permute-start(bf16[1024,1024]{1,0:T(8,128)(2,1)S(1)} %get-tuple-element.72), channel_id=1, source_target_pairs={{0,2},{1,3},{2,0},{3,1},{4,6},{5,7},{6,4},{7,5},{8,10},{9,11},{10,... | collective-permute-start | bytes 6291464 | tf_op jit(solution)/shard_map/ppermute | solution.py:560
  22.5 6.5 %collective-permute-start.3 = (bf16[8,64,128]{2,1,0:T(8,128)(2,1)S(1)}, bf16[8,64,128]{2,1,0:T(8,128)(2,1)S(1)}, u32[]{:S(2)}, u32[]{:S(2)}) collective-permute-start(bf16[8,64,128]{2,1,0:T(8,128)(2,1)S(1)} %get-tuple-element.74), channel_id=1, source_target_pairs={{0,4},{4,8},{8,12},{12,16},{16,20},{20,24},{24,28},{28,0},{1,5},{5... | collective-permute-start | bytes 393224 | tf_op jit(solution)/shard_map/ppermute | solution.py:551
  25.5 5.6 %collective-permute-start.4 = (bf16[8,64,128]{2,1,0:T(8,128)(2,1)S(1)}, bf16[8,64,128]{2,1,0:T(8,128)(2,1)S(1)}, u32[]{:S(2)}, u32[]{:S(2)}) collective-permute-start(bf16[8,64,128]{2,1,0:T(8,128)(2,1)S(1)} %get-tuple-element.75), channel_id=1, source_target_pairs={{0,8},{4,12},{8,16},{12,20},{16,24},{20,28},{24,0},{28,4},{1,9},{5... | collective-permute-start | bytes 393224 | tf_op jit(solution)/shard_map/ppermute | solution.py:551
  29.0 12.2 %collective-permute-start.5 = (bf16[8,64,128]{2,1,0:T(8,128)(2,1)S(1)}, bf16[8,64,128]{2,1,0:T(8,128)(2,1)S(1)}, u32[]{:S(2)}, u32[]{:S(2)}) collective-permute-start(bf16[8,64,128]{2,1,0:T(8,128)(2,1)S(1)} %get-tuple-element.76), channel_id=1, source_target_pairs={{0,12},{4,16},{8,20},{12,24},{16,28},{20,0},{24,4},{28,8},{1,13},{... | collective-permute-start | bytes 393224 | tf_op jit(solution)/shard_map/ppermute | solution.py:551
  29.1 15.1 %collective-permute-start.6 = (bf16[8,64,128]{2,1,0:T(8,128)(2,1)S(1)}, bf16[8,64,128]{2,1,0:T(8,128)(2,1)S(1)}, u32[]{:S(2)}, u32[]{:S(2)}) collective-permute-start(bf16[8,64,128]{2,1,0:T(8,128)(2,1)S(1)} %get-tuple-element.77), channel_id=1, source_target_pairs={{0,16},{4,20},{8,24},{12,28},{16,0},{20,4},{24,8},{28,12},{1,17},{... | collective-permute-start | bytes 393224 | tf_op jit(solution)/shard_map/ppermute | solution.py:551
  31.1 19.3 %collective-permute-start.7 = (bf16[8,64,128]{2,1,0:T(8,128)(2,1)S(1)}, bf16[8,64,128]{2,1,0:T(8,128)(2,1)S(1)}, u32[]{:S(2)}, u32[]{:S(2)}) collective-permute-start(bf16[8,64,128]{2,1,0:T(8,128)(2,1)S(1)} %get-tuple-element.78), channel_id=1, source_target_pairs={{0,20},{4,24},{8,28},{12,0},{16,4},{20,8},{24,12},{28,16},{1,21},{... | collective-permute-start | bytes 393224 | tf_op jit(solution)/shard_map/ppermute | solution.py:551
  41.3 9.1 %collective-permute-start.8 = (bf16[8,64,128]{2,1,0:T(8,128)(2,1)S(1)}, bf16[8,64,128]{2,1,0:T(8,128)(2,1)S(1)}, u32[]{:S(2)}, u32[]{:S(2)}) collective-permute-start(bf16[8,64,128]{2,1,0:T(8,128)(2,1)S(1)} %get-tuple-element.79), channel_id=1, source_target_pairs={{0,24},{4,28},{8,0},{12,4},{16,8},{20,12},{24,16},{28,20},{1,25},{... | collective-permute-start | bytes 393224 | tf_op jit(solution)/shard_map/ppermute | solution.py:551
  44.2 6.2 %collective-permute-start.9 = (bf16[8,64,128]{2,1,0:T(8,128)(2,1)S(1)}, bf16[8,64,128]{2,1,0:T(8,128)(2,1)S(1)}, u32[]{:S(2)}, u32[]{:S(2)}) collective-permute-start(bf16[8,64,128]{2,1,0:T(8,128)(2,1)S(1)} %get-tuple-element.80), channel_id=1, source_target_pairs={{0,28},{4,0},{8,4},{12,8},{16,12},{20,16},{24,20},{28,24},{1,29},{... | collective-permute-start | bytes 393224 | tf_op jit(solution)/shard_map/ppermute | solution.py:551
  57.4 6.6 %collective-permute-start.10 = (bf16[8,64,128]{2,1,0:T(8,128)(2,1)S(1)}, bf16[8,64,128]{2,1,0:T(8,128)(2,1)S(1)}, u32[]{:S(2)}, u32[]{:S(2)}) collective-permute-start(bf16[8,64,128]{2,1,0:T(8,128)(2,1)S(1)} %get-tuple-element.82), channel_id=1, source_target_pairs={{0,4},{4,8},{8,12},{12,16},{16,20},{20,24},{24,28},{28,0},{1,5},{5... | collective-permute-start | bytes 393224 | tf_op jit(solution)/shard_map/ppermute | solution.py:551
  58.8 7.6 %collective-permute-start.11 = (bf16[8,64,128]{2,1,0:T(8,128)(2,1)S(1)}, bf16[8,64,128]{2,1,0:T(8,128)(2,1)S(1)}, u32[]{:S(2)}, u32[]{:S(2)}) collective-permute-start(bf16[8,64,128]{2,1,0:T(8,128)(2,1)S(1)} %get-tuple-element.83), channel_id=1, source_target_pairs={{0,8},{4,12},{8,16},{12,20},{16,24},{20,28},{24,0},{28,4},{1,9},{5... | collective-permute-start | bytes 393224 | tf_op jit(solution)/shard_map/ppermute | solution.py:551
  60.8 9.2 %collective-permute-start.12 = (bf16[8,64,128]{2,1,0:T(8,128)(2,1)S(1)}, bf16[8,64,128]{2,1,0:T(8,128)(2,1)S(1)}, u32[]{:S(2)}, u32[]{:S(2)}) collective-permute-start(bf16[8,64,128]{2,1,0:T(8,128)(2,1)S(1)} %get-tuple-element.84), channel_id=1, source_target_pairs={{0,12},{4,16},{8,20},{12,24},{16,28},{20,0},{24,4},{28,8},{1,13},{... | collective-permute-start | bytes 393224 | tf_op jit(solution)/shard_map/ppermute | solution.py:551
  64.1 13.5 %collective-permute-start.13 = (bf16[8,64,128]{2,1,0:T(8,128)(2,1)S(1)}, bf16[8,64,128]{2,1,0:T(8,128)(2,1)S(1)}, u32[]{:S(2)}, u32[]{:S(2)}) collective-permute-start(bf16[8,64,128]{2,1,0:T(8,128)(2,1)S(1)} %get-tuple-element.85), channel_id=1, source_target_pairs={{0,16},{4,20},{8,24},{12,28},{16,0},{20,4},{24,8},{28,12},{1,17},{... | collective-permute-start | bytes 393224 | tf_op jit(solution)/shard_map/ppermute | solution.py:551
  66.4 18.0 %collective-permute-start.14 = (bf16[8,64,128]{2,1,0:T(8,128)(2,1)S(1)}, bf16[8,64,128]{2,1,0:T(8,128)(2,1)S(1)}, u32[]{:S(2)}, u32[]{:S(2)}) collective-permute-start(bf16[8,64,128]{2,1,0:T(8,128)(2,1)S(1)} %get-tuple-element.86), channel_id=1, source_target_pairs={{0,20},{4,24},{8,28},{12,0},{16,4},{20,8},{24,12},{28,16},{1,21},{... | collective-permute-start | bytes 393224 | tf_op jit(solution)/shard_map/ppermute | solution.py:551
  70.0 17.1 %collective-permute-start.15 = (bf16[8,64,128]{2,1,0:T(8,128)(2,1)S(1)}, bf16[8,64,128]{2,1,0:T(8,128)(2,1)S(1)}, u32[]{:S(2)}, u32[]{:S(2)}) collective-permute-start(bf16[8,64,128]{2,1,0:T(8,128)(2,1)S(1)} %get-tuple-element.87), channel_id=1, source_target_pairs={{0,24},{4,28},{8,0},{12,4},{16,8},{20,12},{24,16},{28,20},{1,25},{... | collective-permute-start | bytes 393224 | tf_op jit(solution)/shard_map/ppermute | solution.py:551
  77.6 9.6 %collective-permute-start.16 = (bf16[8,64,128]{2,1,0:T(8,128)(2,1)S(1)}, bf16[8,64,128]{2,1,0:T(8,128)(2,1)S(1)}, u32[]{:S(2)}, u32[]{:S(2)}) collective-permute-start(bf16[8,64,128]{2,1,0:T(8,128)(2,1)S(1)} %get-tuple-element.88), channel_id=1, source_target_pairs={{0,28},{4,0},{8,4},{12,8},{16,12},{20,16},{24,20},{28,24},{1,29},{... | collective-permute-start | bytes 393224 | tf_op jit(solution)/shard_map/ppermute | solution.py:551
  88.7 81.8 %collective-permute-start.35 = (bf16[1024,1024]{1,0:T(8,128)(2,1)S(1)}, bf16[1024,1024]{1,0:T(8,128)(2,1)S(1)}, u32[]{:S(2)}, u32[]{:S(2)}) collective-permute-start(bf16[1024,1024]{1,0:T(8,128)(2,1)S(1)} %collective-permute-done.1.refs_10_), channel_id=1, source_target_pairs={{0,4},{4,0},{8,12},{12,8},{16,20},{20,16},{24,28},{28,24},{1,5},{5... | collective-permute-start | bytes 6291464 | tf_op jit(solution)/shard_map/ppermute | solution.py:560
  88.8 81.8 %collective-permute-start.36 = (bf16[1024,1024]{1,0:T(8,128)(2,1)S(1)}, bf16[1024,1024]{1,0:T(8,128)(2,1)S(1)}, u32[]{:S(2)}, u32[]{:S(2)}) collective-permute-start(bf16[1024,1024]{1,0:T(8,128)(2,1)S(1)} %collective-permute-done.2.refs_12_), channel_id=1, source_target_pairs={{0,4},{4,0},{8,12},{12,8},{16,20},{20,16},{24,28},{28,24},{1,5},{5... | collective-permute-start | bytes 6291464 | tf_op jit(solution)/shard_map/ppermute | solution.py:560
  89.3 6.8 %collective-permute-start.19 = (bf16[8,64,128]{2,1,0:T(8,128)(2,1)S(1)}, bf16[8,64,128]{2,1,0:T(8,128)(2,1)S(1)}, u32[]{:S(2)}, u32[]{:S(2)}) collective-permute-start(bf16[8,64,128]{2,1,0:T(8,128)(2,1)S(1)} %get-tuple-element.93), channel_id=1, source_target_pairs={{0,4},{4,8},{8,12},{12,16},{16,20},{20,24},{24,28},{28,0},{1,5},{5... | collective-permute-start | bytes 393224 | tf_op jit(solution)/shard_map/ppermute | solution.py:551
  89.3 7.0 %collective-permute-start.20 = (bf16[8,64,128]{2,1,0:T(8,128)(2,1)S(1)}, bf16[8,64,128]{2,1,0:T(8,128)(2,1)S(1)}, u32[]{:S(2)}, u32[]{:S(2)}) collective-permute-start(bf16[8,64,128]{2,1,0:T(8,128)(2,1)S(1)} %get-tuple-element.94), channel_id=1, source_target_pairs={{0,8},{4,12},{8,16},{12,20},{16,24},{20,28},{24,0},{28,4},{1,9},{5... | collective-permute-start | bytes 393224 | tf_op jit(solution)/shard_map/ppermute | solution.py:551
  89.3 16.4 %collective-permute-start.21 = (bf16[8,64,128]{2,1,0:T(8,128)(2,1)S(1)}, bf16[8,64,128]{2,1,0:T(8,128)(2,1)S(1)}, u32[]{:S(2)}, u32[]{:S(2)}) collective-permute-start(bf16[8,64,128]{2,1,0:T(8,128)(2,1)S(1)} %get-tuple-element.95), channel_id=1, source_target_pairs={{0,12},{4,16},{8,20},{12,24},{16,28},{20,0},{24,4},{28,8},{1,13},{... | collective-permute-start | bytes 393224 | tf_op jit(solution)/shard_map/ppermute | solution.py:551
  96.1 12.5 %collective-permute-start.22 = (bf16[8,64,128]{2,1,0:T(8,128)(2,1)S(1)}, bf16[8,64,128]{2,1,0:T(8,128)(2,1)S(1)}, u32[]{:S(2)}, u32[]{:S(2)}) collective-permute-start(bf16[8,64,128]{2,1,0:T(8,128)(2,1)S(1)} %get-tuple-element.96), channel_id=1, source_target_pairs={{0,16},{4,20},{8,24},{12,28},{16,0},{20,4},{24,8},{28,12},{1,17},{... | collective-permute-start | bytes 393224 | tf_op jit(solution)/shard_map/ppermute | solution.py:551
  96.3 12.4 %collective-permute-start.23 = (bf16[8,64,128]{2,1,0:T(8,128)(2,1)S(1)}, bf16[8,64,128]{2,1,0:T(8,128)(2,1)S(1)}, u32[]{:S(2)}, u32[]{:S(2)}) collective-permute-start(bf16[8,64,128]{2,1,0:T(8,128)(2,1)S(1)} %get-tuple-element.97), channel_id=1, source_target_pairs={{0,20},{4,24},{8,28},{12,0},{16,4},{20,8},{24,12},{28,16},{1,21},{... | collective-permute-start | bytes 393224 | tf_op jit(solution)/shard_map/ppermute | solution.py:551
  105.7 8.9 %collective-permute-start.24 = (bf16[8,64,128]{2,1,0:T(8,128)(2,1)S(1)}, bf16[8,64,128]{2,1,0:T(8,128)(2,1)S(1)}, u32[]{:S(2)}, u32[]{:S(2)}) collective-permute-start(bf16[8,64,128]{2,1,0:T(8,128)(2,1)S(1)} %get-tuple-element.98), channel_id=1, source_target_pairs={{0,24},{4,28},{8,0},{12,4},{16,8},{20,12},{24,16},{28,20},{1,25},{... | collective-permute-start | bytes 393224 | tf_op jit(solution)/shard_map/ppermute | solution.py:551
  108.6 6.0 %collective-permute-start.25 = (bf16[8,64,128]{2,1,0:T(8,128)(2,1)S(1)}, bf16[8,64,128]{2,1,0:T(8,128)(2,1)S(1)}, u32[]{:S(2)}, u32[]{:S(2)}) collective-permute-start(bf16[8,64,128]{2,1,0:T(8,128)(2,1)S(1)} %get-tuple-element.99), channel_id=1, source_target_pairs={{0,28},{4,0},{8,4},{12,8},{16,12},{20,16},{24,20},{28,24},{1,29},{... | collective-permute-start | bytes 393224 | tf_op jit(solution)/shard_map/ppermute | solution.py:551
  123.5 6.3 %collective-permute-start.28 = (bf16[4,64,128]{2,1,0:T(8,128)(2,1)S(1)}, bf16[4,64,128]{2,1,0:T(8,128)(2,1)S(1)}, u32[]{:S(2)}, u32[]{:S(2)}) collective-permute-start(bf16[4,64,128]{2,1,0:T(8,128)(2,1)S(1)} %get-tuple-element.103), channel_id=1, source_target_pairs={{0,12},{4,16},{8,20},{12,24},{16,28},{20,0},{24,4},{28,8},{1,13},{... | collective-permute-start | bytes 196616 | tf_op jit(solution)/shard_map/ppermute | solution.py:551
  125.3 6.5 %collective-permute-start.29 = (bf16[4,64,128]{2,1,0:T(8,128)(2,1)S(1)}, bf16[4,64,128]{2,1,0:T(8,128)(2,1)S(1)}, u32[]{:S(2)}, u32[]{:S(2)}) collective-permute-start(bf16[4,64,128]{2,1,0:T(8,128)(2,1)S(1)} %get-tuple-element.104), channel_id=1, source_target_pairs={{0,16},{4,20},{8,24},{12,28},{16,0},{20,4},{24,8},{28,12},{1,17},{... | collective-permute-start | bytes 196616 | tf_op jit(solution)/shard_map/ppermute | solution.py:551
  126.2 9.8 %collective-permute-start.39 = (bf16[4,64,128]{2,1,0:T(8,128)(2,1)S(1)}, bf16[4,64,128]{2,1,0:T(8,128)(2,1)S(1)}, u32[]{:S(2)}, u32[]{:S(2)}) collective-permute-start(bf16[4,64,128]{2,1,0:T(8,128)(2,1)S(1)} %get-tuple-element.120), channel_id=1, source_target_pairs={{0,4},{4,8},{8,12},{12,16},{16,20},{20,24},{24,28},{28,0},{1,5},{5... | collective-permute-start | bytes 196616 | tf_op jit(solution)/shard_map/ppermute | solution.py:551
  129.8 6.2 %collective-permute-start.40 = (bf16[4,64,128]{2,1,0:T(8,128)(2,1)S(1)}, bf16[4,64,128]{2,1,0:T(8,128)(2,1)S(1)}, u32[]{:S(2)}, u32[]{:S(2)}) collective-permute-start(bf16[4,64,128]{2,1,0:T(8,128)(2,1)S(1)} %get-tuple-element.121), channel_id=1, source_target_pairs={{0,8},{4,12},{8,16},{12,20},{16,24},{20,28},{24,0},{28,4},{1,9},{5... | collective-permute-start | bytes 196616 | tf_op jit(solution)/shard_map/ppermute | solution.py:551
  131.8 8.0 %collective-permute-start.41 = (bf16[4,64,128]{2,1,0:T(8,128)(2,1)S(1)}, bf16[4,64,128]{2,1,0:T(8,128)(2,1)S(1)}, u32[]{:S(2)}, u32[]{:S(2)}) collective-permute-start(bf16[4,64,128]{2,1,0:T(8,128)(2,1)S(1)} %get-tuple-element.122), channel_id=1, source_target_pairs={{0,12},{4,16},{8,20},{12,24},{16,28},{20,0},{24,4},{28,8},{1,13},{... | collective-permute-start | bytes 196616 | tf_op jit(solution)/shard_map/ppermute | solution.py:551
  136.0 6.1 %collective-permute-start.42 = (bf16[4,64,128]{2,1,0:T(8,128)(2,1)S(1)}, bf16[4,64,128]{2,1,0:T(8,128)(2,1)S(1)}, u32[]{:S(2)}, u32[]{:S(2)}) collective-permute-start(bf16[4,64,128]{2,1,0:T(8,128)(2,1)S(1)} %get-tuple-element.123), channel_id=1, source_target_pairs={{0,16},{4,20},{8,24},{12,28},{16,0},{20,4},{24,8},{28,12},{1,17},{... | collective-permute-start | bytes 196616 | tf_op jit(solution)/shard_map/ppermute | solution.py:551
  136.0 6.4 %collective-permute-start.43 = (bf16[4,64,128]{2,1,0:T(8,128)(2,1)S(1)}, bf16[4,64,128]{2,1,0:T(8,128)(2,1)S(1)}, u32[]{:S(2)}, u32[]{:S(2)}) collective-permute-start(bf16[4,64,128]{2,1,0:T(8,128)(2,1)S(1)} %get-tuple-element.124), channel_id=1, source_target_pairs={{0,20},{4,24},{8,28},{12,0},{16,4},{20,8},{24,12},{28,16},{1,21},{... | collective-permute-start | bytes 196616 | tf_op jit(solution)/shard_map/ppermute | solution.py:551
  139.8 6.7 %collective-permute-start.44 = (bf16[4,64,128]{2,1,0:T(8,128)(2,1)S(1)}, bf16[4,64,128]{2,1,0:T(8,128)(2,1)S(1)}, u32[]{:S(2)}, u32[]{:S(2)}) collective-permute-start(bf16[4,64,128]{2,1,0:T(8,128)(2,1)S(1)} %get-tuple-element.125), channel_id=1, source_target_pairs={{0,24},{4,28},{8,0},{12,4},{16,8},{20,12},{24,16},{28,20},{1,25},{... | collective-permute-start | bytes 196616 | tf_op jit(solution)/shard_map/ppermute | solution.py:551
  142.1 4.4 %collective-permute-start.45 = (bf16[4,64,128]{2,1,0:T(8,128)(2,1)S(1)}, bf16[4,64,128]{2,1,0:T(8,128)(2,1)S(1)}, u32[]{:S(2)}, u32[]{:S(2)}) collective-permute-start(bf16[4,64,128]{2,1,0:T(8,128)(2,1)S(1)} %get-tuple-element.126), channel_id=1, source_target_pairs={{0,28},{4,0},{8,4},{12,8},{16,12},{20,16},{24,20},{28,24},{1,29},{... | collective-permute-start | bytes 196616 | tf_op jit(solution)/shard_map/ppermute | solution.py:551
  142.4 6.5 %collective-permute-start.30 = (bf16[4,64,128]{2,1,0:T(8,128)(2,1)S(1)}, bf16[4,64,128]{2,1,0:T(8,128)(2,1)S(1)}, u32[]{:S(2)}, u32[]{:S(2)}) collective-permute-start(bf16[4,64,128]{2,1,0:T(8,128)(2,1)S(1)} %get-tuple-element.105), channel_id=1, source_target_pairs={{0,20},{4,24},{8,28},{12,0},{16,4},{20,8},{24,12},{28,16},{1,21},{... | collective-permute-start | bytes 196616 | tf_op jit(solution)/shard_map/ppermute | solution.py:551
  146.5 5.1 %collective-permute-start.32 = (bf16[4,64,128]{2,1,0:T(8,128)(2,1)S(1)}, bf16[4,64,128]{2,1,0:T(8,128)(2,1)S(1)}, u32[]{:S(2)}, u32[]{:S(2)}) collective-permute-start(bf16[4,64,128]{2,1,0:T(8,128)(2,1)S(1)} %get-tuple-element.107), channel_id=1, source_target_pairs={{0,28},{4,0},{8,4},{12,8},{16,12},{20,16},{24,20},{28,24},{1,29},{... | collective-permute-start | bytes 196616 | tf_op jit(solution)/shard_map/ppermute | solution.py:551
  149.0 7.1 %collective-permute-start.46 = (bf16[512,256]{1,0:T(8,128)(2,1)S(1)}, bf16[512,256]{1,0:T(8,128)(2,1)S(1)}, u32[]{:S(2)}, u32[]{:S(2)}) collective-permute-start(bf16[512,256]{1,0:T(8,128)(2,1)S(1)} %get-tuple-element.127.refs_4_), channel_id=1, source_target_pairs={{0,1},{1,0},{2,3},{3,2},{4,5},{5,4},{6,7},{7,6},{8,9},{9,8},{10,11... | collective-permute-start | bytes 786440 | tf_op jit(solution)/shard_map/ppermute | solution.py:560
  150.4 20.2 %collective-permute-start.18 = (bf16[512,512]{1,0:T(8,128)(2,1)S(1)}, bf16[512,512]{1,0:T(8,128)(2,1)S(1)}, u32[]{:S(2)}, u32[]{:S(2)}) collective-permute-start(bf16[512,512]{1,0:T(8,128)(2,1)S(1)} %get-tuple-element.91.refs_1_), channel_id=1, source_target_pairs={{0,2},{1,3},{2,0},{3,1},{4,6},{5,7},{6,4},{7,5},{8,10},{9,11},{10,... | collective-permute-start | bytes 1572872 | tf_op jit(solution)/shard_map/ppermute | solution.py:560
  151.6 19.0 %collective-permute-start.17 = (bf16[512,512]{1,0:T(8,128)(2,1)S(1)}, bf16[512,512]{1,0:T(8,128)(2,1)S(1)}, u32[]{:S(2)}, u32[]{:S(2)}) collective-permute-start(bf16[512,512]{1,0:T(8,128)(2,1)S(1)} %get-tuple-element.90.refs_0_), channel_id=1, source_target_pairs={{0,1},{1,0},{2,3},{3,2},{4,5},{5,4},{6,7},{7,6},{8,9},{9,8},{10,11... | collective-permute-start | bytes 1572872 | tf_op jit(solution)/shard_map/ppermute | solution.py:560
  156.1 12.5 %collective-permute-start.47 = (bf16[512,256]{1,0:T(8,128)(2,1)S(1)}, bf16[512,256]{1,0:T(8,128)(2,1)S(1)}, u32[]{:S(2)}, u32[]{:S(2)}) collective-permute-start(bf16[512,256]{1,0:T(8,128)(2,1)S(1)} %get-tuple-element.128.refs_5_), channel_id=1, source_target_pairs={{0,2},{1,3},{2,0},{3,1},{4,6},{5,7},{6,4},{7,5},{8,10},{9,11},{10,... | collective-permute-start | bytes 786440 | tf_op jit(solution)/shard_map/ppermute | solution.py:560
  168.6 7.3 %collective-permute-start.33 = (bf16[512,256]{1,0:T(8,128)(2,1)S(1)}, bf16[512,256]{1,0:T(8,128)(2,1)S(1)}, u32[]{:S(2)}, u32[]{:S(2)}) collective-permute-start(bf16[512,256]{1,0:T(8,128)(2,1)S(1)} %get-tuple-element.108.refs_4_), channel_id=1, source_target_pairs={{0,1},{1,0},{2,3},{3,2},{4,5},{5,4},{6,7},{7,6},{8,9},{9,8},{10,11... | collective-permute-start | bytes 786440 | tf_op jit(solution)/shard_map/ppermute | solution.py:560
  174.4 26.8 %collective-permute-start.48 = (bf16[1024,256]{1,0:T(8,128)(2,1)S(1)}, bf16[1024,256]{1,0:T(8,128)(2,1)S(1)}, u32[]{:S(2)}, u32[]{:S(2)}) collective-permute-start(bf16[1024,256]{1,0:T(8,128)(2,1)S(1)} %get-tuple-element.130), channel_id=1, source_target_pairs={{0,2},{1,3},{2,0},{3,1},{4,6},{5,7},{6,4},{7,5},{8,10},{9,11},{10,... | collective-permute-start | bytes 1572872 | tf_op jit(solution)/shard_map/ppermute | solution.py:560
  175.7 25.5 %collective-permute-start.49 = (bf16[1024,256]{1,0:T(8,128)(2,1)S(1)}, bf16[1024,256]{1,0:T(8,128)(2,1)S(1)}, u32[]{:S(2)}, u32[]{:S(2)}) collective-permute-start(bf16[1024,256]{1,0:T(8,128)(2,1)S(1)} %get-tuple-element.132), channel_id=1, source_target_pairs={{0,1},{1,0},{2,3},{3,2},{4,5},{5,4},{6,7},{7,6},{8,9},{9,8},{10,11... | collective-permute-start | bytes 1572872 | tf_op jit(solution)/shard_map/ppermute | solution.py:560
  175.7 16.6 %collective-permute-start.34 = (bf16[512,256]{1,0:T(8,128)(2,1)S(1)}, bf16[512,256]{1,0:T(8,128)(2,1)S(1)}, u32[]{:S(2)}, u32[]{:S(2)}) collective-permute-start(bf16[512,256]{1,0:T(8,128)(2,1)S(1)} %get-tuple-element.109.refs_5_), channel_id=1, source_target_pairs={{0,2},{1,3},{2,0},{3,1},{4,6},{5,7},{6,4},{7,5},{8,10},{9,11},{10,... | collective-permute-start | bytes 786440 | tf_op jit(solution)/shard_map/ppermute | solution.py:560
  196.0 17.6 %collective-permute-start.37 = (bf16[1024,256]{1,0:T(8,128)(2,1)S(1)}, bf16[1024,256]{1,0:T(8,128)(2,1)S(1)}, u32[]{:S(2)}, u32[]{:S(2)}) collective-permute-start(bf16[1024,256]{1,0:T(8,128)(2,1)S(1)} %get-tuple-element.116), channel_id=1, source_target_pairs={{0,2},{1,3},{2,0},{3,1},{4,6},{5,7},{6,4},{7,5},{8,10},{9,11},{10,... | collective-permute-start | bytes 1572872 | tf_op jit(solution)/shard_map/ppermute | solution.py:560
  197.3 16.3 %collective-permute-start.38 = (bf16[1024,256]{1,0:T(8,128)(2,1)S(1)}, bf16[1024,256]{1,0:T(8,128)(2,1)S(1)}, u32[]{:S(2)}, u32[]{:S(2)}) collective-permute-start(bf16[1024,256]{1,0:T(8,128)(2,1)S(1)} %get-tuple-element.118), channel_id=1, source_target_pairs={{0,1},{1,0},{2,3},{3,2},{4,5},{5,4},{6,7},{7,6},{8,9},{9,8},{10,11... | collective-permute-start | bytes 1572872 | tf_op jit(solution)/shard_map/ppermute | solution.py:560
  203.5 10.2 %collective-permute-start.50 = (bf16[1024,128]{1,0:T(8,128)(2,1)S(1)}, bf16[1024,128]{1,0:T(8,128)(2,1)S(1)}, u32[]{:S(2)}, u32[]{:S(2)}) collective-permute-start(bf16[1024,128]{1,0:T(8,128)(2,1)S(1)} %get-tuple-element.133), channel_id=1, source_target_pairs={{0,4},{4,8},{8,12},{12,16},{16,20},{20,24},{24,28},{1,5},{5,9},{9,... | collective-permute-start | bytes 786440 | tf_op jit(solution)/shard_map/ppermute | solution.py:556
  (21 other events, 289.2 us)
